TPU v7x, 128 devices: a whole 4x4x4 slice. The times are simulated.
128 devices in a mesh: seq: 32 (over z, x, core), doc: 4 (over y).
Axes of the slice: x: 4, y: 4, z: 4, core: 2. Of those that a mesh axis runs over, the one named last changes fastest.
Arguments:
- values: bfloat16 [4, 8192, 4096], P('doc', 'seq'), may hold values from -6 to 6
- b_in: bfloat16 [4, 8192, 128], P('doc', 'seq'), may hold values from -0.032958984 to 0.032958984
- c_in: bfloat16 [4, 8192, 128], P('doc', 'seq'), may hold values from -6 to 6
- log_decay: float32 [4, 64, 8192], P('doc', None, 'seq'), may hold values from -1 to 0, as said below
- skip: float32 [64], replicated, may hold values from 0.5 to 1.5
- owner: int32 [4, 64], P(None, 'seq'), may hold values from -1 to 3, as said below
Outputs:
- owned: bfloat16 [4, 256, 128, 4096], P('doc', 'seq')
Inputs may be any that keep to these rules, and one draw needn't show every extreme that they name: `log_decay`: all entries are at most 0. In each head the per-token rates vary from token to token and from shard to shard. Within each shard of 2 blocks of a document, both blocks name the same owner (so no block is marked -1); in general -1 marks a block that is not kept.
All inputs are finite; a program needn't handle non-finite values.
Results may differ from a plain program's by a relative error of at most 0.0063.
Values may be sent and summed in bfloat16 or wider, within the bound.
No kernel may reach another device: no remote copies, remote signals or barrier semaphores. Data moves between devices by JAX's collectives and lax.ppermute only.
A program may use at most 192 MiB of HBM per device.

v0:
```python
import functools

import jax
import jax.numpy as jnp
from jax import lax
from jax.experimental import pallas as pl
from jax.experimental.pallas import tpu as pltpu
from jax.sharding import PartitionSpec as P

Q = 128
ROW = 4
CORES = 2
GH = 8
HDIM = 64
WIDE = 1024
EARLY = (16, 24)
TAIL = 16
F32 = jnp.float32
BF = jnp.bfloat16


def iota(shape, dim):
    return lax.broadcasted_iota(jnp.int32, shape, dim)


def dot(a, b, ca=1, cb=0):
    return lax.dot_general(a, b, (((ca,), (cb,)), ((), ())), preferred_element_type=F32)


def thirds(x):
    hi = x.astype(BF)
    rest = x - hi.astype(F32)
    mid = rest.astype(BF)
    lo = (rest - mid.astype(F32)).astype(BF)
    return hi, mid, lo


def triangle(n, strict_upper=False):
    rows, cols = iota((n, n), 0), iota((n, n), 1)
    keep = cols > rows if strict_upper else cols <= rows
    return jnp.where(keep, 1.0, 0.0).astype(BF)


def summed(weights, log_decay):
    heads = log_decay.shape[0]
    parts = jnp.concatenate([p.astype(F32) for p in thirds(log_decay)], axis=0).astype(BF)
    sums = dot(weights, parts, 1, 1)
    return sums[:, 0:heads] + sums[:, heads : 2 * heads] + sums[:, 2 * heads : 3 * heads]


def coded(sums):
    return jnp.concatenate([p.astype(F32) for p in thirds(sums)], axis=1).astype(BF)


def spread(code, first_head, heads, width, count):
    shape = (3 * heads, count * width)
    head = jnp.bitwise_and(iota(shape, 0), heads - 1)
    want = lax.shift_right_logical(iota(shape, 1), width.bit_length() - 1) + first_head
    return dot(code, jnp.where(head == want, 1.0, 0.0).astype(BF))


def states_kernel(place, values, log_decay, b_in, mine, other, code, held):
    step = pl.program_id(0)
    tokens, width = values.shape
    heads = log_decay.shape[0]
    n = b_in.shape[1]
    count = width // HDIM
    per_half = mine.shape[1] // width

    @pl.when(step == 0)
    def _():
        code[0:tokens, :] = coded(summed(triangle(tokens, True), log_decay[...]))
        code[tokens:, :] = coded(summed(jnp.ones((TAIL, tokens), BF), log_decay[...]))

    wide = spread(code[...], step * count, heads, HDIM, count)
    scaled = (values[...].astype(F32) * jnp.exp(wide[0:tokens])).astype(BF)
    held[step, 0:n, :] = dot(b_in[...], scaled, 0, 0).astype(BF)
    held[step, n:, :] = tail_of(wide[tokens : tokens + 1])

    @pl.when(step == pl.num_programs(0) - 1)
    def _():
        core = place[3]
        for i in range(per_half):
            mine[:, i * width : (i + 1) * width] = held[core * per_half + i]
            other[:, i * width : (i + 1) * width] = held[(1 - core) * per_half + i]


def chip_kernel(place, mine, theirs, *refs):
    outs, held = refs[:-1], refs[-1]
    n, pw = outs[0].shape[0] - TAIL, outs[0].shape[1]
    core = place[3]
    for g in range(ROW):
        at = slice(g * pw, (g + 1) * pw)
        a, b = mine[0:n, at].astype(F32), theirs[0:n, at].astype(F32)
        ta, tb = tail_total(mine, n, at), tail_total(theirs, n, at)
        state = jnp.where(core == 0, jnp.exp(tb), 1.0) * a + jnp.where(core == 0, 1.0, jnp.exp(ta)) * b
        slot = lax.rem(g - place[0] + ROW, ROW)
        held[slot, 0:n, :] = state.astype(BF)
        held[slot, n:, :] = tail_of(ta + tb)
    for k, out in enumerate(outs):
        out[...] = held[k]


def tail_total(piece, n, lanes):
    tail = piece[n : n + TAIL, lanes].astype(F32)
    return tail[0:1] + tail[1:2] + tail[2:3]


def tail_of(total):
    hi, mid, lo = thirds(total)
    row = iota((TAIL, total.shape[1]), 0)
    tail = jnp.where(row == 0, hi.astype(F32), jnp.where(row == 1, mid.astype(F32), lo.astype(F32)))
    return tail.astype(BF)


def total_of(piece, n):
    tail = piece[n : n + TAIL, :].astype(F32)
    return tail[0:1] + tail[1:2] + tail[2:3]


def row_kernel(place, *refs):
    pieces, out = refs[:-1], refs[-1]
    n = out.shape[0] - TAIL
    me = place[0]
    where = [lax.rem(me - k + ROW, ROW) for k in range(ROW)]
    totals = [total_of(p, n) for p in pieces]
    acc = jnp.zeros((n, out.shape[1]), F32)
    for k in range(ROW):
        later = jnp.zeros_like(totals[0])
        for j in range(ROW):
            if j != k:
                later = later + jnp.where(where[j] > where[k], totals[j], 0.0)
        acc = acc + jnp.exp(later) * pieces[k][0:n, :].astype(F32)
    total = totals[0]
    for j in range(1, ROW):
        total = total + totals[j]
    out[0:n, :] = acc.astype(BF)
    out[n:, :] = tail_of(total)


def enter_kernel(place, *refs):
    pieces, rows = refs[:ROW], refs[ROW : ROW + 3]
    outs, held, totals, sent = refs[ROW + 3 : 2 * ROW + 3], refs[-3], refs[-2], refs[-1]
    n = outs[0].shape[0]
    me = place[0]
    for k in range(ROW):
        slot = lax.rem(me - k + ROW, ROW)
        held[slot] = pieces[k][0:n, :]
        totals[slot] = jnp.broadcast_to(total_of(pieces[k], n), totals.shape[1:])
    one, two, three = rows
    level = place[1]
    near = total_of(one, n)
    zero = jnp.zeros_like(near)
    enter = jnp.where(level > 0, zero + 1.0, zero) * one[0:n, :].astype(F32)
    enter = enter + jnp.where(level > 1, jnp.exp(near), zero) * two[0:n, :].astype(F32)
    near = near + total_of(two, n)
    enter = enter + jnp.where(level > 2, jnp.exp(near), zero) * three[0:n, :].astype(F32)
    for q in range(ROW):
        sent[lax.rem(q - me + ROW, ROW)] = enter.astype(BF)
        if q + 1 < ROW:
            enter = jnp.exp(totals[q][0:1]) * enter + held[q].astype(F32)
    for k in range(ROW):
        outs[k][...] = sent[k]


def local_part(skip, first_head, vals, code, log_decay, b_in, c_in, emit):
    tokens, width = vals.shape
    hdim = width // GH
    blocks = tokens // Q
    columns = spread(code, first_head, code.shape[1] // 3, Q, GH)
    parts = jnp.concatenate([p.astype(F32) for p in thirds(log_decay)], axis=0).astype(BF)
    line = dot(parts, triangle(tokens), 1, 1)
    line = line[0:GH] + line[GH : 2 * GH] + line[2 * GH : 3 * GH]
    scores = dot(c_in, b_in, 1, 1)
    keep = iota((Q, Q), 0) >= iota((Q, Q), 1)
    lanes = iota((Q, 2 * hdim), 1) < hdim
    for pair in range(GH // 2):
        col = slice(pair * 2 * hdim, (pair + 1) * 2 * hdim)
        mine = vals[:, col]
        halves = [
            [jnp.where(lanes, mine[j * Q : (j + 1) * Q], 0).astype(BF) for j in range(blocks)],
            [jnp.where(lanes, 0, mine[j * Q : (j + 1) * Q]).astype(BF) for j in range(blocks)],
        ]
        gain = jnp.where(lanes[0:1], skip[first_head + 2 * pair], skip[first_head + 2 * pair + 1])
        for i in range(blocks):
            left, right = [], []
            for side in range(2):
                head = 2 * pair + side
                for j in range(i + 1):
                    gap = columns[i * Q : (i + 1) * Q, head * Q : (head + 1) * Q]
                    gap = gap - line[head : head + 1, j * Q : (j + 1) * Q]
                    if i == j:
                        gap = jnp.where(keep, gap, -1e30)
                    here = scores[i * Q : (i + 1) * Q, j * Q : (j + 1) * Q]
                    left.append((here * jnp.exp(gap)).astype(BF))
                    right.append(halves[side][j])
            acc = dot(jnp.concatenate(left, axis=1), jnp.concatenate(right, axis=0))
            emit(i, pair * 2 * hdim, acc + gain * mine[i * Q : (i + 1) * Q].astype(F32))


def first_local_kernel(skip, values, all_decay, log_decay, b_in, c_in, out, code):
    step = pl.program_id(0)
    tokens, width = values.shape
    heads = all_decay.shape[0]
    ends = out.shape[1] - 2 * Q

    @pl.when(step == 0)
    def _():
        sums = summed(triangle(tokens), all_decay[...])
        code[...] = coded(sums)
        out[:, ends : ends + Q] = c_in[...]
        decay = jnp.concatenate([jnp.exp(sums), jnp.zeros((tokens, Q - heads), F32)], axis=1)
        out[:, ends + Q :] = decay.astype(BF)

    def emit(i, lane, x):
        at = pl.multiple_of(step * width + lane, Q)
        out[i * Q : (i + 1) * Q, pl.ds(at, x.shape[1])] = x.astype(BF)

    local_part(skip, step * GH, values[...], code[...], log_decay[...], b_in[...], c_in[...], emit)


def local_kernel(first_group, skip, values, log_decay, code, b_in, c_in, out):
    group = pl.program_id(0) + first_group

    def emit(i, lane, x):
        out[i * Q : (i + 1) * Q, lane : lane + x.shape[1]] = x.astype(out.dtype)

    local_part(skip, group * GH, values[...], code[...], log_decay[...], b_in[...], c_in[...], emit)


def split_kernel(place, mine, theirs, *refs):
    enters, keep, give, held = refs[:ROW], refs[ROW], refs[ROW + 1], refs[ROW + 2]
    n, pw = enters[0].shape
    core = place[3]
    for k in range(ROW):
        held[lax.rem(place[0] - k + ROW, ROW)] = enters[k][...]

    def emit(earlier, first, second):
        for g in range(ROW):
            at = slice(g * pw, (g + 1) * pw)
            enter = held[g]
            decay = jnp.exp(tail_total(earlier, n, at))
            first[:, at] = enter
            second[:, at] = (decay * enter.astype(F32) + earlier[0:n, at].astype(F32)).astype(BF)

    @pl.when(core == 0)
    def _():
        emit(mine, keep, give)

    @pl.when(core != 0)
    def _():
        emit(theirs, give, keep)


def sorted_kernel(place, keep, got, early, late):
    half = keep.shape[1]
    cut = early.shape[1]

    def emit(first, second):
        lo = min(cut, half)
        early[:, 0:lo] = first[:, 0:lo]
        if cut < half:
            late[:, 0 : half - cut] = first[:, cut:]
            late[:, half - cut :] = second[...]
        else:
            early[:, half:] = second[:, 0 : cut - half]
            late[...] = second[:, cut - half :]

    @pl.when(place[3] == 0)
    def _():
        emit(keep, got)

    @pl.when(place[3] != 0)
    def _():
        emit(got, keep)


def owned_plan(place, owner, docs):
    me = place[2]
    plans = []
    for r in range(docs):
        doc = lax.rem(me + r, docs)
        first, second = owner[doc, 0] == me, owner[doc, 1] == me
        plans.append((doc, first, second))
    return plans


def write_owned(plan, r, rows, out, lanes, sems, zeros=None, act="start"):
    doc, first, second = plan
    both = jnp.logical_and(first, second)

    def go(when, source, to, i):
        @pl.when(when)
        def _():
            copy = pltpu.make_async_copy(source, out.at[to, :, lanes], sems.at[2 * r + i])
            copy.start() if act == "start" else copy.wait()

    if rows is not None:
        go(first, rows.at[0:Q], 2 * doc, 0)
        go(jnp.logical_and(jnp.logical_not(first), second), rows.at[Q : 2 * Q], 2 * doc, 0)
        go(both, rows.at[Q : 2 * Q], 2 * doc + 1, 1)
    if zeros is not None:
        go(jnp.logical_not(jnp.logical_or(first, second)), zeros, 2 * doc, 0)
        go(jnp.logical_not(both), zeros, 2 * doc + 1, 1)


def read_part(sources, r, target, sems, act="start"):
    copy = pltpu.make_async_copy(sources[r], target.at[r], sems.at[r])
    copy.start() if act == "start" else copy.wait()


def finish_kernel(place, owner, *refs):
    firsts, others, enters = refs[0:4], refs[4:8], refs[8:12]
    out, first, other, enter, done, zeros, s_first, s_other, s_enter, s_out, s_zero = refs[12:]
    plans = owned_plan(place, owner, 4)
    groups = ((firsts, first, s_first), (others, other, s_other), (enters, enter, s_enter))
    lanes = pl.ds(0, done.shape[2])

    def some(plan):
        return jnp.logical_or(plan[1], plan[2])

    for r, plan in enumerate(plans):

        @pl.when(some(plan))
        def _():
            for sources, target, sems in groups:
                read_part(sources, r, target, sems)

    zeros[...] = jnp.zeros_like(zeros)
    for r, plan in enumerate(plans):
        write_owned(plan, r, None, out, pl.ds(0, zeros.shape[1]), s_zero, zeros)

    ends = first.shape[2] - 2 * Q
    step = 512
    for r, plan in enumerate(plans):

        @pl.when(some(plan))
        def _():
            for sources, target, sems in groups:
                read_part(sources, r, target, sems, "wait")
            c = first[r, :, ends : ends + Q]
            decay = first[r, :, ends + Q :]
            for at in range(0, done.shape[2], step):
                head = iota((Q, step), 0)
                pick = jnp.where(head == (iota((Q, step), 1) + at) // HDIM, 1.0, 0.0).astype(BF)
                add = dot(decay, pick) * dot(c, enter[r, :, at : at + step])
                here = first[r, :, at : at + step] if at < ends else other[r, :, at - ends : at - ends + step]
                done[r, :, at : at + step] = (here.astype(F32) + add).astype(BF)

        write_owned(plan, r, done.at[r], out, lanes, s_out)
    for r, plan in enumerate(plans):
        write_owned(plan, r, done.at[r], out, lanes, s_out, None, "wait")
        write_owned(plan, r, None, out, pl.ds(0, zeros.shape[1]), s_zero, zeros, "wait")


def owned_kernel(first_lane, place, owner, *refs):
    sources = refs[:4]
    out, held, s_in, s_out = refs[-4:]
    plans = owned_plan(place, owner, 4)
    lanes = pl.ds(first_lane, held.shape[2])
    for act in ("start", "wait"):
        for r, plan in enumerate(plans):

            @pl.when(jnp.logical_or(plan[1], plan[2]))
            def _():
                read_part(sources, r, held, s_in, act)

            if act == "wait":
                write_owned(plan, r, held.at[r], out, lanes, s_out)
    for r, plan in enumerate(plans):
        write_owned(plan, r, held.at[r], out, lanes, s_out, None, "wait")


def carried_kernel(first_head, enter, local, code, c_in, out):
    step = pl.program_id(0)
    width = local.shape[1]
    count = width // HDIM
    decay = jnp.exp(spread(code[...], first_head + step * count, code.shape[1] // 3, HDIM, count))
    out[...] = (local[...] + decay * dot(c_in[...], enter[...])).astype(BF)


def near(arrays):
    return [pltpu.with_memory_space_constraint(x, pltpu.VMEM) for x in arrays]


def whole_spec(shape):
    return pl.BlockSpec(shape, lambda *_: (0,) * len(shape))


def whole(values, b_in, c_in, log_decay, skip, owner):
    seq_n = lax.axis_size("seq")
    doc_n = lax.axis_size("doc")
    per_level = ROW * CORES
    levels = seq_n // per_level
    values, b_in, c_in, log_decay = values[0], b_in[0], c_in[0], log_decay[0]
    tokens, width = values.shape
    heads = log_decay.shape[0]
    n = b_in.shape[1]
    groups = heads // GH
    gw = width // groups
    seq_at = lax.axis_index("seq")
    doc_at = lax.axis_index("doc")
    place = jnp.stack([seq_at % per_level // CORES, seq_at // per_level, doc_at, seq_at % CORES]).astype(jnp.int32)

    def shifted(x, step_x=0, step_z=0, swap=0):
        pairs = []
        for i in range(seq_n):
            z, at, core = i // per_level, i % per_level // CORES, i % CORES
            z, at, core = (z + step_z) % levels, (at + step_x) % ROW, (core + swap) % CORES
            pairs.append((i, z * per_level + at * CORES + core))
        return lax.ppermute(x, "seq", pairs)

    def along_row(pieces):
        return [pieces[0]] + [shifted(pieces[k], step_x=k) for k in range(1, ROW)]

    def over_docs(x, k):
        return lax.ppermute(x, "doc", [(d, (d + k) % doc_n) for d in range(doc_n)])

    def over_all_docs(x, far_by):
        before = over_docs(x, 1)
        after = over_docs(x, doc_n - 1)
        far = over_docs(before, 1) if far_by > 0 else over_docs(after, doc_n - 1)
        return [x, after, far, before]

    smem = pl.BlockSpec(memory_space=pltpu.SMEM)
    vmem = pl.BlockSpec(memory_space=pltpu.VMEM)
    anywhere = pl.BlockSpec(memory_space=pl.ANY)
    prefetch = pltpu.PrefetchScalarGridSpec
    code_shape = jax.ShapeDtypeStruct((tokens, 3 * heads), BF)
    early = sum(EARLY)
    early_width = early * HDIM

    first_width = EARLY[0] * HDIM
    first, code = pl.pallas_call(
        first_local_kernel,
        name="local_first",
        out_shape=[jax.ShapeDtypeStruct((tokens, first_width + 2 * Q), BF), code_shape],
        grid=(EARLY[0] // GH,),
        in_specs=[
            smem,
            pl.BlockSpec((tokens, gw), lambda g: (0, g)),
            whole_spec((heads, tokens)),
            pl.BlockSpec((GH, tokens), lambda g: (g, 0)),
            whole_spec((tokens, n)),
            whole_spec((tokens, n)),
        ],
        out_specs=[whole_spec((tokens, first_width + 2 * Q)), whole_spec(code_shape.shape)],
    )(skip, values, log_decay, log_decay, b_in, c_in)
    firsts = over_all_docs(first, 1)

    half = width // CORES
    pw = half // ROW
    half_shape = jax.ShapeDtypeStruct((n + TAIL, half), BF)
    piece = jax.ShapeDtypeStruct((n + TAIL, pw), BF)
    mine, other_half = pl.pallas_call(
        states_kernel,
        name="states",
        out_shape=[half_shape] * 2,
        grid_spec=prefetch(
            num_scalar_prefetch=1,
            grid=(width // WIDE,),
            in_specs=[
                pl.BlockSpec((tokens, WIDE), lambda k, at: (0, k)),
                whole_spec((heads, tokens)),
                whole_spec((tokens, n)),
            ],
            out_specs=[whole_spec(half_shape.shape)] * 2,
            scratch_shapes=[
                pltpu.VMEM((tokens + TAIL, 3 * heads), BF),
                pltpu.VMEM((width // WIDE, n + TAIL, WIDE), BF),
            ],
        ),
    )(place, values, log_decay, b_in)
    theirs = shifted(other_half, swap=1)
    pieces = pl.pallas_call(
        chip_kernel,
        name="chip",
        out_shape=[piece] * ROW,
        in_specs=[smem, vmem, vmem],
        out_specs=[vmem] * ROW,
        scratch_shapes=[pltpu.VMEM((ROW,) + piece.shape, BF)],
    )(place, *near([mine, theirs]))
    pieces = along_row(pieces)

    def local_of(start, count, dtype):
        base = start // GH
        return pl.pallas_call(
            functools.partial(local_kernel, base),
            out_shape=jax.ShapeDtypeStruct((tokens, count * HDIM), dtype),
            grid=(count // GH,),
            in_specs=[
                smem,
                pl.BlockSpec((tokens, gw), lambda g: (0, g + base)),
                pl.BlockSpec((GH, tokens), lambda g: (g + base, 0)),
                whole_spec(code.shape),
                whole_spec((tokens, n)),
                whole_spec((tokens, n)),
            ],
            out_specs=pl.BlockSpec((tokens, gw), lambda g: (0, g)),
        )(skip, values, log_decay, code, b_in, c_in)

    other = local_of(EARLY[0], EARLY[1], BF)
    others = over_all_docs(other, -1)
    late_local = local_of(early, heads - early, F32)

    row = pl.pallas_call(
        row_kernel, name="row", out_shape=piece, in_specs=[smem] + [vmem] * ROW, out_specs=vmem
    )(place, *near(pieces))
    rows = [shifted(row, step_z=k) for k in (1, 2, 3)]
    enter = jax.ShapeDtypeStruct((n, pw), BF)
    enters = pl.pallas_call(
        enter_kernel,
        name="enter",
        out_shape=[enter] * ROW,
        in_specs=[smem] + [vmem] * (ROW + 3),
        out_specs=[vmem] * ROW,
        scratch_shapes=[
            pltpu.VMEM((ROW, n, pw), BF),
            pltpu.VMEM((ROW, 8, pw), F32),
            pltpu.VMEM((ROW, n, pw), BF),
        ],
    )(place, *near(pieces + rows))
    enters = along_row(enters)
    keep, give = pl.pallas_call(
        split_kernel,
        name="split",
        out_shape=[jax.ShapeDtypeStruct((n, half), BF)] * 2,
        in_specs=[smem] + [vmem] * (ROW + 2),
        out_specs=[vmem] * 2,
        scratch_shapes=[pltpu.VMEM((ROW, n, pw), BF)],
    )(place, *near([mine, theirs] + enters))
    got = shifted(give, swap=1)
    enter_early, enter_late = pl.pallas_call(
        sorted_kernel,
        name="sorted",
        out_shape=[
            jax.ShapeDtypeStruct((n, early_width), BF),
            jax.ShapeDtypeStruct((n, width - early_width), BF),
        ],
        in_specs=[smem] + [vmem] * 2,
        out_specs=[vmem] * 2,
    )(place, *near([keep, got]))
    early_enters = over_all_docs(enter_early, 1)

    late_width = width - early_width
    late = pl.pallas_call(
        functools.partial(carried_kernel, early),
        name="carried",
        out_shape=jax.ShapeDtypeStruct((tokens, late_width), BF),
        grid=(late_width // gw,),
        in_specs=[
            pl.BlockSpec((n, gw), lambda k: (0, k)),
            pl.BlockSpec((tokens, gw), lambda k: (0, k)),
            whole_spec(code.shape),
            whole_spec((tokens, n)),
        ],
        out_specs=pl.BlockSpec((tokens, gw), lambda k: (0, k)),
    )(enter_late, late_local, code, c_in)
    lates = over_all_docs(late, -1)

    dma = pltpu.SemaphoreType.DMA
    result = jax.ShapeDtypeStruct((doc_n * 2, Q, width), BF)
    owned = pl.pallas_call(
        finish_kernel,
        name="finish",
        out_shape=result,
        in_specs=[smem] * 2 + [anywhere] * 12,
        out_specs=anywhere,
        scratch_shapes=[
            pltpu.VMEM((doc_n,) + first.shape, BF),
            pltpu.VMEM((doc_n,) + other.shape, BF),
            pltpu.VMEM((doc_n,) + enter_early.shape, BF),
            pltpu.VMEM((doc_n, tokens, early_width), BF),
            pltpu.VMEM((Q, width), BF),
            dma((doc_n,)),
            dma((doc_n,)),
            dma((doc_n,)),
            dma((doc_n * 2,)),
            dma((doc_n * 2,)),
        ],
    )(place, owner, *firsts, *others, *early_enters)
    owned = pl.pallas_call(
        functools.partial(owned_kernel, early_width),
        name="owned",
        out_shape=result,
        in_specs=[smem] * 2 + [anywhere] * 5,
        out_specs=anywhere,
        scratch_shapes=[pltpu.VMEM((doc_n,) + late.shape, BF), dma((doc_n,)), dma((doc_n * 2,))],
        input_output_aliases={6: 0},
    )(place, owner, *lates, owned)
    return owned[None]


def solution(mesh):
    in_specs = (
        P("doc", "seq", None),
        P("doc", "seq", None),
        P("doc", "seq", None),
        P("doc", None, "seq"),
        P(),
        P(None, "seq"),
    )
    out_specs = P("doc", "seq", None, None)
    return jax.shard_map(whole, mesh=mesh, in_specs=in_specs, out_specs=out_specs, check_vma=False)
```

profile of v0, /device:TPU:2, one launch (start us, length us, event | category | flops | bytes accessed | tf_op | source)
XLA Modules:
  0.0 171.0 jit_solution(9365257017546516310)
XLA Ops:
  0.0 0.6 pad_add_fusion.place
  0.6 5.8 %states.1 = (bf16[144,2048]{1,0:T(8,128)(2,1)}, bf16[144,2048]{1,0:T(8,128)(2,1)}) custom-call(s32[4]{0:T(128)} %pad_add_fusion.place, bf16[256,4096]{1,0:T(8,128)(2,1)} %bitcast.9, f32[64,256]{1,0:T(8,128)} %bitcast.13, bf16[256,128]{1,0:T(8,128)(2,1)} %bitcast.18), custom_call_target="tpu_custom_call" | custom-call | tf_op jit(solution)/shard_map/states/pallas_call | solution.py:455
  6.4 0.0 collective-permute-start
  6.4 2.2 %collective-permute-done.theirs = bf16[144,2048]{1,0:T(8,128)(2,1)S(1)} collective-permute-done((bf16[144,2048]{1,0:T(8,128)(2,1)}, bf16[144,2048]{1,0:T(8,128)(2,1)S(1)}, u32[]{:S(2)}, u32[]{:S(2)}) %collective-permute-start) | collective-permute-done | bytes 589856 | tf_op jit(solution)/shard_map/ppermute | solution.py:411
  8.6 1.1 copy-done
  9.7 1.9 %chip.1 = (bf16[144,512]{1,0:T(8,128)(2,1)}, bf16[144,512]{1,0:T(8,128)(2,1)}, bf16[144,512]{1,0:T(8,128)(2,1)}, bf16[144,512]{1,0:T(8,128)(2,1)}) custom-call(s32[4]{0:T(128)} %pad_add_fusion.place, bf16[144,2048]{1,0:T(8,128)(2,1)S(1)} %copy-done, bf16[144,2048]{1,0:T(8,128)(2,1)S(1)} %collective-permute-done.theirs), custom_call_target="tpu_custom_call" | custom-call | tf_op jit(solution)/shard_map/chip/pallas_call | solution.py:475
  11.6 1.5 collective-permute-start.1
  13.1 1.0 collective-permute-start.2
  14.1 2.3 %collective-permute-start.3 = (bf16[144,512]{1,0:T(8,128)(2,1)}, bf16[144,512]{1,0:T(8,128)(2,1)S(1)}, u32[]{:S(2)}, u32[]{:S(2)}) collective-permute-start(bf16[144,512]{1,0:T(8,128)(2,1)} %get-tuple-element.26), channel_id=1, source_target_pairs={{0,24},{4,28},{8,0},{12,4},{16,8},{20,12},{24,16},{28,20},{32,56},... | collective-permute-start | bytes 442376 | tf_op jit(solution)/shard_map/ppermute | solution.py:411
  16.4 2.0 %collective-permute-done.1.refs_1_ = bf16[144,512]{1,0:T(8,128)(2,1)S(1)} collective-permute-done((bf16[144,512]{1,0:T(8,128)(2,1)}, bf16[144,512]{1,0:T(8,128)(2,1)S(1)}, u32[]{:S(2)}, u32[]{:S(2)}) %collective-permute-start.1) | collective-permute-done | bytes 147488 | tf_op jit(solution)/shard_map/ppermute | solution.py:411
  18.4 3.1 %collective-permute-done.2.refs_2_ = bf16[144,512]{1,0:T(8,128)(2,1)S(1)} collective-permute-done((bf16[144,512]{1,0:T(8,128)(2,1)}, bf16[144,512]{1,0:T(8,128)(2,1)S(1)}, u32[]{:S(2)}, u32[]{:S(2)}) %collective-permute-start.2) | collective-permute-done | bytes 147488 | tf_op jit(solution)/shard_map/ppermute | solution.py:411
  21.5 1.3 collective-permute-done.3.refs_3_
  22.8 0.9 copy-done.2
  23.7 1.6 row.1
  25.3 4.1 %collective-permute-start.6 = (bf16[144,512]{1,0:T(8,128)(2,1)}, bf16[144,512]{1,0:T(8,128)(2,1)S(1)}, u32[]{:S(2)}, u32[]{:S(2)}) collective-permute-start(bf16[144,512]{1,0:T(8,128)(2,1)} %row.1), channel_id=1, source_target_pairs={{0,96},{4,100},{8,104},{12,108},{16,112},{20,116},{24,120},{28,124... | collective-permute-start | bytes 442376 | tf_op jit(solution)/shard_map/ppermute | solution.py:411
  29.4 0.0 collective-permute-start.5
  29.4 1.3 collective-permute-start.4
  30.7 4.8 %collective-permute-done.6.refs_6_ = bf16[144,512]{1,0:T(8,128)(2,1)S(1)} collective-permute-done((bf16[144,512]{1,0:T(8,128)(2,1)}, bf16[144,512]{1,0:T(8,128)(2,1)S(1)}, u32[]{:S(2)}, u32[]{:S(2)}) %collective-permute-start.6) | collective-permute-done | bytes 147488 | tf_op jit(solution)/shard_map/ppermute | solution.py:411
  35.5 2.1 %collective-permute-done.5.refs_5_ = bf16[144,512]{1,0:T(8,128)(2,1)S(1)} collective-permute-done((bf16[144,512]{1,0:T(8,128)(2,1)}, bf16[144,512]{1,0:T(8,128)(2,1)S(1)}, u32[]{:S(2)}, u32[]{:S(2)}) %collective-permute-start.5) | collective-permute-done | bytes 147488 | tf_op jit(solution)/shard_map/ppermute | solution.py:411
  37.6 1.2 collective-permute-done.4.refs_4_
  38.8 1.8 %enter.1 = (bf16[128,512]{1,0:T(8,128)(2,1)}, bf16[128,512]{1,0:T(8,128)(2,1)}, bf16[128,512]{1,0:T(8,128)(2,1)}, bf16[128,512]{1,0:T(8,128)(2,1)}) custom-call(s32[4]{0:T(128)} %pad_add_fusion.place, bf16[144,512]{1,0:T(8,128)(2,1)S(1)} %copy-done.2, bf16[144,512]{1,0:T(8,128)(2,1)S(1)} %collective-permute-done.1.refs_1_, ...), custom_call_target="tpu_custom_call" | custom-call | tf_op jit(solution)/shard_map/enter/pallas_call | solution.py:511
  40.6 1.0 collective-permute-start.7
  41.6 1.7 collective-permute-start.8
  43.3 1.9 %collective-permute-start.9 = (bf16[128,512]{1,0:T(8,128)(2,1)}, bf16[128,512]{1,0:T(8,128)(2,1)S(1)}, u32[]{:S(2)}, u32[]{:S(2)}) collective-permute-start(bf16[128,512]{1,0:T(8,128)(2,1)} %get-tuple-element.30), channel_id=1, source_target_pairs={{0,24},{4,28},{8,0},{12,4},{16,8},{20,12},{24,16},{28,20},{32,56},... | collective-permute-start | bytes 393224 | tf_op jit(solution)/shard_map/ppermute | solution.py:411
  45.2 1.3 collective-permute-done.7.refs_1_
  46.5 2.9 %collective-permute-done.8.refs_2_ = bf16[128,512]{1,0:T(8,128)(2,1)S(1)} collective-permute-done((bf16[128,512]{1,0:T(8,128)(2,1)}, bf16[128,512]{1,0:T(8,128)(2,1)S(1)}, u32[]{:S(2)}, u32[]{:S(2)}) %collective-permute-start.8) | collective-permute-done | bytes 131104 | tf_op jit(solution)/shard_map/ppermute | solution.py:411
  49.3 1.4 collective-permute-done.9.refs_3_
  50.7 1.1 copy-done.1
  51.8 0.9 copy-done.4
  52.7 1.9 %split.1 = (bf16[128,2048]{1,0:T(8,128)(2,1)}, bf16[128,2048]{1,0:T(8,128)(2,1)}) custom-call(s32[4]{0:T(128)} %pad_add_fusion.place, bf16[144,2048]{1,0:T(8,128)(2,1)S(1)} %copy-done.1, bf16[144,2048]{1,0:T(8,128)(2,1)S(1)} %collective-permute-done.theirs, bf16[128,512]{1,0:T(8,128)(2,1)S(1)} %copy-done.4, ...), custom_call_target="tpu_custom_call" | custom-call | tf_op jit(solution)/shard_map/split/pallas_call | solution.py:524
  54.6 0.0 collective-permute-start.10
  54.6 4.2 %local_first.1 = (bf16[256,1280]{1,0:T(8,128)(2,1)}, bf16[256,192]{1,0:T(8,128)(2,1)}) custom-call(f32[64]{0:T(128)} %skip.5, bf16[256,4096]{1,0:T(8,128)(2,1)} %bitcast.10, f32[64,256]{1,0:T(8,128)} %bitcast.14, f32[64,256]{1,0:T(8,128)} %bitcast.15, bf16[256,128]{1,0:T(8,128)(2,1)} %bitcast.19, bf16[256,128]{1,0:T(8,128)(2,1)} %bitcast.22), custom_call_target="tpu_custom_call" | custom-call | tf_op jit(solution)/shard_map/local_first/pallas_call | solution.py:434
  58.8 1.6 collective-permute-start.15
  60.4 1.7 collective-permute-start.14
  62.0 4.6 %shard_map.65.refs_4_ = bf16[256,1536]{1,0:T(8,128)(2,1)} custom-call(f32[64]{0:T(128)} %skip.5, bf16[256,4096]{1,0:T(8,128)(2,1)} %bitcast.11, f32[64,256]{1,0:T(8,128)} %bitcast.16, bf16[256,192]{1,0:T(8,128)(2,1)} %get-tuple-element.34.code, bf16[256,128]{1,0:T(8,128)(2,1)} %bitcast.20, bf16[256,128]{1,0:T(8,128)(2,1)} %bitcast.23), custom_call_target="tpu_custom_call" | custom-call | tf_op jit(solution)/shard_map/pallas_call | solution.py:487
  66.7 0.4 collective-permute-start.19
  67.1 2.9 %collective-permute-start.17 = (bf16[256,1536]{1,0:T(8,128)(2,1)}, bf16[256,1536]{1,0:T(8,128)(2,1)}, u32[]{:S(2)}, u32[]{:S(2)}) collective-permute-start(bf16[256,1536]{1,0:T(8,128)(2,1)} %shard_map.65.refs_4_), channel_id=1, source_target_pairs={{0,3},{1,0},{2,1},{3,2},{4,7},{5,4},{6,5},{7,6},{8,11},{9,8},{10,9... | collective-permute-start | bytes 2359304 | tf_op jit(solution)/shard_map/ppermute | solution.py:417
  69.9 4.8 %shard_map.64.local = f32[256,1536]{1,0:T(8,128)} custom-call(f32[64]{0:T(128)} %skip.5, bf16[256,4096]{1,0:T(8,128)(2,1)} %bitcast.12, f32[64,256]{1,0:T(8,128)} %bitcast.17, bf16[256,192]{1,0:T(8,128)(2,1)} %get-tuple-element.34.code, bf16[256,128]{1,0:T(8,128)(2,1)} %bitcast.21, bf16[256,128]{1,0:T(8,128)(2,1)} %bitcast.24), custom_call_target="tpu_custom_call" | custom-call | tf_op jit(solution)/shard_map/pallas_call | solution.py:487
  74.7 0.0 collective-permute-done.10.got
  74.7 1.7 %sorted.1 = (bf16[128,2560]{1,0:T(8,128)(2,1)}, bf16[128,1536]{1,0:T(8,128)(2,1)}) custom-call(s32[4]{0:T(128)} %pad_add_fusion.place, bf16[128,2048]{1,0:T(8,128)(2,1)S(1)} %copy-done.3, bf16[128,2048]{1,0:T(8,128)(2,1)S(1)} %collective-permute-done.10.got), custom_call_target="tpu_custom_call" | custom-call | tf_op jit(solution)/shard_map/sorted/pallas_call | solution.py:533
  76.5 3.8 %carried.1.refs_0_ = bf16[256,1536]{1,0:T(8,128)(2,1)} custom-call(bf16[128,1536]{1,0:T(8,128)(2,1)} %get-tuple-element.33.enter, f32[256,1536]{1,0:T(8,128)} %shard_map.64.local, bf16[256,192]{1,0:T(8,128)(2,1)} %get-tuple-element.34.code, bf16[256,128]{1,0:T(8,128)(2,1)} %bitcast.25), custom_call_target="tpu_custom_call" | custom-call | tf_op jit(solution)/shard_map/carried/pallas_call | solution.py:546
  80.2 0.6 collective-permute-start.11
  80.8 0.0 collective-permute-done.15.refs_3_
  80.8 1.4 collective-permute-start.16
  82.3 0.0 collective-permute-done.14.refs_1_
  82.3 0.3 collective-permute-start.21
  82.5 12.6 %collective-permute-done.17.refs_5_ = bf16[256,1536]{1,0:T(8,128)(2,1)} collective-permute-done((bf16[256,1536]{1,0:T(8,128)(2,1)}, bf16[256,1536]{1,0:T(8,128)(2,1)}, u32[]{:S(2)}, u32[]{:S(2)}) %collective-permute-start.17) | collective-permute-done | bytes 786464 | tf_op jit(solution)/shard_map/ppermute | solution.py:417
  95.2 2.9 %collective-permute-start.18 = (bf16[256,1536]{1,0:T(8,128)(2,1)}, bf16[256,1536]{1,0:T(8,128)(2,1)}, u32[]{:S(2)}, u32[]{:S(2)}) collective-permute-start(bf16[256,1536]{1,0:T(8,128)(2,1)} %collective-permute-done.17.refs_5_), channel_id=1, source_target_pairs={{0,3},{1,0},{2,1},{3,2},{4,7},{5,4},{6,5},{7,6},{8,11},{9,8},{10,9... | collective-permute-start | bytes 2359304 | tf_op jit(solution)/shard_map/ppermute | solution.py:417
  98.0 0.0 collective-permute-done.19.refs_7_
  98.0 0.1 collective-permute-start.13
  98.1 13.8 %collective-permute-done.11.refs_1_ = bf16[256,1536]{1,0:T(8,128)(2,1)S(1)} collective-permute-done((bf16[256,1536]{1,0:T(8,128)(2,1)}, bf16[256,1536]{1,0:T(8,128)(2,1)S(1)}, u32[]{:S(2)}, u32[]{:S(2)}) %collective-permute-start.11) | collective-permute-done | bytes 786464 | tf_op jit(solution)/shard_map/ppermute | solution.py:417
  111.9 2.9 %collective-permute-start.12 = (bf16[256,1536]{1,0:T(8,128)(2,1)S(1)}, bf16[256,1536]{1,0:T(8,128)(2,1)S(1)}, u32[]{:S(2)}, u32[]{:S(2)}) collective-permute-start(bf16[256,1536]{1,0:T(8,128)(2,1)S(1)} %collective-permute-done.11.refs_1_), channel_id=1, source_target_pairs={{0,3},{1,0},{2,1},{3,2},{4,7},{5,4},{6,5},{7,6},{8,11},{9,8},{10,9... | collective-permute-start | bytes 2359304 | tf_op jit(solution)/shard_map/ppermute | solution.py:417
  114.8 0.6 collective-permute-start.20
  115.4 7.5 %collective-permute-done.21.refs_11_ = bf16[128,2560]{1,0:T(8,128)(2,1)} collective-permute-done((bf16[128,2560]{1,0:T(8,128)(2,1)}, bf16[128,2560]{1,0:T(8,128)(2,1)}, u32[]{:S(2)}, u32[]{:S(2)}) %collective-permute-start.21) | collective-permute-done | bytes 655392 | tf_op jit(solution)/shard_map/ppermute | solution.py:417
  122.9 0.4 collective-permute-start.22
  123.3 0.7 copy.9.owner
  123.9 4.9 %collective-permute-done.18.refs_6_ = bf16[256,1536]{1,0:T(8,128)(2,1)} collective-permute-done((bf16[256,1536]{1,0:T(8,128)(2,1)}, bf16[256,1536]{1,0:T(8,128)(2,1)}, u32[]{:S(2)}, u32[]{:S(2)}) %collective-permute-start.18) | collective-permute-done | bytes 786464 | tf_op jit(solution)/shard_map/ppermute | solution.py:417
  128.9 30.1 %collective-permute-done.20.refs_9_ = bf16[128,2560]{1,0:T(8,128)(2,1)} collective-permute-done((bf16[128,2560]{1,0:T(8,128)(2,1)}, bf16[128,2560]{1,0:T(8,128)(2,1)}, u32[]{:S(2)}, u32[]{:S(2)}) %collective-permute-start.20) | collective-permute-done | bytes 655392 | tf_op jit(solution)/shard_map/ppermute | solution.py:417
  159.0 6.8 %finish.1.refs_4_ = bf16[8,128,4096]{2,1,0:T(8,128)(2,1)} custom-call(s32[4]{0:T(128)} %pad_add_fusion.place, s32[4,2]{1,0:T(4,128)} %copy.9.owner, bf16[256,1280]{1,0:T(8,128)(2,1)} %get-tuple-element.35.refs_0_, bf16[256,1280]{1,0:T(8,128)(2,1)} %copy-done.9, bf16[256,1280]{1,0:T(8,128)(2,1)} %collective-permute-done.16.refs_2_, ...), custom_call_target="tpu_custom_call" | custom-call | tf_op jit(solution)/shard_map/finish/pallas_call | solution.py:563
  165.8 0.0 collective-permute-done.13.refs_3_
  165.8 0.0 collective-permute-done.12.refs_2_
  165.8 0.9 copy-done.6
  166.7 0.9 copy-done.7
  167.5 3.3 %owned.1 = bf16[8,128,4096]{2,1,0:T(8,128)(2,1)} custom-call(s32[4]{0:T(128)} %pad_add_fusion.place, s32[4,2]{1,0:T(4,128)} %copy.9.owner, bf16[256,1536]{1,0:T(8,128)(2,1)} %carried.1.refs_0_, bf16[256,1536]{1,0:T(8,128)(2,1)} %copy-done.5, bf16[256,1536]{1,0:T(8,128)(2,1)} %copy-done.7, ...), custom_call_target="tpu_custom_call", output_to_operand_aliasing={{}: (6, {})} | custom-call | tf_op jit(solution)/shard_map/owned/pallas_call | solution.py:582
  (18 shorter events, 0.0 us)
Async XLA Ops:
  6.4 2.2 %collective-permute-start = (bf16[144,2048]{1,0:T(8,128)(2,1)}, bf16[144,2048]{1,0:T(8,128)(2,1)S(1)}, u32[]{:S(2)}, u32[]{:S(2)}) collective-permute-start(bf16[144,2048]{1,0:T(8,128)(2,1)} %get-tuple-element.22), channel_id=1, source_target_pairs={{0,4},{4,0},{8,12},{12,8},{16,20},{20,16},{24,28},{28,24},{32,36},... | collective-permute-start | bytes 1769480 | tf_op jit(solution)/shard_map/ppermute | solution.py:411
  8.6 1.1 copy-start
  11.6 6.8 %collective-permute-start.1 = (bf16[144,512]{1,0:T(8,128)(2,1)}, bf16[144,512]{1,0:T(8,128)(2,1)S(1)}, u32[]{:S(2)}, u32[]{:S(2)}) collective-permute-start(bf16[144,512]{1,0:T(8,128)(2,1)} %get-tuple-element.24), channel_id=1, source_target_pairs={{0,8},{4,12},{8,16},{12,20},{16,24},{20,28},{24,0},{28,4},{32,40},... | collective-permute-start | bytes 442376 | tf_op jit(solution)/shard_map/ppermute | solution.py:411
  13.1 8.4 %collective-permute-start.2 = (bf16[144,512]{1,0:T(8,128)(2,1)}, bf16[144,512]{1,0:T(8,128)(2,1)S(1)}, u32[]{:S(2)}, u32[]{:S(2)}) collective-permute-start(bf16[144,512]{1,0:T(8,128)(2,1)} %get-tuple-element.25), channel_id=1, source_target_pairs={{0,16},{4,20},{8,24},{12,28},{16,0},{20,4},{24,8},{28,12},{32,48},... | collective-permute-start | bytes 442376 | tf_op jit(solution)/shard_map/ppermute | solution.py:411
  14.1 8.7 %collective-permute-start.3 = (bf16[144,512]{1,0:T(8,128)(2,1)}, bf16[144,512]{1,0:T(8,128)(2,1)S(1)}, u32[]{:S(2)}, u32[]{:S(2)}) collective-permute-start(bf16[144,512]{1,0:T(8,128)(2,1)} %get-tuple-element.26), channel_id=1, source_target_pairs={{0,24},{4,28},{8,0},{12,4},{16,8},{20,12},{24,16},{28,20},{32,56},... | collective-permute-start | bytes 442376 | tf_op jit(solution)/shard_map/ppermute | solution.py:411
  22.8 0.9 copy-start.2
  23.7 99.6 %copy-start.10 = (s32[4,2]{0,1:T(2,128)S(1)}, s32[4,2]{0,1:T(2,128)}, u32[]{:S(2)}) copy-start(s32[4,2]{0,1:T(2,128)} %param.11) | copy-start | bytes 100
  25.3 10.2 %collective-permute-start.6 = (bf16[144,512]{1,0:T(8,128)(2,1)}, bf16[144,512]{1,0:T(8,128)(2,1)S(1)}, u32[]{:S(2)}, u32[]{:S(2)}) collective-permute-start(bf16[144,512]{1,0:T(8,128)(2,1)} %row.1), channel_id=1, source_target_pairs={{0,96},{4,100},{8,104},{12,108},{16,112},{20,116},{24,120},{28,124... | collective-permute-start | bytes 442376 | tf_op jit(solution)/shard_map/ppermute | solution.py:411
  29.4 8.1 %collective-permute-start.5 = (bf16[144,512]{1,0:T(8,128)(2,1)}, bf16[144,512]{1,0:T(8,128)(2,1)S(1)}, u32[]{:S(2)}, u32[]{:S(2)}) collective-permute-start(bf16[144,512]{1,0:T(8,128)(2,1)} %row.1), channel_id=1, source_target_pairs={{0,64},{4,68},{8,72},{12,76},{16,80},{20,84},{24,88},{28,92},{32,9... | collective-permute-start | bytes 442376 | tf_op jit(solution)/shard_map/ppermute | solution.py:411
  29.4 9.4 %collective-permute-start.4 = (bf16[144,512]{1,0:T(8,128)(2,1)}, bf16[144,512]{1,0:T(8,128)(2,1)S(1)}, u32[]{:S(2)}, u32[]{:S(2)}) collective-permute-start(bf16[144,512]{1,0:T(8,128)(2,1)} %row.1), channel_id=1, source_target_pairs={{0,32},{4,36},{8,40},{12,44},{16,48},{20,52},{24,56},{28,60},{32,6... | collective-permute-start | bytes 442376 | tf_op jit(solution)/shard_map/ppermute | solution.py:411
  40.6 5.9 %collective-permute-start.7 = (bf16[128,512]{1,0:T(8,128)(2,1)}, bf16[128,512]{1,0:T(8,128)(2,1)S(1)}, u32[]{:S(2)}, u32[]{:S(2)}) collective-permute-start(bf16[128,512]{1,0:T(8,128)(2,1)} %get-tuple-element.28), channel_id=1, source_target_pairs={{0,8},{4,12},{8,16},{12,20},{16,24},{20,28},{24,0},{28,4},{32,40},... | collective-permute-start | bytes 393224 | tf_op jit(solution)/shard_map/ppermute | solution.py:411
  41.6 7.7 %collective-permute-start.8 = (bf16[128,512]{1,0:T(8,128)(2,1)}, bf16[128,512]{1,0:T(8,128)(2,1)S(1)}, u32[]{:S(2)}, u32[]{:S(2)}) collective-permute-start(bf16[128,512]{1,0:T(8,128)(2,1)} %get-tuple-element.29), channel_id=1, source_target_pairs={{0,16},{4,20},{8,24},{12,28},{16,0},{20,4},{24,8},{28,12},{32,48},... | collective-permute-start | bytes 393224 | tf_op jit(solution)/shard_map/ppermute | solution.py:411
  43.3 7.4 %collective-permute-start.9 = (bf16[128,512]{1,0:T(8,128)(2,1)}, bf16[128,512]{1,0:T(8,128)(2,1)S(1)}, u32[]{:S(2)}, u32[]{:S(2)}) collective-permute-start(bf16[128,512]{1,0:T(8,128)(2,1)} %get-tuple-element.30), channel_id=1, source_target_pairs={{0,24},{4,28},{8,0},{12,4},{16,8},{20,12},{24,16},{28,20},{32,56},... | collective-permute-start | bytes 393224 | tf_op jit(solution)/shard_map/ppermute | solution.py:411
  50.7 1.1 copy-start.1
  51.8 0.9 copy-start.4
  54.6 20.1 %copy-start.3 = (bf16[128,2048]{1,0:T(8,128)(2,1)S(1)}, bf16[128,2048]{1,0:T(8,128)(2,1)}, u32[]{:S(2)}) copy-start(bf16[128,2048]{1,0:T(8,128)(2,1)} %get-tuple-element.31.keep) | copy-start | bytes 1572868
  54.6 20.1 %collective-permute-start.10 = (bf16[128,2048]{1,0:T(8,128)(2,1)}, bf16[128,2048]{1,0:T(8,128)(2,1)S(1)}, u32[]{:S(2)}, u32[]{:S(2)}) collective-permute-start(bf16[128,2048]{1,0:T(8,128)(2,1)} %get-tuple-element.32), channel_id=1, source_target_pairs={{0,4},{4,0},{8,12},{12,8},{16,20},{20,16},{24,28},{28,24},{32,36},... | collective-permute-start | bytes 1572872 | tf_op jit(solution)/shard_map/ppermute | solution.py:411
  58.8 22.0 %collective-permute-start.15 = (bf16[256,1280]{1,0:T(8,128)(2,1)}, bf16[256,1280]{1,0:T(8,128)(2,1)}, u32[]{:S(2)}, u32[]{:S(2)}) collective-permute-start(bf16[256,1280]{1,0:T(8,128)(2,1)} %get-tuple-element.35.refs_0_), channel_id=1, source_target_pairs={{0,1},{1,2},{2,3},{3,0},{4,5},{5,6},{6,7},{7,4},{8,9},{9,10},{10,1... | collective-permute-start | bytes 1966088 | tf_op jit(solution)/shard_map/ppermute | solution.py:417
  60.4 21.9 %collective-permute-start.14 = (bf16[256,1280]{1,0:T(8,128)(2,1)}, bf16[256,1280]{1,0:T(8,128)(2,1)S(1)}, u32[]{:S(2)}, u32[]{:S(2)}) collective-permute-start(bf16[256,1280]{1,0:T(8,128)(2,1)} %get-tuple-element.35.refs_0_), channel_id=1, source_target_pairs={{0,3},{1,0},{2,1},{3,2},{4,7},{5,4},{6,5},{7,6},{8,11},{9,8},{10,9... | collective-permute-start | bytes 1966088 | tf_op jit(solution)/shard_map/ppermute | solution.py:417
  66.7 31.3 %collective-permute-start.19 = (bf16[256,1536]{1,0:T(8,128)(2,1)}, bf16[256,1536]{1,0:T(8,128)(2,1)S(1)}, u32[]{:S(2)}, u32[]{:S(2)}) collective-permute-start(bf16[256,1536]{1,0:T(8,128)(2,1)} %shard_map.65.refs_4_), channel_id=1, source_target_pairs={{0,1},{1,2},{2,3},{3,0},{4,5},{5,6},{6,7},{7,4},{8,9},{9,10},{10,1... | collective-permute-start | bytes 2359304 | tf_op jit(solution)/shard_map/ppermute | solution.py:417
  67.1 28.1 %collective-permute-start.17 = (bf16[256,1536]{1,0:T(8,128)(2,1)}, bf16[256,1536]{1,0:T(8,128)(2,1)}, u32[]{:S(2)}, u32[]{:S(2)}) collective-permute-start(bf16[256,1536]{1,0:T(8,128)(2,1)} %shard_map.65.refs_4_), channel_id=1, source_target_pairs={{0,3},{1,0},{2,1},{3,2},{4,7},{5,4},{6,5},{7,6},{8,11},{9,8},{10,9... | collective-permute-start | bytes 2359304 | tf_op jit(solution)/shard_map/ppermute | solution.py:417
  80.2 31.7 %collective-permute-start.11 = (bf16[256,1536]{1,0:T(8,128)(2,1)}, bf16[256,1536]{1,0:T(8,128)(2,1)S(1)}, u32[]{:S(2)}, u32[]{:S(2)}) collective-permute-start(bf16[256,1536]{1,0:T(8,128)(2,1)} %carried.1.refs_0_), channel_id=1, source_target_pairs={{0,3},{1,0},{2,1},{3,2},{4,7},{5,4},{6,5},{7,6},{8,11},{9,8},{10,9... | collective-permute-start | bytes 2359304 | tf_op jit(solution)/shard_map/ppermute | solution.py:417
  80.8 33.9 %collective-permute-start.16 = (bf16[256,1280]{1,0:T(8,128)(2,1)}, bf16[256,1280]{1,0:T(8,128)(2,1)}, u32[]{:S(2)}, u32[]{:S(2)}) collective-permute-start(bf16[256,1280]{1,0:T(8,128)(2,1)} %collective-permute-done.15.refs_3_), channel_id=1, source_target_pairs={{0,1},{1,2},{2,3},{3,0},{4,5},{5,6},{6,7},{7,4},{8,9},{9,10},{10,1... | collective-permute-start | bytes 1966088 | tf_op jit(solution)/shard_map/ppermute | solution.py:417
  82.3 15.8 %copy-start.9 = (bf16[256,1280]{1,0:T(8,128)(2,1)}, bf16[256,1280]{1,0:T(8,128)(2,1)S(1)}, u32[]{:S(2)}) copy-start(bf16[256,1280]{1,0:T(8,128)(2,1)S(1)} %collective-permute-done.14.refs_1_) | copy-start | bytes 1966084
  82.3 40.6 %collective-permute-start.21 = (bf16[128,2560]{1,0:T(8,128)(2,1)}, bf16[128,2560]{1,0:T(8,128)(2,1)}, u32[]{:S(2)}, u32[]{:S(2)}) collective-permute-start(bf16[128,2560]{1,0:T(8,128)(2,1)} %get-tuple-element.36.refs_8_), channel_id=1, source_target_pairs={{0,1},{1,2},{2,3},{3,0},{4,5},{5,6},{6,7},{7,4},{8,9},{9,10},{10,1... | collective-permute-start | bytes 1966088 | tf_op jit(solution)/shard_map/ppermute | solution.py:417
  95.2 33.7 %collective-permute-start.18 = (bf16[256,1536]{1,0:T(8,128)(2,1)}, bf16[256,1536]{1,0:T(8,128)(2,1)}, u32[]{:S(2)}, u32[]{:S(2)}) collective-permute-start(bf16[256,1536]{1,0:T(8,128)(2,1)} %collective-permute-done.17.refs_5_), channel_id=1, source_target_pairs={{0,3},{1,0},{2,1},{3,2},{4,7},{5,4},{6,5},{7,6},{8,11},{9,8},{10,9... | collective-permute-start | bytes 2359304 | tf_op jit(solution)/shard_map/ppermute | solution.py:417
  98.0 60.9 %copy-start.8 = (bf16[256,1536]{1,0:T(8,128)(2,1)}, bf16[256,1536]{1,0:T(8,128)(2,1)S(1)}, u32[]{:S(2)}) copy-start(bf16[256,1536]{1,0:T(8,128)(2,1)S(1)} %collective-permute-done.19.refs_7_) | copy-start | bytes 2359300
  98.0 67.7 %collective-permute-start.13 = (bf16[256,1536]{1,0:T(8,128)(2,1)}, bf16[256,1536]{1,0:T(8,128)(2,1)S(1)}, u32[]{:S(2)}, u32[]{:S(2)}) collective-permute-start(bf16[256,1536]{1,0:T(8,128)(2,1)} %carried.1.refs_0_), channel_id=1, source_target_pairs={{0,1},{1,2},{2,3},{3,0},{4,5},{5,6},{6,7},{7,4},{8,9},{9,10},{10,1... | collective-permute-start | bytes 2359304 | tf_op jit(solution)/shard_map/ppermute | solution.py:417
  111.9 53.8 %copy-start.5 = (bf16[256,1536]{1,0:T(8,128)(2,1)}, bf16[256,1536]{1,0:T(8,128)(2,1)S(1)}, u32[]{:S(2)}) copy-start(bf16[256,1536]{1,0:T(8,128)(2,1)S(1)} %collective-permute-done.11.refs_1_) | copy-start | bytes 2359300
  111.9 53.9 %collective-permute-start.12 = (bf16[256,1536]{1,0:T(8,128)(2,1)S(1)}, bf16[256,1536]{1,0:T(8,128)(2,1)S(1)}, u32[]{:S(2)}, u32[]{:S(2)}) collective-permute-start(bf16[256,1536]{1,0:T(8,128)(2,1)S(1)} %collective-permute-done.11.refs_1_), channel_id=1, source_target_pairs={{0,3},{1,0},{2,1},{3,2},{4,7},{5,4},{6,5},{7,6},{8,11},{9,8},{10,9... | collective-permute-start | bytes 2359304 | tf_op jit(solution)/shard_map/ppermute | solution.py:417
  114.8 44.2 %collective-permute-start.20 = (bf16[128,2560]{1,0:T(8,128)(2,1)}, bf16[128,2560]{1,0:T(8,128)(2,1)}, u32[]{:S(2)}, u32[]{:S(2)}) collective-permute-start(bf16[128,2560]{1,0:T(8,128)(2,1)} %get-tuple-element.36.refs_8_), channel_id=1, source_target_pairs={{0,3},{1,0},{2,1},{3,2},{4,7},{5,4},{6,5},{7,6},{8,11},{9,8},{10,9... | collective-permute-start | bytes 1966088 | tf_op jit(solution)/shard_map/ppermute | solution.py:417
  122.9 36.1 %collective-permute-start.22 = (bf16[128,2560]{1,0:T(8,128)(2,1)}, bf16[128,2560]{1,0:T(8,128)(2,1)}, u32[]{:S(2)}, u32[]{:S(2)}) collective-permute-start(bf16[128,2560]{1,0:T(8,128)(2,1)} %collective-permute-done.21.refs_11_), channel_id=1, source_target_pairs={{0,1},{1,2},{2,3},{3,0},{4,5},{5,6},{6,7},{7,4},{8,9},{9,10},{10,1... | collective-permute-start | bytes 1966088 | tf_op jit(solution)/shard_map/ppermute | solution.py:417
  165.8 0.9 copy-start.6
  166.7 0.9 copy-start.7
where the time goes:
time: 172 us; the launch traced here: 171 us
  waiting for transfers between devices  91.3 us (53%)
  Pallas kernels  42.2 us (25%)
  starting transfers between devices  30.3 us (18%)
  local copies, waits for them, and re-layouts  6.37 us (4%)
    ppermute x12, waiting for transfers between devices, over_docs(): return lax.ppermute(x, 'doc', [(d, (d + k) % doc_n) for d in range(doc_n)])  69 us
    ppermute x11, waiting for transfers between devices, shifted(): return lax.ppermute(x, 'seq', pairs)  22.3 us
    ppermute x12, starting transfers between devices, over_docs(): return lax.ppermute(x, 'doc', [(d, (d + k) % doc_n) for d in range(doc_n)])  15.5 us
    ppermute x11, starting transfers between devices, shifted(): return lax.ppermute(x, 'seq', pairs)  14.8 us
    pallas_call x2, Pallas kernels, local_of(): pl.pallas_call(functools.partial(local_kernel, base), out_shape=jax.Shape...  9.46 us
    pallas_call x1, Pallas kernels, whole(): pl.pallas_call(finish_kernel, name='finish', out_shape=result, in_specs=[...  6.78 us
    unnamed x23, local copies, waits for them, and re-layouts  6.37 us
    pallas_call x1, Pallas kernels, whole(): pl.pallas_call(states_kernel, name='states', out_shape=[half_shape] * 2,...  5.83 us
  transfers between devices with their start and end apart: 23, of which 15 were waited for; matrix products, arithmetic and copies ran while one was open for 0% of the time, Pallas kernels for 15%

commit v1 on v0

v1 whole, which is shorter than its diff:
```python
import functools

import jax
import jax.numpy as jnp
from jax import lax
from jax.experimental import pallas as pl
from jax.experimental.pallas import tpu as pltpu
from jax.sharding import PartitionSpec as P

Q = 128
ROW = 4
CORES = 2
GH = 8
HDIM = 64
WIDE = 1024
EARLY = (24, 16)
TAIL = 16
LOG2E = 1.4426950408889634
F32 = jnp.float32
BF = jnp.bfloat16


def iota(shape, dim):
    return lax.broadcasted_iota(jnp.int32, shape, dim)


def dot(a, b, ca=1, cb=0):
    return lax.dot_general(a, b, (((ca,), (cb,)), ((), ())), preferred_element_type=F32)


def core_at():
    return lax.rem(lax.axis_index("seq"), CORES)


def row_at():
    return lax.rem(lax.div(lax.axis_index("seq"), CORES), ROW)


def level_at():
    return lax.div(lax.axis_index("seq"), CORES * ROW)


def thirds(x):
    hi = x.astype(BF)
    rest = x - hi.astype(F32)
    mid = rest.astype(BF)
    lo = (rest - mid.astype(F32)).astype(BF)
    return hi, mid, lo


def triangle(n, strict_upper=False):
    rows, cols = iota((n, n), 0), iota((n, n), 1)
    keep = cols > rows if strict_upper else cols <= rows
    return jnp.where(keep, 1.0, 0.0).astype(BF)


def summed(weights, log_decay):
    heads = log_decay.shape[0]
    parts = jnp.concatenate([p.astype(F32) for p in thirds(log_decay)], axis=0).astype(BF)
    sums = dot(weights, parts, 1, 1)
    return sums[:, 0:heads] + sums[:, heads : 2 * heads] + sums[:, 2 * heads : 3 * heads]


def states_kernel(values_at, decay_at, b_at, mine, other, values, log_decay, b_in, pick, held, sems):
    tokens, width = values.shape
    wait = bring(((decay_at, log_decay), (b_at, b_in)), values_at, 0, values, WIDE, sems)
    n = b_in.shape[1]
    count = WIDE // HDIM
    steps = width // WIDE
    core = core_at()
    shape = pick.shape
    head = jnp.bitwise_and(iota(shape, 0), count - 1)
    keep = (head == lax.shift_right_logical(iota(shape, 1), HDIM.bit_length() - 1)) & (iota(shape, 0) < 3 * count)
    pick[...] = jnp.where(keep, 1.0, 0.0).astype(BF)
    wait()
    weights = jnp.concatenate([triangle(tokens, True), jnp.ones((TAIL, tokens), BF)], axis=0)
    parts = [p.astype(F32) for p in thirds(summed(weights, log_decay[...] * LOG2E))]
    for i in range(steps):
        cut = [p[:, i * count : (i + 1) * count] for p in parts]
        code = jnp.concatenate(cut + [jnp.zeros_like(cut[0])], axis=1).astype(BF)
        wide = dot(code, pick[...])
        wait(i)
        vals = values[:, i * WIDE : (i + 1) * WIDE].astype(F32)
        scaled = (vals * jnp.exp2(wide[0:tokens])).astype(BF)
        half, at = i * WIDE // mine.shape[1], i * WIDE % mine.shape[1]
        held[half, 0:n, at : at + WIDE] = dot(b_in[...], scaled, 0, 0).astype(BF)
        held[half, n:, at : at + WIDE] = tail_of(wide[tokens : tokens + 1])
    mine[...] = held[core]
    other[...] = held[1 - core]


def chip_kernel(mine, theirs, *refs):
    outs, earlier, held = refs[:-2], refs[-2], refs[-1]
    n, pw = outs[0].shape[0] - TAIL, outs[0].shape[1]
    core = core_at()
    for g in range(ROW):
        at = slice(g * pw, (g + 1) * pw)
        a, b = mine[0:n, at].astype(F32), theirs[0:n, at].astype(F32)
        ta, tb = tail_total(mine, n, at), tail_total(theirs, n, at)
        state = jnp.where(core == 0, jnp.exp2(tb), 1.0) * a + jnp.where(core == 0, 1.0, jnp.exp2(ta)) * b
        slot = lax.rem(g - row_at() + ROW, ROW)
        held[slot, 0:n, :] = state.astype(BF)
        held[slot, n:, :] = tail_of(ta + tb)
    for k, out in enumerate(outs):
        out[...] = held[k]

    @pl.when(core == 0)
    def _():
        earlier[...] = mine[...]

    @pl.when(core != 0)
    def _():
        earlier[...] = theirs[...]


def tail_total(piece, n, lanes):
    tail = piece[n : n + TAIL, lanes].astype(F32)
    return tail[0:1] + tail[1:2] + tail[2:3]


def tail_of(total):
    hi, mid, lo = thirds(total)
    row = iota((TAIL, total.shape[1]), 0)
    tail = jnp.where(row == 0, hi.astype(F32), jnp.where(row == 1, mid.astype(F32), lo.astype(F32)))
    return tail.astype(BF)


def total_of(piece, n):
    tail = piece[n : n + TAIL, :].astype(F32)
    return tail[0:1] + tail[1:2] + tail[2:3]


def row_kernel(*refs):
    pieces, out = refs[:-1], refs[-1]
    n = out.shape[0] - TAIL
    me = row_at()
    where = [lax.rem(me - k + ROW, ROW) for k in range(ROW)]
    totals = [total_of(p, n) for p in pieces]
    acc = jnp.zeros((n, out.shape[1]), F32)
    for k in range(ROW):
        later = jnp.zeros_like(totals[0])
        for j in range(ROW):
            if j != k:
                later = later + jnp.where(where[j] > where[k], totals[j], 0.0)
        acc = acc + jnp.exp2(later) * pieces[k][0:n, :].astype(F32)
    total = totals[0]
    for j in range(1, ROW):
        total = total + totals[j]
    out[0:n, :] = acc.astype(BF)
    out[n:, :] = tail_of(total)


def enter_kernel(*refs):
    pieces, rows = refs[:ROW], refs[ROW : ROW + 3]
    outs, held, totals, sent = refs[ROW + 3 : 2 * ROW + 3], refs[-3], refs[-2], refs[-1]
    n = outs[0].shape[0]
    me = row_at()
    for k in range(ROW):
        slot = lax.rem(me - k + ROW, ROW)
        held[slot] = pieces[k][0:n, :]
        totals[slot] = jnp.broadcast_to(total_of(pieces[k], n), totals.shape[1:])
    one, two, three = rows
    level = level_at()
    near = total_of(one, n)
    zero = jnp.zeros_like(near)
    enter = jnp.where(level > 0, zero + 1.0, zero) * one[0:n, :].astype(F32)
    enter = enter + jnp.where(level > 1, jnp.exp2(near), zero) * two[0:n, :].astype(F32)
    near = near + total_of(two, n)
    enter = enter + jnp.where(level > 2, jnp.exp2(near), zero) * three[0:n, :].astype(F32)
    for q in range(ROW):
        sent[lax.rem(q - me + ROW, ROW)] = enter.astype(BF)
        if q + 1 < ROW:
            enter = jnp.exp2(totals[q][0:1]) * enter + held[q].astype(F32)
    for k in range(ROW):
        outs[k][...] = sent[k]


def token_sums(lower, log_decay):
    heads = log_decay.shape[0]
    parts = jnp.concatenate([p.astype(F32) for p in thirds(log_decay * LOG2E)], axis=0).astype(BF)
    sums = dot(lower, parts, 1, 1)
    line = dot(parts, lower, 1, 1)
    return (
        sums[:, 0:heads] + sums[:, heads : 2 * heads] + sums[:, 2 * heads : 3 * heads],
        line[0:heads] + line[heads : 2 * heads] + line[2 * heads : 3 * heads],
    )


def local_part(skip, first_head, vals, sums, line, scores, emit):
    tokens, width = vals.shape
    hdim = width // GH
    blocks = tokens // Q
    keep = iota((Q, Q), 0) >= iota((Q, Q), 1)
    lanes = iota((Q, 2 * hdim), 1) < hdim
    for pair in range(GH // 2):
        col = slice(pair * 2 * hdim, (pair + 1) * 2 * hdim)
        mine = vals[:, col]
        halves = [
            [jnp.where(lanes, mine[j * Q : (j + 1) * Q], 0).astype(BF) for j in range(blocks)],
            [jnp.where(lanes, 0, mine[j * Q : (j + 1) * Q]).astype(BF) for j in range(blocks)],
        ]
        gain = jnp.where(lanes[0:1], skip[first_head + 2 * pair], skip[first_head + 2 * pair + 1])
        for i in range(blocks):
            left, right = [], []
            for side in range(2):
                head = 2 * pair + side
                column = jnp.broadcast_to(sums[i * Q : (i + 1) * Q, head : head + 1], (Q, Q))
                for j in range(i + 1):
                    gap = column - line[head : head + 1, j * Q : (j + 1) * Q]
                    if i == j:
                        gap = jnp.where(keep, gap, -1e30)
                    here = scores[i * Q : (i + 1) * Q, j * Q : (j + 1) * Q]
                    left.append((here * jnp.exp2(gap)).astype(BF))
                    right.append(halves[side][j])
            acc = dot(jnp.concatenate(left, axis=1), jnp.concatenate(right, axis=0))
            emit(i, pair * 2 * hdim, acc + gain * mine[i * Q : (i + 1) * Q].astype(F32))


def bring(small, values_at, first_lane, values, width, sems):
    n = len(small)
    copies = [pltpu.make_async_copy(x, y, sems.at[i]) for i, (x, y) in enumerate(small)]

    def lanes(i):
        at = i * width
        if not isinstance(i, int):
            at = pl.multiple_of(at, width)
        return pltpu.make_async_copy(
            values_at.at[:, pl.ds(first_lane + at, width)], values.at[:, pl.ds(at, width)], sems.at[n + i]
        )

    for copy in copies:
        copy.start()
    for i in range(values.shape[1] // width):
        lanes(i).start()

    def wait(i=None):
        if i is not None:
            lanes(i).wait()
            return
        for copy in copies:
            copy.wait()

    return wait


def local_groups(start, skip, values, sums, line, scores, emit, wait):
    width = GH * HDIM
    for i in range(values.shape[1] // width):
        wait(i)
        heads = slice(i * GH, (i + 1) * GH)

        def put(block, lane, x):
            emit(block, i * width + lane, x)

        vals = values[:, i * width : (i + 1) * width]
        local_part(skip, start + i * GH, vals, sums[:, heads], line[heads], scores, put)


def first_local_kernel(skip, values_at, decay_at, b_at, c_at, out, values, log_decay, b_in, c_in, lower, scores, sems):
    tokens = values.shape[0]
    heads = log_decay.shape[0]
    ends = out.shape[1] - 2 * Q
    small = ((decay_at, log_decay), (b_at, b_in), (c_at, c_in))
    wait = bring(small, values_at, 0, values, GH * HDIM, sems)
    lower[...] = triangle(tokens)
    wait()
    scores[...] = dot(c_in[...], b_in[...], 1, 1)
    sums, line = token_sums(lower[...], log_decay[...])
    out[:, ends : ends + Q] = c_in[...]
    decay = jnp.concatenate([jnp.exp2(sums), jnp.zeros((tokens, Q - heads), F32)], axis=1)
    out[:, ends + Q :] = decay.astype(BF)

    def emit(i, at, x):
        out[i * Q : (i + 1) * Q, at : at + x.shape[1]] = x.astype(BF)

    local_groups(0, skip, values, sums, line, scores, emit, wait)


def other_local_kernel(start, skip, values_at, decay_at, b_at, c_at, out, values, log_decay, b_in, c_in, lower, scores, sems):
    small = ((decay_at, log_decay), (b_at, b_in), (c_at, c_in))
    wait = bring(small, values_at, start * HDIM, values, GH * HDIM, sems)
    lower[...] = triangle(values.shape[0])
    wait()
    scores[...] = dot(c_in[...], b_in[...], 1, 1)
    count = values.shape[1] // HDIM
    sums, line = token_sums(lower[...], log_decay[start : start + count, :])

    def emit(i, at, x):
        out[i * Q : (i + 1) * Q, at : at + x.shape[1]] = x.astype(BF)

    local_groups(start, skip, values, sums, line, scores, emit, wait)


def late_kernel(
    start, skip, enter, first_at, values_at, decay_at, b_at, c_at, out,
    decays, values, log_decay, b_in, c_in, lower, scores, sems,
):
    small = (
        (decay_at, log_decay),
        (b_at, b_in),
        (c_at, c_in),
        (first_at.at[:, pl.ds(first_at.shape[1] - Q, Q)], decays),
    )
    wait = bring(small, values_at, start * HDIM, values, GH * HDIM, sems)
    lower[...] = triangle(values.shape[0])
    wait()
    scores[...] = dot(c_in[...], b_in[...], 1, 1)
    count = values.shape[1] // HDIM
    sums, line = token_sums(lower[...], log_decay[start : start + count, :])
    row = iota((Q, Q), 0)
    side = lax.shift_right_logical(iota((Q, Q), 1), HDIM.bit_length() - 1)

    def emit(i, at, x):
        pick = jnp.where(row == side + (start + at // HDIM), 1.0, 0.0).astype(BF)
        rows = slice(i * Q, (i + 1) * Q)
        add = dot(decays[rows, :], pick) * dot(c_in[rows, :], enter[:, at : at + Q])
        out[rows, at : at + Q] = (x + add).astype(BF)

    local_groups(start, skip, values, sums, line, scores, emit, wait)


def put_half(half, lanes, value, early, late):
    at = half * (early.shape[1] + late.shape[1]) // CORES + lanes.start
    size = lanes.stop - lanes.start
    if at + size <= early.shape[1]:
        early[:, at : at + size] = value
    else:
        late[:, at - early.shape[1] : at - early.shape[1] + size] = value


def split_kernel(earlier, *refs):
    enters, early, late, give, held = refs[:ROW], refs[ROW], refs[ROW + 1], refs[ROW + 2], refs[ROW + 3]
    n, pw = enters[0].shape
    core = core_at()
    for k in range(ROW):
        held[lax.rem(row_at() - k + ROW, ROW)] = enters[k][...]

    def emit(half):
        for g in range(ROW):
            at = slice(g * pw, (g + 1) * pw)
            enter = held[g]
            decay = jnp.exp2(tail_total(earlier, n, at))
            after = (decay * enter.astype(F32) + earlier[0:n, at].astype(F32)).astype(BF)
            put_half(half, at, enter if half == 0 else after, early, late)
            give[:, at] = after if half == 0 else enter

    for half in range(CORES):

        @pl.when(core == half)
        def _():
            emit(half)


def sorted_kernel(got, early_in, late_in, early, late):
    for half in range(CORES):

        @pl.when(core_at() != half)
        def _():
            for at in range(0, got.shape[1], GH * HDIM):
                lanes = slice(at, at + GH * HDIM)
                put_half(half, lanes, got[:, lanes], early, late)


def owned_plan(owner, docs):
    me = lax.axis_index("doc")
    plans = []
    for r in range(docs):
        doc = lax.rem(me + r, docs)
        first, second = owner[doc, 0] == me, owner[doc, 1] == me
        plans.append((doc, first, second))
    return plans


def write_owned(plan, r, rows, out, lanes, sems, zeros=None, act="start"):
    doc, first, second = plan
    both = jnp.logical_and(first, second)

    def go(when, source, to, i):
        @pl.when(when)
        def _():
            copy = pltpu.make_async_copy(source, out.at[to, :, lanes], sems.at[2 * r + i])
            copy.start() if act == "start" else copy.wait()

    if rows is not None:
        go(first, rows.at[0:Q], 2 * doc, 0)
        go(jnp.logical_and(jnp.logical_not(first), second), rows.at[Q : 2 * Q], 2 * doc, 0)
        go(both, rows.at[Q : 2 * Q], 2 * doc + 1, 1)
    if zeros is not None:
        go(jnp.logical_not(jnp.logical_or(first, second)), zeros, 2 * doc, 0)
        go(jnp.logical_not(both), zeros, 2 * doc + 1, 1)


def read_part(sources, r, target, sems, act="start"):
    copy = pltpu.make_async_copy(sources[r], target.at[r], sems.at[r])
    copy.start() if act == "start" else copy.wait()


def finish_kernel(owner, *refs):
    firsts, others, enters = refs[0:4], refs[4:8], refs[8:12]
    out, first, other, enter, done, zeros, s_first, s_other, s_enter, s_out, s_zero = refs[12:]
    plans = owned_plan(owner, 4)
    groups = ((firsts, first, s_first), (others, other, s_other), (enters, enter, s_enter))
    lanes = pl.ds(0, done.shape[2])

    def some(plan):
        return jnp.logical_or(plan[1], plan[2])

    for r, plan in enumerate(plans):

        @pl.when(some(plan))
        def _():
            for sources, target, sems in groups:
                read_part(sources, r, target, sems)

    zeros[...] = jnp.zeros_like(zeros)
    for r, plan in enumerate(plans):
        write_owned(plan, r, None, out, pl.ds(0, zeros.shape[1]), s_zero, zeros)

    ends = first.shape[2] - 2 * Q
    step = 512
    for r, plan in enumerate(plans):

        @pl.when(some(plan))
        def _():
            for sources, target, sems in groups:
                read_part(sources, r, target, sems, "wait")
            c = first[r, :, ends : ends + Q]
            decay = first[r, :, ends + Q :]
            for at in range(0, done.shape[2], step):
                head = iota((Q, step), 0)
                pick = jnp.where(head == (iota((Q, step), 1) + at) // HDIM, 1.0, 0.0).astype(BF)
                add = dot(decay, pick) * dot(c, enter[r, :, at : at + step])
                here = first[r, :, at : at + step] if at < ends else other[r, :, at - ends : at - ends + step]
                done[r, :, at : at + step] = (here.astype(F32) + add).astype(BF)

        write_owned(plan, r, done.at[r], out, lanes, s_out)
    for r, plan in enumerate(plans):
        write_owned(plan, r, done.at[r], out, lanes, s_out, None, "wait")
        write_owned(plan, r, None, out, pl.ds(0, zeros.shape[1]), s_zero, zeros, "wait")


def owned_kernel(first_lane, owner, *refs):
    sources = refs[:4]
    out, held, s_in, s_out = refs[-4:]
    plans = owned_plan(owner, 4)
    lanes = pl.ds(first_lane, held.shape[2])
    for act in ("start", "wait"):
        for r, plan in enumerate(plans):

            @pl.when(jnp.logical_or(plan[1], plan[2]))
            def _():
                read_part(sources, r, held, s_in, act)

            if act == "wait":
                write_owned(plan, r, held.at[r], out, lanes, s_out)
    for r, plan in enumerate(plans):
        write_owned(plan, r, held.at[r], out, lanes, s_out, None, "wait")


def inside(shape):
    return pltpu.VMEM(shape.shape, shape.dtype)


def near(arrays):
    return [pltpu.with_memory_space_constraint(x, pltpu.VMEM) for x in arrays]


def far(arrays):
    return [pltpu.with_memory_space_constraint(x, pltpu.HBM) for x in arrays]


def whole(values, b_in, c_in, log_decay, skip, owner):
    seq_n = lax.axis_size("seq")
    doc_n = lax.axis_size("doc")
    per_level = ROW * CORES
    levels = seq_n // per_level
    values, b_in, c_in, log_decay = values[0], b_in[0], c_in[0], log_decay[0]
    tokens, width = values.shape
    heads = log_decay.shape[0]
    n = b_in.shape[1]

    def shifted(x, step_x=0, step_z=0, swap=0):
        pairs = []
        for i in range(seq_n):
            z, at, core = i // per_level, i % per_level // CORES, i % CORES
            z, at, core = (z + step_z) % levels, (at + step_x) % ROW, (core + swap) % CORES
            pairs.append((i, z * per_level + at * CORES + core))
        return lax.ppermute(x, "seq", pairs)

    def along_row(pieces):
        return [pieces[0]] + [shifted(pieces[k], step_x=k) for k in range(1, ROW)]

    def over_docs(x, k):
        return lax.ppermute(x, "doc", [(d, (d + k) % doc_n) for d in range(doc_n)])

    def over_all_docs(x, far_by):
        before = over_docs(x, 1)
        after = over_docs(x, doc_n - 1)
        far = over_docs(before, 1) if far_by > 0 else over_docs(after, doc_n - 1)
        return [x, after, far, before]

    smem = pl.BlockSpec(memory_space=pltpu.SMEM)
    vmem = pl.BlockSpec(memory_space=pltpu.VMEM)
    anywhere = pl.BlockSpec(memory_space=pl.ANY)
    early = sum(EARLY)
    early_width = early * HDIM

    first_width = EARLY[0] * HDIM
    dma = pltpu.SemaphoreType.DMA

    def local_scratch(count, small=3):
        return [
            pltpu.VMEM((tokens, count * HDIM), BF),
            pltpu.VMEM((heads, tokens), F32),
            pltpu.VMEM((tokens, n), BF),
            pltpu.VMEM((tokens, n), BF),
            pltpu.VMEM((tokens, tokens), BF),
            pltpu.VMEM((tokens, tokens), F32),
            dma((small + count // GH,)),
        ]

    first = pl.pallas_call(
        first_local_kernel,
        name="local_first",
        out_shape=jax.ShapeDtypeStruct((tokens, first_width + 2 * Q), BF),
        in_specs=[smem] + [anywhere] * 4,
        out_specs=vmem,
        scratch_shapes=local_scratch(EARLY[0]),
    )(skip, values, log_decay, b_in, c_in)
    firsts = over_all_docs(first, -1)

    half = width // CORES
    pw = half // ROW
    half_shape = jax.ShapeDtypeStruct((n + TAIL, half), BF)
    piece = jax.ShapeDtypeStruct((n + TAIL, pw), BF)
    mine, other_half = pl.pallas_call(
        states_kernel,
        name="states",
        out_shape=[inside(half_shape)] * 2,
        in_specs=[anywhere] * 3,
        out_specs=[vmem] * 2,
        scratch_shapes=[
            pltpu.VMEM((tokens, width), BF),
            pltpu.VMEM((heads, tokens), F32),
            pltpu.VMEM((tokens, n), BF),
            pltpu.VMEM((4 * WIDE // HDIM, WIDE), BF),
            pltpu.VMEM((CORES,) + half_shape.shape, BF),
            dma((2 + width // WIDE,)),
        ],
    )(values, log_decay, b_in)
    theirs = shifted(other_half, swap=1)
    *pieces, earlier = pl.pallas_call(
        chip_kernel,
        name="chip",
        out_shape=[inside(piece)] * ROW + [inside(half_shape)],
        in_specs=[vmem, vmem],
        out_specs=[vmem] * (ROW + 1),
        scratch_shapes=[pltpu.VMEM((ROW,) + piece.shape, BF)],
    )(*near([mine, theirs]))
    pieces = along_row(pieces)

    other = pl.pallas_call(
        functools.partial(other_local_kernel, EARLY[0]),
        name="local_other",
        out_shape=jax.ShapeDtypeStruct((tokens, EARLY[1] * HDIM), BF),
        in_specs=[smem] + [anywhere] * 4,
        out_specs=vmem,
        scratch_shapes=local_scratch(EARLY[1]),
    )(skip, values, log_decay, b_in, c_in)
    others = over_all_docs(other, 1)

    row = pl.pallas_call(
        row_kernel, name="row", out_shape=inside(piece), in_specs=[vmem] * ROW, out_specs=vmem
    )(*near(pieces))
    rows = [shifted(row, step_z=k) for k in (1, 2, 3)]
    enter = jax.ShapeDtypeStruct((n, pw), BF)
    enters = pl.pallas_call(
        enter_kernel,
        name="enter",
        out_shape=[inside(enter)] * ROW,
        in_specs=[vmem] * (ROW + 3),
        out_specs=[vmem] * ROW,
        scratch_shapes=[
            pltpu.VMEM((ROW, n, pw), BF),
            pltpu.VMEM((ROW, 8, pw), F32),
            pltpu.VMEM((ROW, n, pw), BF),
        ],
    )(*near(pieces + rows))
    enters = along_row(enters)
    enter_shapes = [pltpu.VMEM((n, early_width), BF), pltpu.VMEM((n, width - early_width), BF)]
    enter_early, enter_late, give = pl.pallas_call(
        split_kernel,
        name="split",
        out_shape=enter_shapes + [pltpu.VMEM((n, half), BF)],
        in_specs=[vmem] * (ROW + 1),
        out_specs=[vmem] * 3,
        scratch_shapes=[pltpu.VMEM((ROW, n, pw), BF)],
    )(*near([earlier] + enters))
    got = shifted(give, swap=1)
    enter_early, enter_late = pl.pallas_call(
        sorted_kernel,
        name="sorted",
        out_shape=enter_shapes,
        in_specs=[vmem] * 3,
        out_specs=[vmem] * 2,
        input_output_aliases={1: 0, 2: 1},
    )(*near([got, enter_early, enter_late]))
    early_enters = over_all_docs(enter_early, -1)

    late_width = width - early_width
    late = pl.pallas_call(
        functools.partial(late_kernel, early),
        name="late",
        out_shape=pltpu.VMEM((tokens, late_width), BF),
        in_specs=[smem, vmem] + [anywhere] * 5,
        out_specs=vmem,
        scratch_shapes=[pltpu.VMEM((tokens, Q), BF)] + local_scratch(heads - early, 4),
    )(skip, *near([enter_late]), first, values, log_decay, b_in, c_in)
    lates = over_all_docs(late, 1)

    result = jax.ShapeDtypeStruct((doc_n * 2, Q, width), BF)
    owned = pl.pallas_call(
        finish_kernel,
        name="finish",
        out_shape=result,
        in_specs=[smem] + [anywhere] * 12,
        out_specs=anywhere,
        scratch_shapes=[
            pltpu.VMEM((doc_n,) + first.shape, BF),
            pltpu.VMEM((doc_n,) + other.shape, BF),
            pltpu.VMEM((doc_n,) + enter_early.shape, BF),
            pltpu.VMEM((doc_n, tokens, early_width), BF),
            pltpu.VMEM((Q, width), BF),
            dma((doc_n,)),
            dma((doc_n,)),
            dma((doc_n,)),
            dma((doc_n * 2,)),
            dma((doc_n * 2,)),
        ],
    )(owner, *far(firsts), *far(others), *far(early_enters))
    owned = pl.pallas_call(
        functools.partial(owned_kernel, early_width),
        name="owned",
        out_shape=result,
        in_specs=[smem] + [anywhere] * 5,
        out_specs=anywhere,
        scratch_shapes=[pltpu.VMEM((doc_n,) + late.shape, BF), dma((doc_n,)), dma((doc_n * 2,))],
        input_output_aliases={5: 0},
    )(owner, *far(lates), owned)
    return owned[None]


def solution(mesh):
    in_specs = (
        P("doc", "seq", None),
        P("doc", "seq", None),
        P("doc", "seq", None),
        P("doc", None, "seq"),
        P(),
        P(None, "seq"),
    )
    out_specs = P("doc", "seq", None, None)
    return jax.shard_map(whole, mesh=mesh, in_specs=in_specs, out_specs=out_specs, check_vma=False)
```

time: 172 us -> 162 us (0.942)
  Pallas kernels: 42.2 us -> 27.1 us
  waiting for transfers between devices: 91.3 us -> 101 us
  local copies, waits for them, and re-layouts: 6.37 us -> 2.13 us
    pallas_call x10 -> x9, Pallas kernels: 32.1 us -> 16.9 us  [the longest x1 4.61 us: whole(): pl.pallas_call(first_local_kernel, name='local_first', out_shape=jax.Shap...]
    ppermute x12, waiting for transfers between devices: 69 us -> 79.7 us  [over_docs(): return lax.ppermute(x, 'doc', [(d, (d + k) % doc_n) for d in range(doc_n)])]
    unnamed x23 -> x17, local copies, waits for them, and re-layouts: 6.37 us -> 2.13 us
  transfers between devices with their start and end apart: 23 -> 23, of which waited for: 15 -> 17; matrix products, arithmetic and copies ran while one was open for 0% -> 0% of each run, Pallas kernels for 15% -> 12%
where the time goes in v1:
time: 162 us
  waiting for transfers between devices  101 us (62%)
  starting transfers between devices  30.8 us (19%)
  Pallas kernels  27.1 us (17%)
  local copies, waits for them, and re-layouts  2.13 us (1%)
    ppermute x12, waiting for transfers between devices, over_docs(): return lax.ppermute(x, 'doc', [(d, (d + k) % doc_n) for d in range(doc_n)])  79.7 us
    ppermute x11, waiting for transfers between devices, shifted(): return lax.ppermute(x, 'seq', pairs)  21.5 us
    ppermute x12, starting transfers between devices, over_docs(): return lax.ppermute(x, 'doc', [(d, (d + k) % doc_n) for d in range(doc_n)])  15.7 us
    ppermute x11, starting transfers between devices, shifted(): return lax.ppermute(x, 'seq', pairs)  15.1 us
    pallas_call x1, Pallas kernels, whole(): pl.pallas_call(finish_kernel, name='finish', out_shape=result, in_specs=[...  6.78 us
    pallas_call x1, Pallas kernels, whole(): pl.pallas_call(first_local_kernel, name='local_first', out_shape=jax.Shap...  4.61 us
    pallas_call x1, Pallas kernels, whole(): pl.pallas_call(functools.partial(other_local_kernel, EARLY[0]), name='loc...  3.82 us
    pallas_call x1, Pallas kernels, whole(): pl.pallas_call(functools.partial(late_kernel, early), name='late', out_sh...  3.8 us
  transfers between devices with their start and end apart: 23, of which 17 were waited for; matrix products, arithmetic and copies ran while one was open for 0% of the time, Pallas kernels for 12%

profile of v1, /device:TPU:2, one launch (start us, length us, event | category | flops | bytes accessed | tf_op | source)
XLA Modules:
  0.0 161.5 jit_solution(8458918114213747164)
XLA Ops:
  0.0 3.5 %states.1 = (bf16[144,2048]{1,0:T(8,128)(2,1)S(1)}, bf16[144,2048]{1,0:T(8,128)(2,1)S(1)}) custom-call(bf16[256,4096]{1,0:T(8,128)(2,1)} %bitcast.5, f32[64,256]{1,0:T(8,128)} %bitcast.9, bf16[256,128]{1,0:T(8,128)(2,1)} %bitcast.13), custom_call_target="tpu_custom_call" | custom-call | tf_op jit(solution)/shard_map/states/pallas_call | solution.py:536
  3.5 0.0 copy-start.7
  3.5 0.1 collective-permute-start
  3.6 2.0 %collective-permute-done.theirs = bf16[144,2048]{1,0:T(8,128)(2,1)S(1)} collective-permute-done((bf16[144,2048]{1,0:T(8,128)(2,1)S(1)}, bf16[144,2048]{1,0:T(8,128)(2,1)S(1)}, u32[]{:S(2)}, u32[]{:S(2)}) %collective-permute-start) | collective-permute-done | bytes 589856 | tf_op jit(solution)/shard_map/ppermute | solution.py:488
  5.6 0.4 chip.1
  6.1 0.0 copy-start.2
  6.1 1.6 collective-permute-start.1
  7.6 1.0 collective-permute-start.2
  8.6 2.3 %collective-permute-start.3 = (bf16[144,512]{1,0:T(8,128)(2,1)S(1)}, bf16[144,512]{1,0:T(8,128)(2,1)S(1)}, u32[]{:S(2)}, u32[]{:S(2)}) collective-permute-start(bf16[144,512]{1,0:T(8,128)(2,1)S(1)} %get-tuple-element.27), channel_id=1, source_target_pairs={{0,24},{4,28},{8,0},{12,4},{16,8},{20,12},{24,16},{28,20},{32,56},... | collective-permute-start | bytes 442376 | tf_op jit(solution)/shard_map/ppermute | solution.py:488
  10.9 1.8 %collective-permute-done.1.refs_1_ = bf16[144,512]{1,0:T(8,128)(2,1)S(1)} collective-permute-done((bf16[144,512]{1,0:T(8,128)(2,1)S(1)}, bf16[144,512]{1,0:T(8,128)(2,1)S(1)}, u32[]{:S(2)}, u32[]{:S(2)}) %collective-permute-start.1) | collective-permute-done | bytes 147488 | tf_op jit(solution)/shard_map/ppermute | solution.py:488
  12.7 3.1 %collective-permute-done.2.refs_2_ = bf16[144,512]{1,0:T(8,128)(2,1)S(1)} collective-permute-done((bf16[144,512]{1,0:T(8,128)(2,1)S(1)}, bf16[144,512]{1,0:T(8,128)(2,1)S(1)}, u32[]{:S(2)}, u32[]{:S(2)}) %collective-permute-start.2) | collective-permute-done | bytes 147488 | tf_op jit(solution)/shard_map/ppermute | solution.py:488
  15.9 1.3 collective-permute-done.3.refs_3_
  17.1 0.1 row.1
  17.3 4.2 %collective-permute-start.6 = (bf16[144,512]{1,0:T(8,128)(2,1)S(1)}, bf16[144,512]{1,0:T(8,128)(2,1)S(1)}, u32[]{:S(2)}, u32[]{:S(2)}) collective-permute-start(bf16[144,512]{1,0:T(8,128)(2,1)S(1)} %row.1), channel_id=1, source_target_pairs={{0,96},{4,100},{8,104},{12,108},{16,112},{20,116},{24,120},{28,124... | collective-permute-start | bytes 442376 | tf_op jit(solution)/shard_map/ppermute | solution.py:488
  21.5 0.0 collective-permute-start.5
  21.5 1.3 collective-permute-start.4
  22.8 4.5 %collective-permute-done.6.refs_6_ = bf16[144,512]{1,0:T(8,128)(2,1)S(1)} collective-permute-done((bf16[144,512]{1,0:T(8,128)(2,1)S(1)}, bf16[144,512]{1,0:T(8,128)(2,1)S(1)}, u32[]{:S(2)}, u32[]{:S(2)}) %collective-permute-start.6) | collective-permute-done | bytes 147488 | tf_op jit(solution)/shard_map/ppermute | solution.py:488
  27.3 2.2 %collective-permute-done.5.refs_5_ = bf16[144,512]{1,0:T(8,128)(2,1)S(1)} collective-permute-done((bf16[144,512]{1,0:T(8,128)(2,1)S(1)}, bf16[144,512]{1,0:T(8,128)(2,1)S(1)}, u32[]{:S(2)}, u32[]{:S(2)}) %collective-permute-start.5) | collective-permute-done | bytes 147488 | tf_op jit(solution)/shard_map/ppermute | solution.py:488
  29.4 1.2 collective-permute-done.4.refs_4_
  30.7 0.3 enter.1
  31.0 1.1 collective-permute-start.7
  32.1 1.7 %collective-permute-start.8 = (bf16[128,512]{1,0:T(8,128)(2,1)S(1)}, bf16[128,512]{1,0:T(8,128)(2,1)S(1)}, u32[]{:S(2)}, u32[]{:S(2)}) collective-permute-start(bf16[128,512]{1,0:T(8,128)(2,1)S(1)} %get-tuple-element.30), channel_id=1, source_target_pairs={{0,16},{4,20},{8,24},{12,28},{16,0},{20,4},{24,8},{28,12},{32,48},... | collective-permute-start | bytes 393224 | tf_op jit(solution)/shard_map/ppermute | solution.py:488
  33.8 1.9 %collective-permute-start.9 = (bf16[128,512]{1,0:T(8,128)(2,1)S(1)}, bf16[128,512]{1,0:T(8,128)(2,1)S(1)}, u32[]{:S(2)}, u32[]{:S(2)}) collective-permute-start(bf16[128,512]{1,0:T(8,128)(2,1)S(1)} %get-tuple-element.31), channel_id=1, source_target_pairs={{0,24},{4,28},{8,0},{12,4},{16,8},{20,12},{24,16},{28,20},{32,56},... | collective-permute-start | bytes 393224 | tf_op jit(solution)/shard_map/ppermute | solution.py:488
  35.7 1.1 collective-permute-done.7.refs_1_
  36.7 2.9 %collective-permute-done.8.refs_2_ = bf16[128,512]{1,0:T(8,128)(2,1)S(1)} collective-permute-done((bf16[128,512]{1,0:T(8,128)(2,1)S(1)}, bf16[128,512]{1,0:T(8,128)(2,1)S(1)}, u32[]{:S(2)}, u32[]{:S(2)}) %collective-permute-start.8) | collective-permute-done | bytes 131104 | tf_op jit(solution)/shard_map/ppermute | solution.py:488
  39.6 1.4 collective-permute-done.9.refs_3_
  41.0 0.0 copy-done.2
  41.0 1.1 copy-done.3
  42.0 0.3 split.1
  42.3 0.1 collective-permute-start.10
  42.4 3.8 %local_other.1.refs_4_ = bf16[256,1024]{1,0:T(8,128)(2,1)} custom-call(f32[64]{0:T(128)} %skip.5, bf16[256,4096]{1,0:T(8,128)(2,1)} %bitcast.6, f32[64,256]{1,0:T(8,128)} %bitcast.10, bf16[256,128]{1,0:T(8,128)(2,1)} %bitcast.14, bf16[256,128]{1,0:T(8,128)(2,1)} %bitcast.17), custom_call_target="tpu_custom_call" | custom-call | tf_op jit(solution)/shard_map/local_other/pallas_call | solution.py:562
  46.2 1.6 %collective-permute-start.18 = (bf16[256,1024]{1,0:T(8,128)(2,1)}, bf16[256,1024]{1,0:T(8,128)(2,1)}, u32[]{:S(2)}, u32[]{:S(2)}) collective-permute-start(bf16[256,1024]{1,0:T(8,128)(2,1)} %local_other.1.refs_4_), channel_id=1, source_target_pairs={{0,1},{1,2},{2,3},{3,0},{4,5},{5,6},{6,7},{7,4},{8,9},{9,10},{10,1... | collective-permute-start | bytes 1572872 | tf_op jit(solution)/shard_map/ppermute | solution.py:494
  47.9 4.6 %local_first.1.first_at.refs_0_ = bf16[256,1792]{1,0:T(8,128)(2,1)} custom-call(f32[64]{0:T(128)} %skip.5, bf16[256,4096]{1,0:T(8,128)(2,1)} %bitcast.7, f32[64,256]{1,0:T(8,128)} %bitcast.11, bf16[256,128]{1,0:T(8,128)(2,1)} %bitcast.15, bf16[256,128]{1,0:T(8,128)(2,1)} %bitcast.18), custom_call_target="tpu_custom_call" | custom-call | tf_op jit(solution)/shard_map/local_first/pallas_call | solution.py:522
  52.5 1.7 %collective-permute-start.14 = (bf16[256,1792]{1,0:T(8,128)(2,1)}, bf16[256,1792]{1,0:T(8,128)(2,1)S(1)}, u32[]{:S(2)}, u32[]{:S(2)}) collective-permute-start(bf16[256,1792]{1,0:T(8,128)(2,1)} %local_first.1.first_at.refs_0_), channel_id=1, source_target_pairs={{0,3},{1,0},{2,1},{3,2},{4,7},{5,4},{6,5},{7,6},{8,11},{9,8},{10,9... | collective-permute-start | bytes 2752520 | tf_op jit(solution)/shard_map/ppermute | solution.py:494
  54.2 1.8 %collective-permute-start.17 = (bf16[256,1024]{1,0:T(8,128)(2,1)}, bf16[256,1024]{1,0:T(8,128)(2,1)}, u32[]{:S(2)}, u32[]{:S(2)}) collective-permute-start(bf16[256,1024]{1,0:T(8,128)(2,1)} %local_other.1.refs_4_), channel_id=1, source_target_pairs={{0,3},{1,0},{2,1},{3,2},{4,7},{5,4},{6,5},{7,6},{8,11},{9,8},{10,9... | collective-permute-start | bytes 1572872 | tf_op jit(solution)/shard_map/ppermute | solution.py:494
  56.0 0.2 collective-permute-start.16
  56.3 0.0 collective-permute-done.10.got
  56.3 3.8 %late.1.refs_0_ = bf16[256,1536]{1,0:T(8,128)(2,1)S(1)} custom-call(f32[64]{0:T(128)} %skip.5, bf16[128,1536]{1,0:T(8,128)(2,1)S(1)} %get-tuple-element.35.enter, bf16[256,1792]{1,0:T(8,128)(2,1)} %local_first.1.first_at.refs_0_, bf16[256,4096]{1,0:T(8,128)(2,1)} %bitcast.8, f32[64,256]{1,0:T(8,128)} %bitcast.12, bf16[256,128]{1,0:T(8,128)(2,1)} %bitcast.16, ...), custom_call_target="tpu_custom_call" | custom-call | tf_op jit(solution)/shard_map/late/pallas_call | solution.py:611
  60.1 0.4 collective-permute-start.12
  60.6 2.1 %collective-permute-done.18.refs_7_ = bf16[256,1024]{1,0:T(8,128)(2,1)} collective-permute-done((bf16[256,1024]{1,0:T(8,128)(2,1)}, bf16[256,1024]{1,0:T(8,128)(2,1)}, u32[]{:S(2)}, u32[]{:S(2)}) %collective-permute-start.18) | collective-permute-done | bytes 524320 | tf_op jit(solution)/shard_map/ppermute | solution.py:494
  62.6 1.8 %collective-permute-start.20 = (bf16[128,2560]{1,0:T(8,128)(2,1)S(1)}, bf16[128,2560]{1,0:T(8,128)(2,1)}, u32[]{:S(2)}, u32[]{:S(2)}) collective-permute-start(bf16[128,2560]{1,0:T(8,128)(2,1)S(1)} %get-tuple-element.36.refs_8_), channel_id=1, source_target_pairs={{0,3},{1,0},{2,1},{3,2},{4,7},{5,4},{6,5},{7,6},{8,11},{9,8},{10,9... | collective-permute-start | bytes 1966088 | tf_op jit(solution)/shard_map/ppermute | solution.py:494
  64.4 22.9 %collective-permute-done.17.refs_5_ = bf16[256,1024]{1,0:T(8,128)(2,1)} collective-permute-done((bf16[256,1024]{1,0:T(8,128)(2,1)}, bf16[256,1024]{1,0:T(8,128)(2,1)}, u32[]{:S(2)}, u32[]{:S(2)}) %collective-permute-start.17) | collective-permute-done | bytes 524320 | tf_op jit(solution)/shard_map/ppermute | solution.py:494
  87.3 1.6 collective-permute-start.19
  88.9 0.0 collective-permute-done.14.refs_1_
  88.9 1.7 %collective-permute-start.15 = (bf16[256,1792]{1,0:T(8,128)(2,1)S(1)}, bf16[256,1792]{1,0:T(8,128)(2,1)S(1)}, u32[]{:S(2)}, u32[]{:S(2)}) collective-permute-start(bf16[256,1792]{1,0:T(8,128)(2,1)S(1)} %collective-permute-done.14.refs_1_), channel_id=1, source_target_pairs={{0,3},{1,0},{2,1},{3,2},{4,7},{5,4},{6,5},{7,6},{8,11},{9,8},{10,9... | collective-permute-start | bytes 2752520 | tf_op jit(solution)/shard_map/ppermute | solution.py:494
  90.6 0.0 collective-permute-done.16.refs_3_
  90.6 1.7 %collective-permute-start.11 = (bf16[256,1536]{1,0:T(8,128)(2,1)S(1)}, bf16[256,1536]{1,0:T(8,128)(2,1)}, u32[]{:S(2)}, u32[]{:S(2)}) collective-permute-start(bf16[256,1536]{1,0:T(8,128)(2,1)S(1)} %late.1.refs_0_), channel_id=1, source_target_pairs={{0,3},{1,0},{2,1},{3,2},{4,7},{5,4},{6,5},{7,6},{8,11},{9,8},{10,9... | collective-permute-start | bytes 2359304 | tf_op jit(solution)/shard_map/ppermute | solution.py:494
  92.3 6.9 %collective-permute-done.12.refs_3_ = bf16[256,1536]{1,0:T(8,128)(2,1)} collective-permute-done((bf16[256,1536]{1,0:T(8,128)(2,1)S(1)}, bf16[256,1536]{1,0:T(8,128)(2,1)}, u32[]{:S(2)}, u32[]{:S(2)}) %collective-permute-start.12) | collective-permute-done | bytes 786464 | tf_op jit(solution)/shard_map/ppermute | solution.py:494
  99.2 0.4 collective-permute-start.13
  99.5 10.8 %collective-permute-done.19.refs_6_ = bf16[256,1024]{1,0:T(8,128)(2,1)S(1)} collective-permute-done((bf16[256,1024]{1,0:T(8,128)(2,1)}, bf16[256,1024]{1,0:T(8,128)(2,1)S(1)}, u32[]{:S(2)}, u32[]{:S(2)}) %collective-permute-start.19) | collective-permute-done | bytes 524320 | tf_op jit(solution)/shard_map/ppermute | solution.py:494
  110.3 0.4 collective-permute-start.22
  110.6 0.0 collective-permute-done.20.refs_9_
  110.7 0.4 copy-done.6
  111.1 2.5 %collective-permute-start.21 = (bf16[128,2560]{1,0:T(8,128)(2,1)}, bf16[128,2560]{1,0:T(8,128)(2,1)}, u32[]{:S(2)}, u32[]{:S(2)}) collective-permute-start(bf16[128,2560]{1,0:T(8,128)(2,1)} %collective-permute-done.20.refs_9_), channel_id=1, source_target_pairs={{0,3},{1,0},{2,1},{3,2},{4,7},{5,4},{6,5},{7,6},{8,11},{9,8},{10,9... | collective-permute-start | bytes 1966088 | tf_op jit(solution)/shard_map/ppermute | solution.py:494
  113.5 0.0 copy-done.7
  113.5 0.6 copy.11.owner
  114.1 6.8 %collective-permute-done.15.refs_2_ = bf16[256,1792]{1,0:T(8,128)(2,1)S(1)} collective-permute-done((bf16[256,1792]{1,0:T(8,128)(2,1)S(1)}, bf16[256,1792]{1,0:T(8,128)(2,1)S(1)}, u32[]{:S(2)}, u32[]{:S(2)}) %collective-permute-start.15) | collective-permute-done | bytes 917536 | tf_op jit(solution)/shard_map/ppermute | solution.py:494
  120.9 19.9 %collective-permute-done.22.refs_11_ = bf16[128,2560]{1,0:T(8,128)(2,1)} collective-permute-done((bf16[128,2560]{1,0:T(8,128)(2,1)S(1)}, bf16[128,2560]{1,0:T(8,128)(2,1)}, u32[]{:S(2)}, u32[]{:S(2)}) %collective-permute-start.22) | collective-permute-done | bytes 655392 | tf_op jit(solution)/shard_map/ppermute | solution.py:494
  140.9 10.3 %collective-permute-done.21.refs_10_ = bf16[128,2560]{1,0:T(8,128)(2,1)} collective-permute-done((bf16[128,2560]{1,0:T(8,128)(2,1)}, bf16[128,2560]{1,0:T(8,128)(2,1)}, u32[]{:S(2)}, u32[]{:S(2)}) %collective-permute-start.21) | collective-permute-done | bytes 655392 | tf_op jit(solution)/shard_map/ppermute | solution.py:494
  151.2 6.8 %finish.1.refs_4_ = bf16[8,128,4096]{2,1,0:T(8,128)(2,1)} custom-call(s32[4,2]{1,0:T(4,128)} %copy.11.owner, bf16[256,1792]{1,0:T(8,128)(2,1)} %local_first.1.first_at.refs_0_, bf16[256,1792]{1,0:T(8,128)(2,1)} %copy-done.4, bf16[256,1792]{1,0:T(8,128)(2,1)} %copy-done.5, bf16[256,1792]{1,0:T(8,128)(2,1)} %collective-permute-done.16.refs_3_, ...), custom_call_target="tpu_custom_call" | custom-call | tf_op jit(solution)/shard_map/finish/pallas_call | solution.py:622
  158.0 0.0 copy-done
  158.0 0.0 collective-permute-done.11.refs_1_
  158.0 0.0 collective-permute-done.13.refs_2_
  158.0 3.3 %owned.1 = bf16[8,128,4096]{2,1,0:T(8,128)(2,1)} custom-call(s32[4,2]{1,0:T(4,128)} %copy.11.owner, bf16[256,1536]{1,0:T(8,128)(2,1)} %copy-done, bf16[256,1536]{1,0:T(8,128)(2,1)} %collective-permute-done.11.refs_1_, bf16[256,1536]{1,0:T(8,128)(2,1)} %collective-permute-done.13.refs_2_, ...), custom_call_target="tpu_custom_call", output_to_operand_aliasing={{}: (5, {})} | custom-call | tf_op jit(solution)/shard_map/owned/pallas_call | solution.py:641
  (10 shorter events, 0.1 us)
Async XLA Ops:
  3.5 110.0 %copy-start.7 = (s32[4,2]{0,1:T(2,128)S(1)}, s32[4,2]{0,1:T(2,128)}, u32[]{:S(2)}) copy-start(s32[4,2]{0,1:T(2,128)} %param.11) | copy-start | bytes 100
  3.5 2.1 %collective-permute-start = (bf16[144,2048]{1,0:T(8,128)(2,1)S(1)}, bf16[144,2048]{1,0:T(8,128)(2,1)S(1)}, u32[]{:S(2)}, u32[]{:S(2)}) collective-permute-start(bf16[144,2048]{1,0:T(8,128)(2,1)S(1)} %get-tuple-element.22), channel_id=1, source_target_pairs={{0,4},{4,0},{8,12},{12,8},{16,20},{20,16},{24,28},{28,24},{32,36},... | collective-permute-start | bytes 1769480 | tf_op jit(solution)/shard_map/ppermute | solution.py:488
  6.1 34.9 %copy-start.2 = (bf16[144,2048]{1,0:T(8,128)(2,1)}, bf16[144,2048]{1,0:T(8,128)(2,1)S(1)}, u32[]{:S(2)}) copy-start(bf16[144,2048]{1,0:T(8,128)(2,1)S(1)} %get-tuple-element.23.earlier) | copy-start | bytes 1769476
  6.1 6.7 %collective-permute-start.1 = (bf16[144,512]{1,0:T(8,128)(2,1)S(1)}, bf16[144,512]{1,0:T(8,128)(2,1)S(1)}, u32[]{:S(2)}, u32[]{:S(2)}) collective-permute-start(bf16[144,512]{1,0:T(8,128)(2,1)S(1)} %get-tuple-element.25), channel_id=1, source_target_pairs={{0,8},{4,12},{8,16},{12,20},{16,24},{20,28},{24,0},{28,4},{32,40},... | collective-permute-start | bytes 442376 | tf_op jit(solution)/shard_map/ppermute | solution.py:488
  7.6 8.2 %collective-permute-start.2 = (bf16[144,512]{1,0:T(8,128)(2,1)S(1)}, bf16[144,512]{1,0:T(8,128)(2,1)S(1)}, u32[]{:S(2)}, u32[]{:S(2)}) collective-permute-start(bf16[144,512]{1,0:T(8,128)(2,1)S(1)} %get-tuple-element.26), channel_id=1, source_target_pairs={{0,16},{4,20},{8,24},{12,28},{16,0},{20,4},{24,8},{28,12},{32,48},... | collective-permute-start | bytes 442376 | tf_op jit(solution)/shard_map/ppermute | solution.py:488
  8.6 8.5 %collective-permute-start.3 = (bf16[144,512]{1,0:T(8,128)(2,1)S(1)}, bf16[144,512]{1,0:T(8,128)(2,1)S(1)}, u32[]{:S(2)}, u32[]{:S(2)}) collective-permute-start(bf16[144,512]{1,0:T(8,128)(2,1)S(1)} %get-tuple-element.27), channel_id=1, source_target_pairs={{0,24},{4,28},{8,0},{12,4},{16,8},{20,12},{24,16},{28,20},{32,56},... | collective-permute-start | bytes 442376 | tf_op jit(solution)/shard_map/ppermute | solution.py:488
  17.3 10.0 %collective-permute-start.6 = (bf16[144,512]{1,0:T(8,128)(2,1)S(1)}, bf16[144,512]{1,0:T(8,128)(2,1)S(1)}, u32[]{:S(2)}, u32[]{:S(2)}) collective-permute-start(bf16[144,512]{1,0:T(8,128)(2,1)S(1)} %row.1), channel_id=1, source_target_pairs={{0,96},{4,100},{8,104},{12,108},{16,112},{20,116},{24,120},{28,124... | collective-permute-start | bytes 442376 | tf_op jit(solution)/shard_map/ppermute | solution.py:488
  21.5 7.9 %collective-permute-start.5 = (bf16[144,512]{1,0:T(8,128)(2,1)S(1)}, bf16[144,512]{1,0:T(8,128)(2,1)S(1)}, u32[]{:S(2)}, u32[]{:S(2)}) collective-permute-start(bf16[144,512]{1,0:T(8,128)(2,1)S(1)} %row.1), channel_id=1, source_target_pairs={{0,64},{4,68},{8,72},{12,76},{16,80},{20,84},{24,88},{28,92},{32,9... | collective-permute-start | bytes 442376 | tf_op jit(solution)/shard_map/ppermute | solution.py:488
  21.5 9.2 %collective-permute-start.4 = (bf16[144,512]{1,0:T(8,128)(2,1)S(1)}, bf16[144,512]{1,0:T(8,128)(2,1)S(1)}, u32[]{:S(2)}, u32[]{:S(2)}) collective-permute-start(bf16[144,512]{1,0:T(8,128)(2,1)S(1)} %row.1), channel_id=1, source_target_pairs={{0,32},{4,36},{8,40},{12,44},{16,48},{20,52},{24,56},{28,60},{32,6... | collective-permute-start | bytes 442376 | tf_op jit(solution)/shard_map/ppermute | solution.py:488
  31.0 5.7 %collective-permute-start.7 = (bf16[128,512]{1,0:T(8,128)(2,1)S(1)}, bf16[128,512]{1,0:T(8,128)(2,1)S(1)}, u32[]{:S(2)}, u32[]{:S(2)}) collective-permute-start(bf16[128,512]{1,0:T(8,128)(2,1)S(1)} %get-tuple-element.29), channel_id=1, source_target_pairs={{0,8},{4,12},{8,16},{12,20},{16,24},{20,28},{24,0},{28,4},{32,40},... | collective-permute-start | bytes 393224 | tf_op jit(solution)/shard_map/ppermute | solution.py:488
  32.1 7.5 %collective-permute-start.8 = (bf16[128,512]{1,0:T(8,128)(2,1)S(1)}, bf16[128,512]{1,0:T(8,128)(2,1)S(1)}, u32[]{:S(2)}, u32[]{:S(2)}) collective-permute-start(bf16[128,512]{1,0:T(8,128)(2,1)S(1)} %get-tuple-element.30), channel_id=1, source_target_pairs={{0,16},{4,20},{8,24},{12,28},{16,0},{20,4},{24,8},{28,12},{32,48},... | collective-permute-start | bytes 393224 | tf_op jit(solution)/shard_map/ppermute | solution.py:488
  33.8 7.2 %collective-permute-start.9 = (bf16[128,512]{1,0:T(8,128)(2,1)S(1)}, bf16[128,512]{1,0:T(8,128)(2,1)S(1)}, u32[]{:S(2)}, u32[]{:S(2)}) collective-permute-start(bf16[128,512]{1,0:T(8,128)(2,1)S(1)} %get-tuple-element.31), channel_id=1, source_target_pairs={{0,24},{4,28},{8,0},{12,4},{16,8},{20,12},{24,16},{28,20},{32,56},... | collective-permute-start | bytes 393224 | tf_op jit(solution)/shard_map/ppermute | solution.py:488
  41.0 1.1 copy-start.3
  42.3 13.9 %collective-permute-start.10 = (bf16[128,2048]{1,0:T(8,128)(2,1)S(1)}, bf16[128,2048]{1,0:T(8,128)(2,1)S(1)}, u32[]{:S(2)}, u32[]{:S(2)}) collective-permute-start(bf16[128,2048]{1,0:T(8,128)(2,1)S(1)} %get-tuple-element.32), channel_id=1, source_target_pairs={{0,4},{4,0},{8,12},{12,8},{16,20},{20,16},{24,28},{28,24},{32,36},... | collective-permute-start | bytes 1572872 | tf_op jit(solution)/shard_map/ppermute | solution.py:488
  46.2 16.4 %collective-permute-start.18 = (bf16[256,1024]{1,0:T(8,128)(2,1)}, bf16[256,1024]{1,0:T(8,128)(2,1)}, u32[]{:S(2)}, u32[]{:S(2)}) collective-permute-start(bf16[256,1024]{1,0:T(8,128)(2,1)} %local_other.1.refs_4_), channel_id=1, source_target_pairs={{0,1},{1,2},{2,3},{3,0},{4,5},{5,6},{6,7},{7,4},{8,9},{9,10},{10,1... | collective-permute-start | bytes 1572872 | tf_op jit(solution)/shard_map/ppermute | solution.py:494
  52.5 36.4 %collective-permute-start.14 = (bf16[256,1792]{1,0:T(8,128)(2,1)}, bf16[256,1792]{1,0:T(8,128)(2,1)S(1)}, u32[]{:S(2)}, u32[]{:S(2)}) collective-permute-start(bf16[256,1792]{1,0:T(8,128)(2,1)} %local_first.1.first_at.refs_0_), channel_id=1, source_target_pairs={{0,3},{1,0},{2,1},{3,2},{4,7},{5,4},{6,5},{7,6},{8,11},{9,8},{10,9... | collective-permute-start | bytes 2752520 | tf_op jit(solution)/shard_map/ppermute | solution.py:494
  54.2 33.1 %collective-permute-start.17 = (bf16[256,1024]{1,0:T(8,128)(2,1)}, bf16[256,1024]{1,0:T(8,128)(2,1)}, u32[]{:S(2)}, u32[]{:S(2)}) collective-permute-start(bf16[256,1024]{1,0:T(8,128)(2,1)} %local_other.1.refs_4_), channel_id=1, source_target_pairs={{0,3},{1,0},{2,1},{3,2},{4,7},{5,4},{6,5},{7,6},{8,11},{9,8},{10,9... | collective-permute-start | bytes 1572872 | tf_op jit(solution)/shard_map/ppermute | solution.py:494
  56.0 34.6 %collective-permute-start.16 = (bf16[256,1792]{1,0:T(8,128)(2,1)}, bf16[256,1792]{1,0:T(8,128)(2,1)}, u32[]{:S(2)}, u32[]{:S(2)}) collective-permute-start(bf16[256,1792]{1,0:T(8,128)(2,1)} %local_first.1.first_at.refs_0_), channel_id=1, source_target_pairs={{0,1},{1,2},{2,3},{3,0},{4,5},{5,6},{6,7},{7,4},{8,9},{9,10},{10,1... | collective-permute-start | bytes 2752520 | tf_op jit(solution)/shard_map/ppermute | solution.py:494
  56.3 94.9 %copy-start.1 = (bf16[128,2560]{1,0:T(8,128)(2,1)}, bf16[128,2560]{1,0:T(8,128)(2,1)S(1)}, u32[]{:S(2)}) copy-start(bf16[128,2560]{1,0:T(8,128)(2,1)S(1)} %get-tuple-element.36.refs_8_) | copy-start | bytes 1966084
  60.1 97.9 %copy-start = (bf16[256,1536]{1,0:T(8,128)(2,1)}, bf16[256,1536]{1,0:T(8,128)(2,1)S(1)}, u32[]{:S(2)}) copy-start(bf16[256,1536]{1,0:T(8,128)(2,1)S(1)} %late.1.refs_0_) | copy-start | bytes 2359300
  60.1 39.0 %collective-permute-start.12 = (bf16[256,1536]{1,0:T(8,128)(2,1)S(1)}, bf16[256,1536]{1,0:T(8,128)(2,1)}, u32[]{:S(2)}, u32[]{:S(2)}) collective-permute-start(bf16[256,1536]{1,0:T(8,128)(2,1)S(1)} %late.1.refs_0_), channel_id=1, source_target_pairs={{0,1},{1,2},{2,3},{3,0},{4,5},{5,6},{6,7},{7,4},{8,9},{9,10},{10,1... | collective-permute-start | bytes 2359304 | tf_op jit(solution)/shard_map/ppermute | solution.py:494
  62.6 48.0 %collective-permute-start.20 = (bf16[128,2560]{1,0:T(8,128)(2,1)S(1)}, bf16[128,2560]{1,0:T(8,128)(2,1)}, u32[]{:S(2)}, u32[]{:S(2)}) collective-permute-start(bf16[128,2560]{1,0:T(8,128)(2,1)S(1)} %get-tuple-element.36.refs_8_), channel_id=1, source_target_pairs={{0,3},{1,0},{2,1},{3,2},{4,7},{5,4},{6,5},{7,6},{8,11},{9,8},{10,9... | collective-permute-start | bytes 1966088 | tf_op jit(solution)/shard_map/ppermute | solution.py:494
  87.3 22.9 %collective-permute-start.19 = (bf16[256,1024]{1,0:T(8,128)(2,1)}, bf16[256,1024]{1,0:T(8,128)(2,1)S(1)}, u32[]{:S(2)}, u32[]{:S(2)}) collective-permute-start(bf16[256,1024]{1,0:T(8,128)(2,1)} %collective-permute-done.18.refs_7_), channel_id=1, source_target_pairs={{0,1},{1,2},{2,3},{3,0},{4,5},{5,6},{6,7},{7,4},{8,9},{9,10},{10,1... | collective-permute-start | bytes 1572872 | tf_op jit(solution)/shard_map/ppermute | solution.py:494
  88.9 62.3 %copy-start.4 = (bf16[256,1792]{1,0:T(8,128)(2,1)}, bf16[256,1792]{1,0:T(8,128)(2,1)S(1)}, u32[]{:S(2)}) copy-start(bf16[256,1792]{1,0:T(8,128)(2,1)S(1)} %collective-permute-done.14.refs_1_) | copy-start | bytes 2752516
  88.9 32.0 %collective-permute-start.15 = (bf16[256,1792]{1,0:T(8,128)(2,1)S(1)}, bf16[256,1792]{1,0:T(8,128)(2,1)S(1)}, u32[]{:S(2)}, u32[]{:S(2)}) collective-permute-start(bf16[256,1792]{1,0:T(8,128)(2,1)S(1)} %collective-permute-done.14.refs_1_), channel_id=1, source_target_pairs={{0,3},{1,0},{2,1},{3,2},{4,7},{5,4},{6,5},{7,6},{8,11},{9,8},{10,9... | collective-permute-start | bytes 2752520 | tf_op jit(solution)/shard_map/ppermute | solution.py:494
  90.6 67.4 %collective-permute-start.11 = (bf16[256,1536]{1,0:T(8,128)(2,1)S(1)}, bf16[256,1536]{1,0:T(8,128)(2,1)}, u32[]{:S(2)}, u32[]{:S(2)}) collective-permute-start(bf16[256,1536]{1,0:T(8,128)(2,1)S(1)} %late.1.refs_0_), channel_id=1, source_target_pairs={{0,3},{1,0},{2,1},{3,2},{4,7},{5,4},{6,5},{7,6},{8,11},{9,8},{10,9... | collective-permute-start | bytes 2359304 | tf_op jit(solution)/shard_map/ppermute | solution.py:494
  99.2 58.9 %collective-permute-start.13 = (bf16[256,1536]{1,0:T(8,128)(2,1)}, bf16[256,1536]{1,0:T(8,128)(2,1)}, u32[]{:S(2)}, u32[]{:S(2)}) collective-permute-start(bf16[256,1536]{1,0:T(8,128)(2,1)} %collective-permute-done.12.refs_3_), channel_id=1, source_target_pairs={{0,1},{1,2},{2,3},{3,0},{4,5},{5,6},{6,7},{7,4},{8,9},{9,10},{10,1... | collective-permute-start | bytes 2359304 | tf_op jit(solution)/shard_map/ppermute | solution.py:494
  110.3 0.8 copy-start.6
  110.3 30.6 %collective-permute-start.22 = (bf16[128,2560]{1,0:T(8,128)(2,1)S(1)}, bf16[128,2560]{1,0:T(8,128)(2,1)}, u32[]{:S(2)}, u32[]{:S(2)}) collective-permute-start(bf16[128,2560]{1,0:T(8,128)(2,1)S(1)} %get-tuple-element.36.refs_8_), channel_id=1, source_target_pairs={{0,1},{1,2},{2,3},{3,0},{4,5},{5,6},{6,7},{7,4},{8,9},{9,10},{10,1... | collective-permute-start | bytes 1966088 | tf_op jit(solution)/shard_map/ppermute | solution.py:494
  111.1 40.1 %collective-permute-start.21 = (bf16[128,2560]{1,0:T(8,128)(2,1)}, bf16[128,2560]{1,0:T(8,128)(2,1)}, u32[]{:S(2)}, u32[]{:S(2)}) collective-permute-start(bf16[128,2560]{1,0:T(8,128)(2,1)} %collective-permute-done.20.refs_9_), channel_id=1, source_target_pairs={{0,3},{1,0},{2,1},{3,2},{4,7},{5,4},{6,5},{7,6},{8,11},{9,8},{10,9... | collective-permute-start | bytes 1966088 | tf_op jit(solution)/shard_map/ppermute | solution.py:494
  120.9 30.3 %copy-start.5 = (bf16[256,1792]{1,0:T(8,128)(2,1)}, bf16[256,1792]{1,0:T(8,128)(2,1)S(1)}, u32[]{:S(2)}) copy-start(bf16[256,1792]{1,0:T(8,128)(2,1)S(1)} %collective-permute-done.15.refs_2_) | copy-start | bytes 2752516

commit v2 on v1

--- a/solution.py
+++ b/solution.py
@@ -13,7 +13,8 @@
 GH = 8
 HDIM = 64
 WIDE = 1024
-EARLY = (24, 16)
+EARLY = (16, 16)
+LATE = (8, 24)
 TAIL = 16
 LOG2E = 1.4426950408889634
 F32 = jnp.float32
@@ -38,6 +39,11 @@
 
 def level_at():
     return lax.div(lax.axis_index("seq"), CORES * ROW)
+
+
+def half_of(heads, own):
+    core = core_at() if own else CORES - 1 - core_at()
+    return pl.multiple_of(core * (heads // CORES), heads // CORES)
 
 
 def thirds(x):
@@ -221,11 +227,9 @@
     copies = [pltpu.make_async_copy(x, y, sems.at[i]) for i, (x, y) in enumerate(small)]
 
     def lanes(i):
-        at = i * width
-        if not isinstance(i, int):
-            at = pl.multiple_of(at, width)
+        at = pl.multiple_of(first_lane + i * width, width)
         return pltpu.make_async_copy(
-            values_at.at[:, pl.ds(first_lane + at, width)], values.at[:, pl.ds(at, width)], sems.at[n + i]
+            values_at.at[:, pl.ds(at, width)], values.at[:, i * width : (i + 1) * width], sems.at[n + i]
         )
 
     for copy in copies:
@@ -256,109 +260,85 @@
         local_part(skip, start + i * GH, vals, sums[:, heads], line[heads], scores, put)
 
 
-def first_local_kernel(skip, values_at, decay_at, b_at, c_at, out, values, log_decay, b_in, c_in, lower, scores, sems):
-    tokens = values.shape[0]
-    heads = log_decay.shape[0]
-    ends = out.shape[1] - 2 * Q
+def with_lanes(x):
+    return jnp.concatenate([x, jnp.zeros((x.shape[0], Q - x.shape[1]), F32)], axis=1).astype(BF)
+
+
+def prepared(start, own, count, values_at, decay_at, b_at, c_at, values, log_decay, b_in, c_in, lower, scores, sems):
+    first = half_of(log_decay.shape[0], own) + start
     small = ((decay_at, log_decay), (b_at, b_in), (c_at, c_in))
-    wait = bring(small, values_at, 0, values, GH * HDIM, sems)
-    lower[...] = triangle(tokens)
-    wait()
-    scores[...] = dot(c_in[...], b_in[...], 1, 1)
-    sums, line = token_sums(lower[...], log_decay[...])
-    out[:, ends : ends + Q] = c_in[...]
-    decay = jnp.concatenate([jnp.exp2(sums), jnp.zeros((tokens, Q - heads), F32)], axis=1)
-    out[:, ends + Q :] = decay.astype(BF)
-
-    def emit(i, at, x):
-        out[i * Q : (i + 1) * Q, at : at + x.shape[1]] = x.astype(BF)
-
-    local_groups(0, skip, values, sums, line, scores, emit, wait)
-
-
-def other_local_kernel(start, skip, values_at, decay_at, b_at, c_at, out, values, log_decay, b_in, c_in, lower, scores, sems):
-    small = ((decay_at, log_decay), (b_at, b_in), (c_at, c_in))
-    wait = bring(small, values_at, start * HDIM, values, GH * HDIM, sems)
+    wait = bring(small, values_at, first * HDIM, values, GH * HDIM, sems)
     lower[...] = triangle(values.shape[0])
     wait()
     scores[...] = dot(c_in[...], b_in[...], 1, 1)
-    count = values.shape[1] // HDIM
-    sums, line = token_sums(lower[...], log_decay[start : start + count, :])
+    sums, line = token_sums(lower[...], log_decay[pl.ds(pl.multiple_of(first, GH), count), :])
+    return first, sums, line, wait
+
+
+def first_local_kernel(skip, values_at, decay_at, b_at, c_at, out, values, log_decay, b_in, c_in, lower, scores, sems):
+    ends = out.shape[1] - 2 * Q
+    arrays = (values_at, decay_at, b_at, c_at, values, log_decay, b_in, c_in, lower, scores, sems)
+    first, sums, line, wait = prepared(0, True, log_decay.shape[0] // CORES, *arrays)
+    out[:, ends : ends + Q] = c_in[...]
+    out[:, ends + Q :] = with_lanes(jnp.exp2(sums))
 
     def emit(i, at, x):
         out[i * Q : (i + 1) * Q, at : at + x.shape[1]] = x.astype(BF)
 
-    local_groups(start, skip, values, sums, line, scores, emit, wait)
-
-
-def late_kernel(
-    start, skip, enter, first_at, values_at, decay_at, b_at, c_at, out,
-    decays, values, log_decay, b_in, c_in, lower, scores, sems,
-):
-    small = (
-        (decay_at, log_decay),
-        (b_at, b_in),
-        (c_at, c_in),
-        (first_at.at[:, pl.ds(first_at.shape[1] - Q, Q)], decays),
-    )
-    wait = bring(small, values_at, start * HDIM, values, GH * HDIM, sems)
-    lower[...] = triangle(values.shape[0])
-    wait()
-    scores[...] = dot(c_in[...], b_in[...], 1, 1)
+    local_groups(first, skip, values, sums, line, scores, emit, wait)
+
+
+def other_local_kernel(start, skip, values_at, decay_at, b_at, c_at, out, *scratch):
+    values, scores = scratch[0], scratch[-2]
     count = values.shape[1] // HDIM
-    sums, line = token_sums(lower[...], log_decay[start : start + count, :])
+    first, sums, line, wait = prepared(start, True, count, values_at, decay_at, b_at, c_at, *scratch)
+
+    def emit(i, at, x):
+        out[i * Q : (i + 1) * Q, at : at + x.shape[1]] = x.astype(BF)
+
+    local_groups(first, skip, values, sums, line, scores, emit, wait)
+
+
+def late_kernel(start, skip, enter, values_at, decay_at, b_at, c_at, out, *scratch):
+    values, c_in, scores = scratch[0], scratch[3], scratch[-2]
+    count = values.shape[1] // HDIM
+    first, sums, line, wait = prepared(start, False, count, values_at, decay_at, b_at, c_at, *scratch)
+    decays = with_lanes(jnp.exp2(sums))
     row = iota((Q, Q), 0)
     side = lax.shift_right_logical(iota((Q, Q), 1), HDIM.bit_length() - 1)
 
     def emit(i, at, x):
-        pick = jnp.where(row == side + (start + at // HDIM), 1.0, 0.0).astype(BF)
+        pick = jnp.where(row == side + at // HDIM, 1.0, 0.0).astype(BF)
         rows = slice(i * Q, (i + 1) * Q)
-        add = dot(decays[rows, :], pick) * dot(c_in[rows, :], enter[:, at : at + Q])
+        lane = start * HDIM + at
+        add = dot(decays[rows], pick) * dot(c_in[rows, :], enter[:, lane : lane + Q])
         out[rows, at : at + Q] = (x + add).astype(BF)
 
-    local_groups(start, skip, values, sums, line, scores, emit, wait)
-
-
-def put_half(half, lanes, value, early, late):
-    at = half * (early.shape[1] + late.shape[1]) // CORES + lanes.start
-    size = lanes.stop - lanes.start
-    if at + size <= early.shape[1]:
-        early[:, at : at + size] = value
-    else:
-        late[:, at - early.shape[1] : at - early.shape[1] + size] = value
+    local_groups(first, skip, values, sums, line, scores, emit, wait)
 
 
 def split_kernel(earlier, *refs):
-    enters, early, late, give, held = refs[:ROW], refs[ROW], refs[ROW + 1], refs[ROW + 2], refs[ROW + 3]
+    enters, keep, give, held = refs[:ROW], refs[ROW], refs[ROW + 1], refs[ROW + 2]
     n, pw = enters[0].shape
     core = core_at()
     for k in range(ROW):
         held[lax.rem(row_at() - k + ROW, ROW)] = enters[k][...]
 
-    def emit(half):
+    def emit(before, after):
         for g in range(ROW):
             at = slice(g * pw, (g + 1) * pw)
             enter = held[g]
             decay = jnp.exp2(tail_total(earlier, n, at))
-            after = (decay * enter.astype(F32) + earlier[0:n, at].astype(F32)).astype(BF)
-            put_half(half, at, enter if half == 0 else after, early, late)
-            give[:, at] = after if half == 0 else enter
-
-    for half in range(CORES):
-
-        @pl.when(core == half)
-        def _():
-            emit(half)
-
-
-def sorted_kernel(got, early_in, late_in, early, late):
-    for half in range(CORES):
-
-        @pl.when(core_at() != half)
-        def _():
-            for at in range(0, got.shape[1], GH * HDIM):
-                lanes = slice(at, at + GH * HDIM)
-                put_half(half, lanes, got[:, lanes], early, late)
+            before[:, at] = enter
+            after[:, at] = (decay * enter.astype(F32) + earlier[0:n, at].astype(F32)).astype(BF)
+
+    @pl.when(core == 0)
+    def _():
+        emit(keep, give)
+
+    @pl.when(core != 0)
+    def _():
+        emit(give, keep)
 
 
 def owned_plan(owner, docs):
@@ -400,7 +380,7 @@
     out, first, other, enter, done, zeros, s_first, s_other, s_enter, s_out, s_zero = refs[12:]
     plans = owned_plan(owner, 4)
     groups = ((firsts, first, s_first), (others, other, s_other), (enters, enter, s_enter))
-    lanes = pl.ds(0, done.shape[2])
+    lanes = pl.ds(pl.multiple_of(core_at() * done.shape[2], done.shape[2]), done.shape[2])
 
     def some(plan):
         return jnp.logical_or(plan[1], plan[2])
@@ -439,13 +419,21 @@
         write_owned(plan, r, None, out, pl.ds(0, zeros.shape[1]), s_zero, zeros, "wait")
 
 
-def owned_kernel(first_lane, owner, *refs):
-    sources = refs[:4]
+def owned_kernel(start, which, owner, *refs):
     out, held, s_in, s_out = refs[-4:]
     plans = owned_plan(owner, 4)
-    lanes = pl.ds(first_lane, held.shape[2])
+    width = refs[0].shape[1]
+    half = out.shape[2] // CORES
+    lane = (CORES - 1 - core_at()) * half + start * HDIM
+    lanes = pl.ds(pl.multiple_of(lane, GH * HDIM), width)
+    if isinstance(which, int):
+        for act in ("start", "wait"):
+            write_owned(plans[which], which, refs[0], out, lanes, s_out, None, act)
+        return
+    sources = dict(zip(which, refs))
     for act in ("start", "wait"):
-        for r, plan in enumerate(plans):
+        for r in which:
+            plan = plans[r]
 
             @pl.when(jnp.logical_or(plan[1], plan[2]))
             def _():
@@ -453,8 +441,8 @@
 
             if act == "wait":
                 write_owned(plan, r, held.at[r], out, lanes, s_out)
-    for r, plan in enumerate(plans):
-        write_owned(plan, r, held.at[r], out, lanes, s_out, None, "wait")
+    for r in which:
+        write_owned(plans[r], r, held.at[r], out, lanes, s_out, None, "wait")
 
 
 def inside(shape):
@@ -502,8 +490,6 @@
     smem = pl.BlockSpec(memory_space=pltpu.SMEM)
     vmem = pl.BlockSpec(memory_space=pltpu.VMEM)
     anywhere = pl.BlockSpec(memory_space=pl.ANY)
-    early = sum(EARLY)
-    early_width = early * HDIM
 
     first_width = EARLY[0] * HDIM
     dma = pltpu.SemaphoreType.DMA
@@ -587,36 +573,29 @@
         ],
     )(*near(pieces + rows))
     enters = along_row(enters)
-    enter_shapes = [pltpu.VMEM((n, early_width), BF), pltpu.VMEM((n, width - early_width), BF)]
-    enter_early, enter_late, give = pl.pallas_call(
+    keep, give = pl.pallas_call(
         split_kernel,
         name="split",
-        out_shape=enter_shapes + [pltpu.VMEM((n, half), BF)],
+        out_shape=[pltpu.VMEM((n, half), BF)] * 2,
         in_specs=[vmem] * (ROW + 1),
-        out_specs=[vmem] * 3,
+        out_specs=[vmem] * 2,
         scratch_shapes=[pltpu.VMEM((ROW, n, pw), BF)],
     )(*near([earlier] + enters))
     got = shifted(give, swap=1)
-    enter_early, enter_late = pl.pallas_call(
-        sorted_kernel,
-        name="sorted",
-        out_shape=enter_shapes,
-        in_specs=[vmem] * 3,
-        out_specs=[vmem] * 2,
-        input_output_aliases={1: 0, 2: 1},
-    )(*near([got, enter_early, enter_late]))
-    early_enters = over_all_docs(enter_early, -1)
-
-    late_width = width - early_width
-    late = pl.pallas_call(
-        functools.partial(late_kernel, early),
-        name="late",
-        out_shape=pltpu.VMEM((tokens, late_width), BF),
-        in_specs=[smem, vmem] + [anywhere] * 5,
-        out_specs=vmem,
-        scratch_shapes=[pltpu.VMEM((tokens, Q), BF)] + local_scratch(heads - early, 4),
-    )(skip, *near([enter_late]), first, values, log_decay, b_in, c_in)
-    lates = over_all_docs(late, 1)
+    early_enters = over_all_docs(keep, -1)
+
+    lates = []
+    start = 0
+    for i, count in enumerate(LATE):
+        late = pl.pallas_call(
+            functools.partial(late_kernel, start),
+            out_shape=pltpu.VMEM((tokens, count * HDIM), BF),
+            in_specs=[smem, vmem] + [anywhere] * 4,
+            out_specs=vmem,
+            scratch_shapes=local_scratch(count),
+        )(skip, *near([got]), values, log_decay, b_in, c_in)
+        lates.append((start, over_all_docs(late, -1 if i == 0 else 1)))
+        start += count
 
     result = jax.ShapeDtypeStruct((doc_n * 2, Q, width), BF)
     owned = pl.pallas_call(
@@ -628,8 +607,8 @@
         scratch_shapes=[
             pltpu.VMEM((doc_n,) + first.shape, BF),
             pltpu.VMEM((doc_n,) + other.shape, BF),
-            pltpu.VMEM((doc_n,) + enter_early.shape, BF),
-            pltpu.VMEM((doc_n, tokens, early_width), BF),
+            pltpu.VMEM((doc_n,) + keep.shape, BF),
+            pltpu.VMEM((doc_n, tokens, half), BF),
             pltpu.VMEM((Q, width), BF),
             dma((doc_n,)),
             dma((doc_n,)),
@@ -638,15 +617,31 @@
             dma((doc_n * 2,)),
         ],
     )(owner, *far(firsts), *far(others), *far(early_enters))
-    owned = pl.pallas_call(
-        functools.partial(owned_kernel, early_width),
-        name="owned",
-        out_shape=result,
-        in_specs=[smem] + [anywhere] * 5,
-        out_specs=anywhere,
-        scratch_shapes=[pltpu.VMEM((doc_n,) + late.shape, BF), dma((doc_n,)), dma((doc_n * 2,))],
-        input_output_aliases={5: 0},
-    )(owner, *far(lates), owned)
+
+    def write_late(owned, i, which):
+        start, arrays = lates[i]
+        if isinstance(which, int):
+            arrays = near([arrays[which]])
+        else:
+            arrays = far([arrays[r] for r in which])
+        return pl.pallas_call(
+            functools.partial(owned_kernel, start, which),
+            out_shape=result,
+            in_specs=[smem] + [vmem if len(arrays) == 1 else anywhere] * len(arrays) + [anywhere],
+            out_specs=anywhere,
+            scratch_shapes=[
+                pltpu.VMEM((doc_n,) + arrays[0].shape, BF),
+                dma((doc_n,)),
+                dma((doc_n * 2,)),
+            ],
+            input_output_aliases={1 + len(arrays): 0},
+        )(owner, *arrays, owned)
+
+    near_docs, far_doc = (0, 1, 3), 2
+    for i in range(len(LATE)):
+        owned = write_late(owned, i, near_docs)
+    for i in range(len(LATE)):
+        owned = write_late(owned, i, far_doc)
     return owned[None]
 
 

time: 162 us -> 156 us (0.963)
  the two profiles are of different devices: /device:TPU:2 before, /device:TPU:6 now
where the time goes in v2:
time: 156 us; the launch traced here: 155 us
  waiting for transfers between devices  88.5 us (57%)
  Pallas kernels  33.4 us (21%)
  starting transfers between devices  32.2 us (21%)
    ppermute x15, waiting for transfers between devices, over_docs(): return lax.ppermute(x, 'doc', [(d, (d + k) % doc_n) for d in range(doc_n)])  67.4 us
    ppermute x11, waiting for transfers between devices, shifted(): return lax.ppermute(x, 'seq', pairs)  21.2 us
    ppermute x15, starting transfers between devices, over_docs(): return lax.ppermute(x, 'doc', [(d, (d + k) % doc_n) for d in range(doc_n)])  19.3 us
    ppermute x11, starting transfers between devices, shifted(): return lax.ppermute(x, 'seq', pairs)  12.9 us
    pallas_call x4, Pallas kernels, write_late(): pl.pallas_call(functools.partial(owned_kernel, start, which), out_shape=r...  8.5 us
    pallas_call x2, Pallas kernels, whole(): pl.pallas_call(functools.partial(late_kernel, start), out_shape=pltpu.VME...  6.35 us
    pallas_call x1, Pallas kernels, whole(): pl.pallas_call(finish_kernel, name='finish', out_shape=result, in_specs=[...  6.1 us
    pallas_call x1, Pallas kernels, whole(): pl.pallas_call(first_local_kernel, name='local_first', out_shape=jax.Shap...  3.91 us
  transfers between devices with their start and end apart: 26, of which 16 were waited for; matrix products, arithmetic and copies ran while one was open for 0% of the time, Pallas kernels for 17%

profile of v2, /device:TPU:6, one launch (start us, length us, event | category | flops | bytes accessed | tf_op | source)
XLA Modules:
  0.0 155.2 jit_solution(14387914424575530497)
XLA Ops:
  0.0 3.5 %states.1 = (bf16[144,2048]{1,0:T(8,128)(2,1)S(1)}, bf16[144,2048]{1,0:T(8,128)(2,1)S(1)}) custom-call(bf16[256,4096]{1,0:T(8,128)(2,1)} %bitcast.5, f32[64,256]{1,0:T(8,128)} %bitcast.10, bf16[256,128]{1,0:T(8,128)(2,1)} %bitcast.15), custom_call_target="tpu_custom_call" | custom-call | tf_op jit(solution)/shard_map/states/pallas_call | solution.py:522
  3.5 0.0 copy-start.7
  3.5 0.1 collective-permute-start
  3.6 2.0 %collective-permute-done.theirs = bf16[144,2048]{1,0:T(8,128)(2,1)S(1)} collective-permute-done((bf16[144,2048]{1,0:T(8,128)(2,1)S(1)}, bf16[144,2048]{1,0:T(8,128)(2,1)S(1)}, u32[]{:S(2)}, u32[]{:S(2)}) %collective-permute-start) | collective-permute-done | bytes 589856 | tf_op jit(solution)/shard_map/ppermute | solution.py:476
  5.6 0.4 chip.1
  6.1 0.4 collective-permute-start.1
  6.5 2.5 %collective-permute-start.2 = (bf16[144,512]{1,0:T(8,128)(2,1)S(1)}, bf16[144,512]{1,0:T(8,128)(2,1)S(1)}, u32[]{:S(2)}, u32[]{:S(2)}) collective-permute-start(bf16[144,512]{1,0:T(8,128)(2,1)S(1)} %get-tuple-element.23), channel_id=1, source_target_pairs={{0,16},{4,20},{8,24},{12,28},{16,0},{20,4},{24,8},{28,12},{32,48},... | collective-permute-start | bytes 442376 | tf_op jit(solution)/shard_map/ppermute | solution.py:476
  9.0 0.0 collective-permute-start.3
  9.0 3.8 %collective-permute-done.1.refs_1_ = bf16[144,512]{1,0:T(8,128)(2,1)S(1)} collective-permute-done((bf16[144,512]{1,0:T(8,128)(2,1)S(1)}, bf16[144,512]{1,0:T(8,128)(2,1)S(1)}, u32[]{:S(2)}, u32[]{:S(2)}) %collective-permute-start.1) | collective-permute-done | bytes 147488 | tf_op jit(solution)/shard_map/ppermute | solution.py:476
  12.8 1.9 %collective-permute-done.2.refs_2_ = bf16[144,512]{1,0:T(8,128)(2,1)S(1)} collective-permute-done((bf16[144,512]{1,0:T(8,128)(2,1)S(1)}, bf16[144,512]{1,0:T(8,128)(2,1)S(1)}, u32[]{:S(2)}, u32[]{:S(2)}) %collective-permute-start.2) | collective-permute-done | bytes 147488 | tf_op jit(solution)/shard_map/ppermute | solution.py:476
  14.7 2.0 %collective-permute-done.3.refs_3_ = bf16[144,512]{1,0:T(8,128)(2,1)S(1)} collective-permute-done((bf16[144,512]{1,0:T(8,128)(2,1)S(1)}, bf16[144,512]{1,0:T(8,128)(2,1)S(1)}, u32[]{:S(2)}, u32[]{:S(2)}) %collective-permute-start.3) | collective-permute-done | bytes 147488 | tf_op jit(solution)/shard_map/ppermute | solution.py:476
  16.8 0.1 row.1
  16.9 2.1 %collective-permute-start.4 = (bf16[144,512]{1,0:T(8,128)(2,1)S(1)}, bf16[144,512]{1,0:T(8,128)(2,1)S(1)}, u32[]{:S(2)}, u32[]{:S(2)}) collective-permute-start(bf16[144,512]{1,0:T(8,128)(2,1)S(1)} %row.1), channel_id=1, source_target_pairs={{0,32},{4,36},{8,40},{12,44},{16,48},{20,52},{24,56},{28,60},{32,6... | collective-permute-start | bytes 442376 | tf_op jit(solution)/shard_map/ppermute | solution.py:476
  19.0 3.6 %collective-permute-start.5 = (bf16[144,512]{1,0:T(8,128)(2,1)S(1)}, bf16[144,512]{1,0:T(8,128)(2,1)S(1)}, u32[]{:S(2)}, u32[]{:S(2)}) collective-permute-start(bf16[144,512]{1,0:T(8,128)(2,1)S(1)} %row.1), channel_id=1, source_target_pairs={{0,64},{4,68},{8,72},{12,76},{16,80},{20,84},{24,88},{28,92},{32,9... | collective-permute-start | bytes 442376 | tf_op jit(solution)/shard_map/ppermute | solution.py:476
  22.6 1.0 collective-permute-start.6
  23.6 1.3 collective-permute-done.4.refs_4_
  24.9 4.1 %collective-permute-done.5.refs_5_ = bf16[144,512]{1,0:T(8,128)(2,1)S(1)} collective-permute-done((bf16[144,512]{1,0:T(8,128)(2,1)S(1)}, bf16[144,512]{1,0:T(8,128)(2,1)S(1)}, u32[]{:S(2)}, u32[]{:S(2)}) %collective-permute-start.5) | collective-permute-done | bytes 147488 | tf_op jit(solution)/shard_map/ppermute | solution.py:476
  29.0 0.0 collective-permute-done.6.refs_6_
  29.0 0.3 enter.1
  29.3 0.8 collective-permute-start.7
  30.1 1.8 %collective-permute-start.8 = (bf16[128,512]{1,0:T(8,128)(2,1)S(1)}, bf16[128,512]{1,0:T(8,128)(2,1)S(1)}, u32[]{:S(2)}, u32[]{:S(2)}) collective-permute-start(bf16[128,512]{1,0:T(8,128)(2,1)S(1)} %get-tuple-element.27), channel_id=1, source_target_pairs={{0,16},{4,20},{8,24},{12,28},{16,0},{20,4},{24,8},{28,12},{32,48},... | collective-permute-start | bytes 393224 | tf_op jit(solution)/shard_map/ppermute | solution.py:476
  32.0 0.4 collective-permute-start.9
  32.4 2.5 %collective-permute-done.7.refs_1_ = bf16[128,512]{1,0:T(8,128)(2,1)S(1)} collective-permute-done((bf16[128,512]{1,0:T(8,128)(2,1)S(1)}, bf16[128,512]{1,0:T(8,128)(2,1)S(1)}, u32[]{:S(2)}, u32[]{:S(2)}) %collective-permute-start.7) | collective-permute-done | bytes 131104 | tf_op jit(solution)/shard_map/ppermute | solution.py:476
  34.9 2.2 %collective-permute-done.8.refs_2_ = bf16[128,512]{1,0:T(8,128)(2,1)S(1)} collective-permute-done((bf16[128,512]{1,0:T(8,128)(2,1)S(1)}, bf16[128,512]{1,0:T(8,128)(2,1)S(1)}, u32[]{:S(2)}, u32[]{:S(2)}) %collective-permute-start.8) | collective-permute-done | bytes 131104 | tf_op jit(solution)/shard_map/ppermute | solution.py:476
  37.1 1.4 collective-permute-done.9.refs_3_
  38.4 0.3 split.1
  38.7 0.1 collective-permute-start.10
  38.8 3.9 %local_other.1.refs_4_ = bf16[256,1024]{1,0:T(8,128)(2,1)} custom-call(f32[64]{0:T(128)} %skip.7, bf16[256,4096]{1,0:T(8,128)(2,1)} %bitcast.6, f32[64,256]{1,0:T(8,128)} %bitcast.11, bf16[256,128]{1,0:T(8,128)(2,1)} %bitcast.16, bf16[256,128]{1,0:T(8,128)(2,1)} %bitcast.20), custom_call_target="tpu_custom_call" | custom-call | tf_op jit(solution)/shard_map/local_other/pallas_call | solution.py:548
  42.7 1.6 %collective-permute-start.21 = (bf16[256,1024]{1,0:T(8,128)(2,1)}, bf16[256,1024]{1,0:T(8,128)(2,1)}, u32[]{:S(2)}, u32[]{:S(2)}) collective-permute-start(bf16[256,1024]{1,0:T(8,128)(2,1)} %local_other.1.refs_4_), channel_id=1, source_target_pairs={{0,1},{1,2},{2,3},{3,0},{4,5},{5,6},{6,7},{7,4},{8,9},{9,10},{10,1... | collective-permute-start | bytes 1572872 | tf_op jit(solution)/shard_map/ppermute | solution.py:482
  44.3 3.9 %local_first.1.refs_0_ = bf16[256,1280]{1,0:T(8,128)(2,1)} custom-call(f32[64]{0:T(128)} %skip.7, bf16[256,4096]{1,0:T(8,128)(2,1)} %bitcast.7, f32[64,256]{1,0:T(8,128)} %bitcast.12, bf16[256,128]{1,0:T(8,128)(2,1)} %bitcast.17, bf16[256,128]{1,0:T(8,128)(2,1)} %bitcast.21), custom_call_target="tpu_custom_call" | custom-call | tf_op jit(solution)/shard_map/local_first/pallas_call | solution.py:508
  48.2 1.7 %collective-permute-start.17 = (bf16[256,1280]{1,0:T(8,128)(2,1)}, bf16[256,1280]{1,0:T(8,128)(2,1)S(1)}, u32[]{:S(2)}, u32[]{:S(2)}) collective-permute-start(bf16[256,1280]{1,0:T(8,128)(2,1)} %local_first.1.refs_0_), channel_id=1, source_target_pairs={{0,3},{1,0},{2,1},{3,2},{4,7},{5,4},{6,5},{7,6},{8,11},{9,8},{10,9... | collective-permute-start | bytes 1966088 | tf_op jit(solution)/shard_map/ppermute | solution.py:482
  50.0 1.8 %collective-permute-start.20 = (bf16[256,1024]{1,0:T(8,128)(2,1)}, bf16[256,1024]{1,0:T(8,128)(2,1)}, u32[]{:S(2)}, u32[]{:S(2)}) collective-permute-start(bf16[256,1024]{1,0:T(8,128)(2,1)} %local_other.1.refs_4_), channel_id=1, source_target_pairs={{0,3},{1,0},{2,1},{3,2},{4,7},{5,4},{6,5},{7,6},{8,11},{9,8},{10,9... | collective-permute-start | bytes 1572872 | tf_op jit(solution)/shard_map/ppermute | solution.py:482
  51.8 0.0 collective-permute-done.10.enter
  51.8 3.8 %shard_map.64.refs_0_ = bf16[256,1536]{1,0:T(8,128)(2,1)S(1)} custom-call(f32[64]{0:T(128)} %skip.7, bf16[128,2048]{1,0:T(8,128)(2,1)S(1)} %collective-permute-done.10.enter, bf16[256,4096]{1,0:T(8,128)(2,1)} %bitcast.8, f32[64,256]{1,0:T(8,128)} %bitcast.13, bf16[256,128]{1,0:T(8,128)(2,1)} %bitcast.18, bf16[256,128]{1,0:T(8,128)(2,1)} %bitcast.22), custom_call_target="tpu_custom_call" | custom-call | tf_op jit(solution)/shard_map/pallas_call | solution.py:590
  55.6 0.3 collective-permute-start.11
  55.9 0.4 collective-permute-start.19
  56.3 2.4 %collective-permute-done.21.refs_7_ = bf16[256,1024]{1,0:T(8,128)(2,1)} collective-permute-done((bf16[256,1024]{1,0:T(8,128)(2,1)}, bf16[256,1024]{1,0:T(8,128)(2,1)}, u32[]{:S(2)}, u32[]{:S(2)}) %collective-permute-start.21) | collective-permute-done | bytes 524320 | tf_op jit(solution)/shard_map/ppermute | solution.py:482
  58.7 0.8 collective-permute-start.22
  59.4 6.7 %collective-permute-done.17.refs_1_ = bf16[256,1280]{1,0:T(8,128)(2,1)S(1)} collective-permute-done((bf16[256,1280]{1,0:T(8,128)(2,1)}, bf16[256,1280]{1,0:T(8,128)(2,1)S(1)}, u32[]{:S(2)}, u32[]{:S(2)}) %collective-permute-start.17) | collective-permute-done | bytes 655392 | tf_op jit(solution)/shard_map/ppermute | solution.py:482
  66.1 2.9 %collective-permute-start.18 = (bf16[256,1280]{1,0:T(8,128)(2,1)S(1)}, bf16[256,1280]{1,0:T(8,128)(2,1)}, u32[]{:S(2)}, u32[]{:S(2)}) collective-permute-start(bf16[256,1280]{1,0:T(8,128)(2,1)S(1)} %collective-permute-done.17.refs_1_), channel_id=1, source_target_pairs={{0,3},{1,0},{2,1},{3,2},{4,7},{5,4},{6,5},{7,6},{8,11},{9,8},{10,9... | collective-permute-start | bytes 1966088 | tf_op jit(solution)/shard_map/ppermute | solution.py:482
  69.0 8.5 %collective-permute-done.20.refs_5_ = bf16[256,1024]{1,0:T(8,128)(2,1)} collective-permute-done((bf16[256,1024]{1,0:T(8,128)(2,1)}, bf16[256,1024]{1,0:T(8,128)(2,1)}, u32[]{:S(2)}, u32[]{:S(2)}) %collective-permute-start.20) | collective-permute-done | bytes 524320 | tf_op jit(solution)/shard_map/ppermute | solution.py:482
  77.5 2.9 %collective-permute-start.23 = (bf16[128,2048]{1,0:T(8,128)(2,1)S(1)}, bf16[128,2048]{1,0:T(8,128)(2,1)}, u32[]{:S(2)}, u32[]{:S(2)}) collective-permute-start(bf16[128,2048]{1,0:T(8,128)(2,1)S(1)} %get-tuple-element.30.refs_8_), channel_id=1, source_target_pairs={{0,3},{1,0},{2,1},{3,2},{4,7},{5,4},{6,5},{7,6},{8,11},{9,8},{10,9... | collective-permute-start | bytes 1572872 | tf_op jit(solution)/shard_map/ppermute | solution.py:482
  80.3 11.0 %collective-permute-done.19.refs_3_ = bf16[256,1280]{1,0:T(8,128)(2,1)S(1)} collective-permute-done((bf16[256,1280]{1,0:T(8,128)(2,1)}, bf16[256,1280]{1,0:T(8,128)(2,1)S(1)}, u32[]{:S(2)}, u32[]{:S(2)}) %collective-permute-start.19) | collective-permute-done | bytes 655392 | tf_op jit(solution)/shard_map/ppermute | solution.py:482
  91.4 0.0 collective-permute-start.25
  91.4 11.2 %collective-permute-done.22.refs_6_ = bf16[256,1024]{1,0:T(8,128)(2,1)S(1)} collective-permute-done((bf16[256,1024]{1,0:T(8,128)(2,1)}, bf16[256,1024]{1,0:T(8,128)(2,1)S(1)}, u32[]{:S(2)}, u32[]{:S(2)}) %collective-permute-start.22) | collective-permute-done | bytes 524320 | tf_op jit(solution)/shard_map/ppermute | solution.py:482
  102.6 0.3 collective-permute-start.15
  102.9 0.0 collective-permute-done.11.refs_2_
  102.9 1.7 %collective-permute-start.12 = (bf16[256,1536]{1,0:T(8,128)(2,1)}, bf16[256,1536]{1,0:T(8,128)(2,1)S(1)}, u32[]{:S(2)}, u32[]{:S(2)}) collective-permute-start(bf16[256,1536]{1,0:T(8,128)(2,1)} %collective-permute-done.11.refs_2_), channel_id=1, source_target_pairs={{0,1},{1,2},{2,3},{3,0},{4,5},{5,6},{6,7},{7,4},{8,9},{9,10},{10,1... | collective-permute-start | bytes 2359304 | tf_op jit(solution)/shard_map/ppermute | solution.py:482
  104.6 0.0 collective-permute-done.23.refs_9_
  104.6 1.5 collective-permute-start.24
  106.2 2.5 %shard_map.65.refs_0_ = bf16[256,512]{1,0:T(8,128)(2,1)S(1)} custom-call(f32[64]{0:T(128)} %skip.7, bf16[128,2048]{1,0:T(8,128)(2,1)S(1)} %collective-permute-done.10.enter, bf16[256,4096]{1,0:T(8,128)(2,1)} %bitcast.9, f32[64,256]{1,0:T(8,128)} %bitcast.14, bf16[256,128]{1,0:T(8,128)(2,1)} %bitcast.19, bf16[256,128]{1,0:T(8,128)(2,1)} %bitcast.23), custom_call_target="tpu_custom_call" | custom-call | tf_op jit(solution)/shard_map/pallas_call | solution.py:590
  108.7 0.0 collective-permute-done.18.refs_2_
  108.7 0.1 collective-permute-start.13
  108.8 5.1 %collective-permute-done.25.refs_11_ = bf16[128,2048]{1,0:T(8,128)(2,1)} collective-permute-done((bf16[128,2048]{1,0:T(8,128)(2,1)S(1)}, bf16[128,2048]{1,0:T(8,128)(2,1)}, u32[]{:S(2)}, u32[]{:S(2)}) %collective-permute-start.25) | collective-permute-done | bytes 524320 | tf_op jit(solution)/shard_map/ppermute | solution.py:482
  113.9 0.0 collective-permute-start.16
  113.9 22.4 %collective-permute-done.13.refs_1_ = bf16[256,512]{1,0:T(8,128)(2,1)S(1)} collective-permute-done((bf16[256,512]{1,0:T(8,128)(2,1)S(1)}, bf16[256,512]{1,0:T(8,128)(2,1)S(1)}, u32[]{:S(2)}, u32[]{:S(2)}) %collective-permute-start.13) | collective-permute-done | bytes 262176 | tf_op jit(solution)/shard_map/ppermute | solution.py:482
  136.4 3.3 %collective-permute-start.14 = (bf16[256,512]{1,0:T(8,128)(2,1)S(1)}, bf16[256,512]{1,0:T(8,128)(2,1)S(1)}, u32[]{:S(2)}, u32[]{:S(2)}) collective-permute-start(bf16[256,512]{1,0:T(8,128)(2,1)S(1)} %collective-permute-done.13.refs_1_), channel_id=1, source_target_pairs={{0,3},{1,0},{2,1},{3,2},{4,7},{5,4},{6,5},{7,6},{8,11},{9,8},{10,9... | collective-permute-start | bytes 786440 | tf_op jit(solution)/shard_map/ppermute | solution.py:482
  139.7 0.6 copy.15.owner
  140.3 0.0 collective-permute-done.24.refs_10_
  140.3 6.1 %finish.1.refs_3_ = bf16[8,128,4096]{2,1,0:T(8,128)(2,1)} custom-call(s32[4,2]{1,0:T(4,128)} %copy.15.owner, bf16[256,1280]{1,0:T(8,128)(2,1)} %local_first.1.refs_0_, bf16[256,1280]{1,0:T(8,128)(2,1)} %copy-done.3, bf16[256,1280]{1,0:T(8,128)(2,1)} %collective-permute-done.18.refs_2_, bf16[256,1280]{1,0:T(8,128)(2,1)} %copy-done.4, ...), custom_call_target="tpu_custom_call" | custom-call | tf_op jit(solution)/shard_map/finish/pallas_call | solution.py:601
  146.5 2.5 %shard_map.66.refs_3_ = bf16[8,128,4096]{2,1,0:T(8,128)(2,1)} custom-call(s32[4,2]{1,0:T(4,128)} %copy.15.owner, bf16[256,512]{1,0:T(8,128)(2,1)} %copy-done.1, bf16[256,512]{1,0:T(8,128)(2,1)} %copy-done.6, bf16[256,512]{1,0:T(8,128)(2,1)} %collective-permute-done.16.refs_2_, bf16[8,128,4096]{2,1,0:T(8,128)(2,1)} %finish.1.refs_3_), custom_call_target="tpu_custom_call", output_to_operand_aliasing={{}: (4, {})} | custom-call | tf_op jit(solution)/shard_map/pallas_call | solution.py:627
  148.9 2.8 %shard_map.67.refs_1_ = bf16[8,128,4096]{2,1,0:T(8,128)(2,1)} custom-call(s32[4,2]{1,0:T(4,128)} %copy.15.owner, bf16[256,1536]{1,0:T(8,128)(2,1)} %copy-done, bf16[256,1536]{1,0:T(8,128)(2,1)} %collective-permute-done.15.refs_1_, bf16[256,1536]{1,0:T(8,128)(2,1)} %collective-permute-done.11.refs_2_, ...), custom_call_target="tpu_custom_call", output_to_operand_aliasing={{}: (4, {})} | custom-call | tf_op jit(solution)/shard_map/pallas_call | solution.py:627
  151.8 1.5 shard_map.68.refs_1_
  153.3 1.7 %shard_map.69 = bf16[8,128,4096]{2,1,0:T(8,128)(2,1)} custom-call(s32[4,2]{1,0:T(4,128)} %copy.15.owner, bf16[256,1536]{1,0:T(8,128)(2,1)S(1)} %collective-permute-done.12.refs_0_, bf16[8,128,4096]{2,1,0:T(8,128)(2,1)} %shard_map.68.refs_1_), custom_call_target="tpu_custom_call", output_to_operand_aliasing={{}: (2, {})} | custom-call | tf_op jit(solution)/shard_map/pallas_call | solution.py:627
  (19 shorter events, 0.0 us)
Async XLA Ops:
  3.5 136.2 %copy-start.7 = (s32[4,2]{0,1:T(2,128)S(1)}, s32[4,2]{0,1:T(2,128)}, u32[]{:S(2)}) copy-start(s32[4,2]{0,1:T(2,128)} %param.11) | copy-start | bytes 100
  3.5 2.1 %collective-permute-start = (bf16[144,2048]{1,0:T(8,128)(2,1)S(1)}, bf16[144,2048]{1,0:T(8,128)(2,1)S(1)}, u32[]{:S(2)}, u32[]{:S(2)}) collective-permute-start(bf16[144,2048]{1,0:T(8,128)(2,1)S(1)} %get-tuple-element.19), channel_id=1, source_target_pairs={{0,4},{4,0},{8,12},{12,8},{16,20},{20,16},{24,28},{28,24},{32,36},... | collective-permute-start | bytes 1769480 | tf_op jit(solution)/shard_map/ppermute | solution.py:476
  6.1 6.8 %collective-permute-start.1 = (bf16[144,512]{1,0:T(8,128)(2,1)S(1)}, bf16[144,512]{1,0:T(8,128)(2,1)S(1)}, u32[]{:S(2)}, u32[]{:S(2)}) collective-permute-start(bf16[144,512]{1,0:T(8,128)(2,1)S(1)} %get-tuple-element.22), channel_id=1, source_target_pairs={{0,8},{4,12},{8,16},{12,20},{16,24},{20,28},{24,0},{28,4},{32,40},... | collective-permute-start | bytes 442376 | tf_op jit(solution)/shard_map/ppermute | solution.py:476
  6.5 8.2 %collective-permute-start.2 = (bf16[144,512]{1,0:T(8,128)(2,1)S(1)}, bf16[144,512]{1,0:T(8,128)(2,1)S(1)}, u32[]{:S(2)}, u32[]{:S(2)}) collective-permute-start(bf16[144,512]{1,0:T(8,128)(2,1)S(1)} %get-tuple-element.23), channel_id=1, source_target_pairs={{0,16},{4,20},{8,24},{12,28},{16,0},{20,4},{24,8},{28,12},{32,48},... | collective-permute-start | bytes 442376 | tf_op jit(solution)/shard_map/ppermute | solution.py:476
  9.0 7.7 %collective-permute-start.3 = (bf16[144,512]{1,0:T(8,128)(2,1)S(1)}, bf16[144,512]{1,0:T(8,128)(2,1)S(1)}, u32[]{:S(2)}, u32[]{:S(2)}) collective-permute-start(bf16[144,512]{1,0:T(8,128)(2,1)S(1)} %get-tuple-element.24), channel_id=1, source_target_pairs={{0,24},{4,28},{8,0},{12,4},{16,8},{20,12},{24,16},{28,20},{32,56},... | collective-permute-start | bytes 442376 | tf_op jit(solution)/shard_map/ppermute | solution.py:476
  16.9 8.0 %collective-permute-start.4 = (bf16[144,512]{1,0:T(8,128)(2,1)S(1)}, bf16[144,512]{1,0:T(8,128)(2,1)S(1)}, u32[]{:S(2)}, u32[]{:S(2)}) collective-permute-start(bf16[144,512]{1,0:T(8,128)(2,1)S(1)} %row.1), channel_id=1, source_target_pairs={{0,32},{4,36},{8,40},{12,44},{16,48},{20,52},{24,56},{28,60},{32,6... | collective-permute-start | bytes 442376 | tf_op jit(solution)/shard_map/ppermute | solution.py:476
  19.0 10.0 %collective-permute-start.5 = (bf16[144,512]{1,0:T(8,128)(2,1)S(1)}, bf16[144,512]{1,0:T(8,128)(2,1)S(1)}, u32[]{:S(2)}, u32[]{:S(2)}) collective-permute-start(bf16[144,512]{1,0:T(8,128)(2,1)S(1)} %row.1), channel_id=1, source_target_pairs={{0,64},{4,68},{8,72},{12,76},{16,80},{20,84},{24,88},{28,92},{32,9... | collective-permute-start | bytes 442376 | tf_op jit(solution)/shard_map/ppermute | solution.py:476
  22.6 6.4 %collective-permute-start.6 = (bf16[144,512]{1,0:T(8,128)(2,1)S(1)}, bf16[144,512]{1,0:T(8,128)(2,1)S(1)}, u32[]{:S(2)}, u32[]{:S(2)}) collective-permute-start(bf16[144,512]{1,0:T(8,128)(2,1)S(1)} %row.1), channel_id=1, source_target_pairs={{0,96},{4,100},{8,104},{12,108},{16,112},{20,116},{24,120},{28,124... | collective-permute-start | bytes 442376 | tf_op jit(solution)/shard_map/ppermute | solution.py:476
  29.3 5.5 %collective-permute-start.7 = (bf16[128,512]{1,0:T(8,128)(2,1)S(1)}, bf16[128,512]{1,0:T(8,128)(2,1)S(1)}, u32[]{:S(2)}, u32[]{:S(2)}) collective-permute-start(bf16[128,512]{1,0:T(8,128)(2,1)S(1)} %get-tuple-element.26), channel_id=1, source_target_pairs={{0,8},{4,12},{8,16},{12,20},{16,24},{20,28},{24,0},{28,4},{32,40},... | collective-permute-start | bytes 393224 | tf_op jit(solution)/shard_map/ppermute | solution.py:476
  30.1 6.9 %collective-permute-start.8 = (bf16[128,512]{1,0:T(8,128)(2,1)S(1)}, bf16[128,512]{1,0:T(8,128)(2,1)S(1)}, u32[]{:S(2)}, u32[]{:S(2)}) collective-permute-start(bf16[128,512]{1,0:T(8,128)(2,1)S(1)} %get-tuple-element.27), channel_id=1, source_target_pairs={{0,16},{4,20},{8,24},{12,28},{16,0},{20,4},{24,8},{28,12},{32,48},... | collective-permute-start | bytes 393224 | tf_op jit(solution)/shard_map/ppermute | solution.py:476
  32.0 6.5 %collective-permute-start.9 = (bf16[128,512]{1,0:T(8,128)(2,1)S(1)}, bf16[128,512]{1,0:T(8,128)(2,1)S(1)}, u32[]{:S(2)}, u32[]{:S(2)}) collective-permute-start(bf16[128,512]{1,0:T(8,128)(2,1)S(1)} %get-tuple-element.28), channel_id=1, source_target_pairs={{0,24},{4,28},{8,0},{12,4},{16,8},{20,12},{24,16},{28,20},{32,56},... | collective-permute-start | bytes 393224 | tf_op jit(solution)/shard_map/ppermute | solution.py:476
  38.7 101.6 %copy-start.2 = (bf16[128,2048]{1,0:T(8,128)(2,1)}, bf16[128,2048]{1,0:T(8,128)(2,1)S(1)}, u32[]{:S(2)}) copy-start(bf16[128,2048]{1,0:T(8,128)(2,1)S(1)} %get-tuple-element.30.refs_8_) | copy-start | bytes 1572868
  38.7 13.0 %collective-permute-start.10 = (bf16[128,2048]{1,0:T(8,128)(2,1)S(1)}, bf16[128,2048]{1,0:T(8,128)(2,1)S(1)}, u32[]{:S(2)}, u32[]{:S(2)}) collective-permute-start(bf16[128,2048]{1,0:T(8,128)(2,1)S(1)} %get-tuple-element.29), channel_id=1, source_target_pairs={{0,4},{4,0},{8,12},{12,8},{16,20},{20,16},{24,28},{28,24},{32,36},... | collective-permute-start | bytes 1572872 | tf_op jit(solution)/shard_map/ppermute | solution.py:476
  42.7 16.0 %collective-permute-start.21 = (bf16[256,1024]{1,0:T(8,128)(2,1)}, bf16[256,1024]{1,0:T(8,128)(2,1)}, u32[]{:S(2)}, u32[]{:S(2)}) collective-permute-start(bf16[256,1024]{1,0:T(8,128)(2,1)} %local_other.1.refs_4_), channel_id=1, source_target_pairs={{0,1},{1,2},{2,3},{3,0},{4,5},{5,6},{6,7},{7,4},{8,9},{9,10},{10,1... | collective-permute-start | bytes 1572872 | tf_op jit(solution)/shard_map/ppermute | solution.py:482
  48.2 17.9 %collective-permute-start.17 = (bf16[256,1280]{1,0:T(8,128)(2,1)}, bf16[256,1280]{1,0:T(8,128)(2,1)S(1)}, u32[]{:S(2)}, u32[]{:S(2)}) collective-permute-start(bf16[256,1280]{1,0:T(8,128)(2,1)} %local_first.1.refs_0_), channel_id=1, source_target_pairs={{0,3},{1,0},{2,1},{3,2},{4,7},{5,4},{6,5},{7,6},{8,11},{9,8},{10,9... | collective-permute-start | bytes 1966088 | tf_op jit(solution)/shard_map/ppermute | solution.py:482
  50.0 27.5 %collective-permute-start.20 = (bf16[256,1024]{1,0:T(8,128)(2,1)}, bf16[256,1024]{1,0:T(8,128)(2,1)}, u32[]{:S(2)}, u32[]{:S(2)}) collective-permute-start(bf16[256,1024]{1,0:T(8,128)(2,1)} %local_other.1.refs_4_), channel_id=1, source_target_pairs={{0,3},{1,0},{2,1},{3,2},{4,7},{5,4},{6,5},{7,6},{8,11},{9,8},{10,9... | collective-permute-start | bytes 1572872 | tf_op jit(solution)/shard_map/ppermute | solution.py:482
  55.6 90.8 %copy-start = (bf16[256,1536]{1,0:T(8,128)(2,1)}, bf16[256,1536]{1,0:T(8,128)(2,1)S(1)}, u32[]{:S(2)}) copy-start(bf16[256,1536]{1,0:T(8,128)(2,1)S(1)} %shard_map.64.refs_0_) | copy-start | bytes 2359300
  55.6 47.3 %collective-permute-start.11 = (bf16[256,1536]{1,0:T(8,128)(2,1)S(1)}, bf16[256,1536]{1,0:T(8,128)(2,1)}, u32[]{:S(2)}, u32[]{:S(2)}) collective-permute-start(bf16[256,1536]{1,0:T(8,128)(2,1)S(1)} %shard_map.64.refs_0_), channel_id=1, source_target_pairs={{0,1},{1,2},{2,3},{3,0},{4,5},{5,6},{6,7},{7,4},{8,9},{9,10},{10,1... | collective-permute-start | bytes 2359304 | tf_op jit(solution)/shard_map/ppermute | solution.py:482
  55.9 35.4 %collective-permute-start.19 = (bf16[256,1280]{1,0:T(8,128)(2,1)}, bf16[256,1280]{1,0:T(8,128)(2,1)S(1)}, u32[]{:S(2)}, u32[]{:S(2)}) collective-permute-start(bf16[256,1280]{1,0:T(8,128)(2,1)} %local_first.1.refs_0_), channel_id=1, source_target_pairs={{0,1},{1,2},{2,3},{3,0},{4,5},{5,6},{6,7},{7,4},{8,9},{9,10},{10,1... | collective-permute-start | bytes 1966088 | tf_op jit(solution)/shard_map/ppermute | solution.py:482
  58.7 43.9 %collective-permute-start.22 = (bf16[256,1024]{1,0:T(8,128)(2,1)}, bf16[256,1024]{1,0:T(8,128)(2,1)S(1)}, u32[]{:S(2)}, u32[]{:S(2)}) collective-permute-start(bf16[256,1024]{1,0:T(8,128)(2,1)} %collective-permute-done.21.refs_7_), channel_id=1, source_target_pairs={{0,1},{1,2},{2,3},{3,0},{4,5},{5,6},{6,7},{7,4},{8,9},{9,10},{10,1... | collective-permute-start | bytes 1572872 | tf_op jit(solution)/shard_map/ppermute | solution.py:482
  66.1 74.2 %copy-start.3 = (bf16[256,1280]{1,0:T(8,128)(2,1)}, bf16[256,1280]{1,0:T(8,128)(2,1)S(1)}, u32[]{:S(2)}) copy-start(bf16[256,1280]{1,0:T(8,128)(2,1)S(1)} %collective-permute-done.17.refs_1_) | copy-start | bytes 1966084
  66.1 42.6 %collective-permute-start.18 = (bf16[256,1280]{1,0:T(8,128)(2,1)S(1)}, bf16[256,1280]{1,0:T(8,128)(2,1)}, u32[]{:S(2)}, u32[]{:S(2)}) collective-permute-start(bf16[256,1280]{1,0:T(8,128)(2,1)S(1)} %collective-permute-done.17.refs_1_), channel_id=1, source_target_pairs={{0,3},{1,0},{2,1},{3,2},{4,7},{5,4},{6,5},{7,6},{8,11},{9,8},{10,9... | collective-permute-start | bytes 1966088 | tf_op jit(solution)/shard_map/ppermute | solution.py:482
  77.5 27.2 %collective-permute-start.23 = (bf16[128,2048]{1,0:T(8,128)(2,1)S(1)}, bf16[128,2048]{1,0:T(8,128)(2,1)}, u32[]{:S(2)}, u32[]{:S(2)}) collective-permute-start(bf16[128,2048]{1,0:T(8,128)(2,1)S(1)} %get-tuple-element.30.refs_8_), channel_id=1, source_target_pairs={{0,3},{1,0},{2,1},{3,2},{4,7},{5,4},{6,5},{7,6},{8,11},{9,8},{10,9... | collective-permute-start | bytes 1572872 | tf_op jit(solution)/shard_map/ppermute | solution.py:482
  91.4 11.6 %copy-start.4 = (bf16[256,1280]{1,0:T(8,128)(2,1)}, bf16[256,1280]{1,0:T(8,128)(2,1)S(1)}, u32[]{:S(2)}) copy-start(bf16[256,1280]{1,0:T(8,128)(2,1)S(1)} %collective-permute-done.19.refs_3_) | copy-start | bytes 1966084
  91.4 22.6 %collective-permute-start.25 = (bf16[128,2048]{1,0:T(8,128)(2,1)S(1)}, bf16[128,2048]{1,0:T(8,128)(2,1)}, u32[]{:S(2)}, u32[]{:S(2)}) collective-permute-start(bf16[128,2048]{1,0:T(8,128)(2,1)S(1)} %get-tuple-element.30.refs_8_), channel_id=1, source_target_pairs={{0,1},{1,2},{2,3},{3,0},{4,5},{5,6},{6,7},{7,4},{8,9},{9,10},{10,1... | collective-permute-start | bytes 1572872 | tf_op jit(solution)/shard_map/ppermute | solution.py:482
  102.6 2.0 %copy-start.5 = (bf16[256,1024]{1,0:T(8,128)(2,1)}, bf16[256,1024]{1,0:T(8,128)(2,1)S(1)}, u32[]{:S(2)}) copy-start(bf16[256,1024]{1,0:T(8,128)(2,1)S(1)} %collective-permute-done.22.refs_6_) | copy-start | bytes 1572868
  102.6 46.3 %collective-permute-start.15 = (bf16[256,1536]{1,0:T(8,128)(2,1)S(1)}, bf16[256,1536]{1,0:T(8,128)(2,1)}, u32[]{:S(2)}, u32[]{:S(2)}) collective-permute-start(bf16[256,1536]{1,0:T(8,128)(2,1)S(1)} %shard_map.64.refs_0_), channel_id=1, source_target_pairs={{0,3},{1,0},{2,1},{3,2},{4,7},{5,4},{6,5},{7,6},{8,11},{9,8},{10,9... | collective-permute-start | bytes 2359304 | tf_op jit(solution)/shard_map/ppermute | solution.py:482
  102.9 50.4 %collective-permute-start.12 = (bf16[256,1536]{1,0:T(8,128)(2,1)}, bf16[256,1536]{1,0:T(8,128)(2,1)S(1)}, u32[]{:S(2)}, u32[]{:S(2)}) collective-permute-start(bf16[256,1536]{1,0:T(8,128)(2,1)} %collective-permute-done.11.refs_2_), channel_id=1, source_target_pairs={{0,1},{1,2},{2,3},{3,0},{4,5},{5,6},{6,7},{7,4},{8,9},{9,10},{10,1... | collective-permute-start | bytes 2359304 | tf_op jit(solution)/shard_map/ppermute | solution.py:482
  104.6 35.7 %collective-permute-start.24 = (bf16[128,2048]{1,0:T(8,128)(2,1)}, bf16[128,2048]{1,0:T(8,128)(2,1)}, u32[]{:S(2)}, u32[]{:S(2)}) collective-permute-start(bf16[128,2048]{1,0:T(8,128)(2,1)} %collective-permute-done.23.refs_9_), channel_id=1, source_target_pairs={{0,3},{1,0},{2,1},{3,2},{4,7},{5,4},{6,5},{7,6},{8,11},{9,8},{10,9... | collective-permute-start | bytes 1572872 | tf_op jit(solution)/shard_map/ppermute | solution.py:482
  108.7 37.8 %copy-start.1 = (bf16[256,512]{1,0:T(8,128)(2,1)}, bf16[256,512]{1,0:T(8,128)(2,1)S(1)}, u32[]{:S(2)}) copy-start(bf16[256,512]{1,0:T(8,128)(2,1)S(1)} %shard_map.65.refs_0_) | copy-start | bytes 786436
  108.7 27.7 %collective-permute-start.13 = (bf16[256,512]{1,0:T(8,128)(2,1)S(1)}, bf16[256,512]{1,0:T(8,128)(2,1)S(1)}, u32[]{:S(2)}, u32[]{:S(2)}) collective-permute-start(bf16[256,512]{1,0:T(8,128)(2,1)S(1)} %shard_map.65.refs_0_), channel_id=1, source_target_pairs={{0,3},{1,0},{2,1},{3,2},{4,7},{5,4},{6,5},{7,6},{8,11},{9,8},{10,9... | collective-permute-start | bytes 786440 | tf_op jit(solution)/shard_map/ppermute | solution.py:482
  113.9 32.5 %collective-permute-start.16 = (bf16[256,512]{1,0:T(8,128)(2,1)S(1)}, bf16[256,512]{1,0:T(8,128)(2,1)}, u32[]{:S(2)}, u32[]{:S(2)}) collective-permute-start(bf16[256,512]{1,0:T(8,128)(2,1)S(1)} %shard_map.65.refs_0_), channel_id=1, source_target_pairs={{0,1},{1,2},{2,3},{3,0},{4,5},{5,6},{6,7},{7,4},{8,9},{9,10},{10,1... | collective-permute-start | bytes 786440 | tf_op jit(solution)/shard_map/ppermute | solution.py:482
  136.4 10.1 %copy-start.6 = (bf16[256,512]{1,0:T(8,128)(2,1)}, bf16[256,512]{1,0:T(8,128)(2,1)S(1)}, u32[]{:S(2)}) copy-start(bf16[256,512]{1,0:T(8,128)(2,1)S(1)} %collective-permute-done.13.refs_1_) | copy-start | bytes 786436
  136.4 15.4 %collective-permute-start.14 = (bf16[256,512]{1,0:T(8,128)(2,1)S(1)}, bf16[256,512]{1,0:T(8,128)(2,1)S(1)}, u32[]{:S(2)}, u32[]{:S(2)}) collective-permute-start(bf16[256,512]{1,0:T(8,128)(2,1)S(1)} %collective-permute-done.13.refs_1_), channel_id=1, source_target_pairs={{0,3},{1,0},{2,1},{3,2},{4,7},{5,4},{6,5},{7,6},{8,11},{9,8},{10,9... | collective-permute-start | bytes 786440 | tf_op jit(solution)/shard_map/ppermute | solution.py:482

commit v3 on v2

--- a/solution.py
+++ b/solution.py
@@ -14,7 +14,7 @@
 HDIM = 64
 WIDE = 1024
 EARLY = (16, 16)
-LATE = (8, 24)
+LATE = (24, 8)
 TAIL = 16
 LOG2E = 1.4426950408889634
 F32 = jnp.float32
@@ -548,7 +548,7 @@
     other = pl.pallas_call(
         functools.partial(other_local_kernel, EARLY[0]),
         name="local_other",
-        out_shape=jax.ShapeDtypeStruct((tokens, EARLY[1] * HDIM), BF),
+        out_shape=pltpu.VMEM((tokens, EARLY[1] * HDIM), BF),
         in_specs=[smem] + [anywhere] * 4,
         out_specs=vmem,
         scratch_shapes=local_scratch(EARLY[1]),
@@ -594,7 +594,7 @@
             out_specs=vmem,
             scratch_shapes=local_scratch(count),
         )(skip, *near([got]), values, log_decay, b_in, c_in)
-        lates.append((start, over_all_docs(late, -1 if i == 0 else 1)))
+        lates.append((start, over_all_docs(late, 1 if i == 0 else -1)))
         start += count
 
     result = jax.ShapeDtypeStruct((doc_n * 2, Q, width), BF)
@@ -638,9 +638,9 @@
         )(owner, *arrays, owned)
 
     near_docs, far_doc = (0, 1, 3), 2
-    for i in range(len(LATE)):
+    for i in (1, 0):
         owned = write_late(owned, i, near_docs)
-    for i in range(len(LATE)):
+    for i in (1, 0):
         owned = write_late(owned, i, far_doc)
     return owned[None]
 

time: 156 us -> 155 us (level)
  no operation moved by 1% of the time
where the time goes in v3:
time: 155 us
  waiting for transfers between devices  88.8 us (57%)
  Pallas kernels  33.4 us (22%)
  starting transfers between devices  31.6 us (20%)
    ppermute x15, waiting for transfers between devices, over_docs(): return lax.ppermute(x, 'doc', [(d, (d + k) % doc_n) for d in range(doc_n)])  67.7 us
    ppermute x11, waiting for transfers between devices, shifted(): return lax.ppermute(x, 'seq', pairs)  21.2 us
    ppermute x15, starting transfers between devices, over_docs(): return lax.ppermute(x, 'doc', [(d, (d + k) % doc_n) for d in range(doc_n)])  18.8 us
    ppermute x11, starting transfers between devices, shifted(): return lax.ppermute(x, 'seq', pairs)  12.8 us
    pallas_call x4, Pallas kernels, write_late(): pl.pallas_call(functools.partial(owned_kernel, start, which), out_shape=r...  8.5 us
    pallas_call x2, Pallas kernels, whole(): pl.pallas_call(functools.partial(late_kernel, start), out_shape=pltpu.VME...  6.33 us
    pallas_call x1, Pallas kernels, whole(): pl.pallas_call(finish_kernel, name='finish', out_shape=result, in_specs=[...  6.1 us
    pallas_call x1, Pallas kernels, whole(): pl.pallas_call(first_local_kernel, name='local_first', out_shape=jax.Shap...  3.91 us
  transfers between devices with their start and end apart: 26, of which 16 were waited for; matrix products, arithmetic and copies ran while one was open for 0% of the time, Pallas kernels for 17%

profile of v3, /device:TPU:6, one launch (start us, length us, event | category | flops | bytes accessed | tf_op | source)
XLA Modules:
  0.0 154.9 jit_solution(9321513541780413218)
XLA Ops:
  0.0 3.5 %states.1 = (bf16[144,2048]{1,0:T(8,128)(2,1)S(1)}, bf16[144,2048]{1,0:T(8,128)(2,1)S(1)}) custom-call(bf16[256,4096]{1,0:T(8,128)(2,1)} %bitcast.5, f32[64,256]{1,0:T(8,128)} %bitcast.10, bf16[256,128]{1,0:T(8,128)(2,1)} %bitcast.15), custom_call_target="tpu_custom_call" | custom-call | tf_op jit(solution)/shard_map/states/pallas_call | solution.py:522
  3.5 0.0 copy-start.7
  3.5 0.1 collective-permute-start
  3.6 2.0 %collective-permute-done.theirs = bf16[144,2048]{1,0:T(8,128)(2,1)S(1)} collective-permute-done((bf16[144,2048]{1,0:T(8,128)(2,1)S(1)}, bf16[144,2048]{1,0:T(8,128)(2,1)S(1)}, u32[]{:S(2)}, u32[]{:S(2)}) %collective-permute-start) | collective-permute-done | bytes 589856 | tf_op jit(solution)/shard_map/ppermute | solution.py:476
  5.6 0.4 chip.1
  6.1 0.4 collective-permute-start.1
  6.5 2.5 %collective-permute-start.2 = (bf16[144,512]{1,0:T(8,128)(2,1)S(1)}, bf16[144,512]{1,0:T(8,128)(2,1)S(1)}, u32[]{:S(2)}, u32[]{:S(2)}) collective-permute-start(bf16[144,512]{1,0:T(8,128)(2,1)S(1)} %get-tuple-element.23), channel_id=1, source_target_pairs={{0,16},{4,20},{8,24},{12,28},{16,0},{20,4},{24,8},{28,12},{32,48},... | collective-permute-start | bytes 442376 | tf_op jit(solution)/shard_map/ppermute | solution.py:476
  9.0 0.0 collective-permute-start.3
  9.0 3.8 %collective-permute-done.1.refs_1_ = bf16[144,512]{1,0:T(8,128)(2,1)S(1)} collective-permute-done((bf16[144,512]{1,0:T(8,128)(2,1)S(1)}, bf16[144,512]{1,0:T(8,128)(2,1)S(1)}, u32[]{:S(2)}, u32[]{:S(2)}) %collective-permute-start.1) | collective-permute-done | bytes 147488 | tf_op jit(solution)/shard_map/ppermute | solution.py:476
  12.8 1.9 %collective-permute-done.2.refs_2_ = bf16[144,512]{1,0:T(8,128)(2,1)S(1)} collective-permute-done((bf16[144,512]{1,0:T(8,128)(2,1)S(1)}, bf16[144,512]{1,0:T(8,128)(2,1)S(1)}, u32[]{:S(2)}, u32[]{:S(2)}) %collective-permute-start.2) | collective-permute-done | bytes 147488 | tf_op jit(solution)/shard_map/ppermute | solution.py:476
  14.7 2.0 %collective-permute-done.3.refs_3_ = bf16[144,512]{1,0:T(8,128)(2,1)S(1)} collective-permute-done((bf16[144,512]{1,0:T(8,128)(2,1)S(1)}, bf16[144,512]{1,0:T(8,128)(2,1)S(1)}, u32[]{:S(2)}, u32[]{:S(2)}) %collective-permute-start.3) | collective-permute-done | bytes 147488 | tf_op jit(solution)/shard_map/ppermute | solution.py:476
  16.8 0.1 row.1
  16.9 2.1 %collective-permute-start.4 = (bf16[144,512]{1,0:T(8,128)(2,1)S(1)}, bf16[144,512]{1,0:T(8,128)(2,1)S(1)}, u32[]{:S(2)}, u32[]{:S(2)}) collective-permute-start(bf16[144,512]{1,0:T(8,128)(2,1)S(1)} %row.1), channel_id=1, source_target_pairs={{0,32},{4,36},{8,40},{12,44},{16,48},{20,52},{24,56},{28,60},{32,6... | collective-permute-start | bytes 442376 | tf_op jit(solution)/shard_map/ppermute | solution.py:476
  19.0 3.6 %collective-permute-start.5 = (bf16[144,512]{1,0:T(8,128)(2,1)S(1)}, bf16[144,512]{1,0:T(8,128)(2,1)S(1)}, u32[]{:S(2)}, u32[]{:S(2)}) collective-permute-start(bf16[144,512]{1,0:T(8,128)(2,1)S(1)} %row.1), channel_id=1, source_target_pairs={{0,64},{4,68},{8,72},{12,76},{16,80},{20,84},{24,88},{28,92},{32,9... | collective-permute-start | bytes 442376 | tf_op jit(solution)/shard_map/ppermute | solution.py:476
  22.6 1.0 collective-permute-start.6
  23.6 1.3 collective-permute-done.4.refs_4_
  24.9 4.1 %collective-permute-done.5.refs_5_ = bf16[144,512]{1,0:T(8,128)(2,1)S(1)} collective-permute-done((bf16[144,512]{1,0:T(8,128)(2,1)S(1)}, bf16[144,512]{1,0:T(8,128)(2,1)S(1)}, u32[]{:S(2)}, u32[]{:S(2)}) %collective-permute-start.5) | collective-permute-done | bytes 147488 | tf_op jit(solution)/shard_map/ppermute | solution.py:476
  29.0 0.0 collective-permute-done.6.refs_6_
  29.0 0.3 enter.1
  29.3 0.8 collective-permute-start.7
  30.1 1.8 %collective-permute-start.8 = (bf16[128,512]{1,0:T(8,128)(2,1)S(1)}, bf16[128,512]{1,0:T(8,128)(2,1)S(1)}, u32[]{:S(2)}, u32[]{:S(2)}) collective-permute-start(bf16[128,512]{1,0:T(8,128)(2,1)S(1)} %get-tuple-element.27), channel_id=1, source_target_pairs={{0,16},{4,20},{8,24},{12,28},{16,0},{20,4},{24,8},{28,12},{32,48},... | collective-permute-start | bytes 393224 | tf_op jit(solution)/shard_map/ppermute | solution.py:476
  32.0 0.4 collective-permute-start.9
  32.4 2.5 %collective-permute-done.7.refs_1_ = bf16[128,512]{1,0:T(8,128)(2,1)S(1)} collective-permute-done((bf16[128,512]{1,0:T(8,128)(2,1)S(1)}, bf16[128,512]{1,0:T(8,128)(2,1)S(1)}, u32[]{:S(2)}, u32[]{:S(2)}) %collective-permute-start.7) | collective-permute-done | bytes 131104 | tf_op jit(solution)/shard_map/ppermute | solution.py:476
  34.9 2.2 %collective-permute-done.8.refs_2_ = bf16[128,512]{1,0:T(8,128)(2,1)S(1)} collective-permute-done((bf16[128,512]{1,0:T(8,128)(2,1)S(1)}, bf16[128,512]{1,0:T(8,128)(2,1)S(1)}, u32[]{:S(2)}, u32[]{:S(2)}) %collective-permute-start.8) | collective-permute-done | bytes 131104 | tf_op jit(solution)/shard_map/ppermute | solution.py:476
  37.1 1.4 collective-permute-done.9.refs_3_
  38.4 1.1 split.1
  39.5 0.0 collective-permute-start.10
  39.5 3.0 %local_other.1.refs_4_ = bf16[256,1024]{1,0:T(8,128)(2,1)S(1)} custom-call(f32[64]{0:T(128)} %skip.7, bf16[256,4096]{1,0:T(8,128)(2,1)} %bitcast.6, f32[64,256]{1,0:T(8,128)} %bitcast.11, bf16[256,128]{1,0:T(8,128)(2,1)} %bitcast.16, bf16[256,128]{1,0:T(8,128)(2,1)} %bitcast.20), custom_call_target="tpu_custom_call" | custom-call | tf_op jit(solution)/shard_map/local_other/pallas_call | solution.py:548
  42.6 1.6 %collective-permute-start.21 = (bf16[256,1024]{1,0:T(8,128)(2,1)S(1)}, bf16[256,1024]{1,0:T(8,128)(2,1)}, u32[]{:S(2)}, u32[]{:S(2)}) collective-permute-start(bf16[256,1024]{1,0:T(8,128)(2,1)S(1)} %local_other.1.refs_4_), channel_id=1, source_target_pairs={{0,1},{1,2},{2,3},{3,0},{4,5},{5,6},{6,7},{7,4},{8,9},{9,10},{10,1... | collective-permute-start | bytes 1572872 | tf_op jit(solution)/shard_map/ppermute | solution.py:482
  44.2 3.9 %local_first.1.refs_0_ = bf16[256,1280]{1,0:T(8,128)(2,1)} custom-call(f32[64]{0:T(128)} %skip.7, bf16[256,4096]{1,0:T(8,128)(2,1)} %bitcast.7, f32[64,256]{1,0:T(8,128)} %bitcast.12, bf16[256,128]{1,0:T(8,128)(2,1)} %bitcast.17, bf16[256,128]{1,0:T(8,128)(2,1)} %bitcast.21), custom_call_target="tpu_custom_call" | custom-call | tf_op jit(solution)/shard_map/local_first/pallas_call | solution.py:508
  48.1 1.7 %collective-permute-start.17 = (bf16[256,1280]{1,0:T(8,128)(2,1)}, bf16[256,1280]{1,0:T(8,128)(2,1)S(1)}, u32[]{:S(2)}, u32[]{:S(2)}) collective-permute-start(bf16[256,1280]{1,0:T(8,128)(2,1)} %local_first.1.refs_0_), channel_id=1, source_target_pairs={{0,3},{1,0},{2,1},{3,2},{4,7},{5,4},{6,5},{7,6},{8,11},{9,8},{10,9... | collective-permute-start | bytes 1966088 | tf_op jit(solution)/shard_map/ppermute | solution.py:482
  49.9 1.8 %collective-permute-start.20 = (bf16[256,1024]{1,0:T(8,128)(2,1)S(1)}, bf16[256,1024]{1,0:T(8,128)(2,1)}, u32[]{:S(2)}, u32[]{:S(2)}) collective-permute-start(bf16[256,1024]{1,0:T(8,128)(2,1)S(1)} %local_other.1.refs_4_), channel_id=1, source_target_pairs={{0,3},{1,0},{2,1},{3,2},{4,7},{5,4},{6,5},{7,6},{8,11},{9,8},{10,9... | collective-permute-start | bytes 1572872 | tf_op jit(solution)/shard_map/ppermute | solution.py:482
  51.7 0.0 collective-permute-done.10.enter
  51.7 3.8 %shard_map.64.refs_0_ = bf16[256,1536]{1,0:T(8,128)(2,1)S(1)} custom-call(f32[64]{0:T(128)} %skip.7, bf16[128,2048]{1,0:T(8,128)(2,1)S(1)} %collective-permute-done.10.enter, bf16[256,4096]{1,0:T(8,128)(2,1)} %bitcast.8, f32[64,256]{1,0:T(8,128)} %bitcast.13, bf16[256,128]{1,0:T(8,128)(2,1)} %bitcast.18, bf16[256,128]{1,0:T(8,128)(2,1)} %bitcast.22), custom_call_target="tpu_custom_call" | custom-call | tf_op jit(solution)/shard_map/pallas_call | solution.py:590
  55.5 0.3 collective-permute-start.11
  55.8 0.4 collective-permute-start.19
  56.2 2.2 %collective-permute-done.21.refs_7_ = bf16[256,1024]{1,0:T(8,128)(2,1)} collective-permute-done((bf16[256,1024]{1,0:T(8,128)(2,1)S(1)}, bf16[256,1024]{1,0:T(8,128)(2,1)}, u32[]{:S(2)}, u32[]{:S(2)}) %collective-permute-start.21) | collective-permute-done | bytes 524320 | tf_op jit(solution)/shard_map/ppermute | solution.py:482
  58.4 0.7 collective-permute-start.22
  59.1 7.0 %collective-permute-done.17.refs_1_ = bf16[256,1280]{1,0:T(8,128)(2,1)S(1)} collective-permute-done((bf16[256,1280]{1,0:T(8,128)(2,1)}, bf16[256,1280]{1,0:T(8,128)(2,1)S(1)}, u32[]{:S(2)}, u32[]{:S(2)}) %collective-permute-start.17) | collective-permute-done | bytes 655392 | tf_op jit(solution)/shard_map/ppermute | solution.py:482
  66.0 2.9 %collective-permute-start.18 = (bf16[256,1280]{1,0:T(8,128)(2,1)S(1)}, bf16[256,1280]{1,0:T(8,128)(2,1)}, u32[]{:S(2)}, u32[]{:S(2)}) collective-permute-start(bf16[256,1280]{1,0:T(8,128)(2,1)S(1)} %collective-permute-done.17.refs_1_), channel_id=1, source_target_pairs={{0,3},{1,0},{2,1},{3,2},{4,7},{5,4},{6,5},{7,6},{8,11},{9,8},{10,9... | collective-permute-start | bytes 1966088 | tf_op jit(solution)/shard_map/ppermute | solution.py:482
  68.9 8.5 %collective-permute-done.20.refs_5_ = bf16[256,1024]{1,0:T(8,128)(2,1)} collective-permute-done((bf16[256,1024]{1,0:T(8,128)(2,1)S(1)}, bf16[256,1024]{1,0:T(8,128)(2,1)}, u32[]{:S(2)}, u32[]{:S(2)}) %collective-permute-start.20) | collective-permute-done | bytes 524320 | tf_op jit(solution)/shard_map/ppermute | solution.py:482
  77.4 2.9 %collective-permute-start.23 = (bf16[128,2048]{1,0:T(8,128)(2,1)}, bf16[128,2048]{1,0:T(8,128)(2,1)}, u32[]{:S(2)}, u32[]{:S(2)}) collective-permute-start(bf16[128,2048]{1,0:T(8,128)(2,1)} %get-tuple-element.30.refs_8_), channel_id=1, source_target_pairs={{0,3},{1,0},{2,1},{3,2},{4,7},{5,4},{6,5},{7,6},{8,11},{9,8},{10,9... | collective-permute-start | bytes 1572872 | tf_op jit(solution)/shard_map/ppermute | solution.py:482
  80.2 11.0 %collective-permute-done.19.refs_3_ = bf16[256,1280]{1,0:T(8,128)(2,1)S(1)} collective-permute-done((bf16[256,1280]{1,0:T(8,128)(2,1)}, bf16[256,1280]{1,0:T(8,128)(2,1)S(1)}, u32[]{:S(2)}, u32[]{:S(2)}) %collective-permute-start.19) | collective-permute-done | bytes 655392 | tf_op jit(solution)/shard_map/ppermute | solution.py:482
  91.3 0.0 collective-permute-start.25
  91.3 11.2 %collective-permute-done.22.refs_6_ = bf16[256,1024]{1,0:T(8,128)(2,1)S(1)} collective-permute-done((bf16[256,1024]{1,0:T(8,128)(2,1)}, bf16[256,1024]{1,0:T(8,128)(2,1)S(1)}, u32[]{:S(2)}, u32[]{:S(2)}) %collective-permute-start.22) | collective-permute-done | bytes 524320 | tf_op jit(solution)/shard_map/ppermute | solution.py:482
  102.5 0.1 collective-permute-start.15
  102.6 0.0 collective-permute-done.11.refs_2_
  102.6 1.9 %collective-permute-start.12 = (bf16[256,1536]{1,0:T(8,128)(2,1)}, bf16[256,1536]{1,0:T(8,128)(2,1)S(1)}, u32[]{:S(2)}, u32[]{:S(2)}) collective-permute-start(bf16[256,1536]{1,0:T(8,128)(2,1)} %collective-permute-done.11.refs_2_), channel_id=1, source_target_pairs={{0,1},{1,2},{2,3},{3,0},{4,5},{5,6},{6,7},{7,4},{8,9},{9,10},{10,1... | collective-permute-start | bytes 2359304 | tf_op jit(solution)/shard_map/ppermute | solution.py:482
  104.5 0.0 collective-permute-done.23.refs_9_
  104.5 1.3 collective-permute-start.24
  105.8 2.5 %shard_map.65.refs_0_ = bf16[256,512]{1,0:T(8,128)(2,1)S(1)} custom-call(f32[64]{0:T(128)} %skip.7, bf16[128,2048]{1,0:T(8,128)(2,1)S(1)} %collective-permute-done.10.enter, bf16[256,4096]{1,0:T(8,128)(2,1)} %bitcast.9, f32[64,256]{1,0:T(8,128)} %bitcast.14, bf16[256,128]{1,0:T(8,128)(2,1)} %bitcast.19, bf16[256,128]{1,0:T(8,128)(2,1)} %bitcast.23), custom_call_target="tpu_custom_call" | custom-call | tf_op jit(solution)/shard_map/pallas_call | solution.py:590
  108.4 0.1 collective-permute-start.13
  108.5 5.4 %collective-permute-done.25.refs_11_ = bf16[128,2048]{1,0:T(8,128)(2,1)} collective-permute-done((bf16[128,2048]{1,0:T(8,128)(2,1)}, bf16[128,2048]{1,0:T(8,128)(2,1)}, u32[]{:S(2)}, u32[]{:S(2)}) %collective-permute-start.25) | collective-permute-done | bytes 524320 | tf_op jit(solution)/shard_map/ppermute | solution.py:482
  113.8 22.5 %collective-permute-done.13.refs_1_ = bf16[256,512]{1,0:T(8,128)(2,1)S(1)} collective-permute-done((bf16[256,512]{1,0:T(8,128)(2,1)S(1)}, bf16[256,512]{1,0:T(8,128)(2,1)S(1)}, u32[]{:S(2)}, u32[]{:S(2)}) %collective-permute-start.13) | collective-permute-done | bytes 262176 | tf_op jit(solution)/shard_map/ppermute | solution.py:482
  136.3 3.1 %collective-permute-start.14 = (bf16[256,512]{1,0:T(8,128)(2,1)S(1)}, bf16[256,512]{1,0:T(8,128)(2,1)S(1)}, u32[]{:S(2)}, u32[]{:S(2)}) collective-permute-start(bf16[256,512]{1,0:T(8,128)(2,1)S(1)} %collective-permute-done.13.refs_1_), channel_id=1, source_target_pairs={{0,3},{1,0},{2,1},{3,2},{4,7},{5,4},{6,5},{7,6},{8,11},{9,8},{10,9... | collective-permute-start | bytes 786440 | tf_op jit(solution)/shard_map/ppermute | solution.py:482
  139.4 0.6 copy.15.owner
  140.0 0.0 collective-permute-done.24.refs_10_
  140.0 6.1 %finish.1.refs_3_ = bf16[8,128,4096]{2,1,0:T(8,128)(2,1)} custom-call(s32[4,2]{1,0:T(4,128)} %copy.15.owner, bf16[256,1280]{1,0:T(8,128)(2,1)} %local_first.1.refs_0_, bf16[256,1280]{1,0:T(8,128)(2,1)} %copy-done.3, bf16[256,1280]{1,0:T(8,128)(2,1)} %collective-permute-done.18.refs_2_, bf16[256,1280]{1,0:T(8,128)(2,1)} %copy-done.4, ...), custom_call_target="tpu_custom_call" | custom-call | tf_op jit(solution)/shard_map/finish/pallas_call | solution.py:601
  146.2 2.5 %shard_map.66.refs_3_ = bf16[8,128,4096]{2,1,0:T(8,128)(2,1)} custom-call(s32[4,2]{1,0:T(4,128)} %copy.15.owner, bf16[256,512]{1,0:T(8,128)(2,1)} %copy-done.2, bf16[256,512]{1,0:T(8,128)(2,1)} %copy-done.6, bf16[256,512]{1,0:T(8,128)(2,1)} %collective-permute-done.16.refs_2_, bf16[8,128,4096]{2,1,0:T(8,128)(2,1)} %finish.1.refs_3_), custom_call_target="tpu_custom_call", output_to_operand_aliasing={{}: (4, {})} | custom-call | tf_op jit(solution)/shard_map/pallas_call | solution.py:627
  148.7 2.8 %shard_map.67.refs_1_ = bf16[8,128,4096]{2,1,0:T(8,128)(2,1)} custom-call(s32[4,2]{1,0:T(4,128)} %copy.15.owner, bf16[256,1536]{1,0:T(8,128)(2,1)} %copy-done, bf16[256,1536]{1,0:T(8,128)(2,1)} %collective-permute-done.15.refs_1_, bf16[256,1536]{1,0:T(8,128)(2,1)} %collective-permute-done.11.refs_2_, ...), custom_call_target="tpu_custom_call", output_to_operand_aliasing={{}: (4, {})} | custom-call | tf_op jit(solution)/shard_map/pallas_call | solution.py:627
  151.5 0.0 collective-permute-done.14.refs_0_
  151.5 1.5 shard_map.68.refs_1_
  153.0 0.0 collective-permute-done.12.refs_0_
  153.0 1.7 %shard_map.69 = bf16[8,128,4096]{2,1,0:T(8,128)(2,1)} custom-call(s32[4,2]{1,0:T(4,128)} %copy.15.owner, bf16[256,1536]{1,0:T(8,128)(2,1)S(1)} %collective-permute-done.12.refs_0_, bf16[8,128,4096]{2,1,0:T(8,128)(2,1)} %shard_map.68.refs_1_), custom_call_target="tpu_custom_call", output_to_operand_aliasing={{}: (2, {})} | custom-call | tf_op jit(solution)/shard_map/pallas_call | solution.py:627
  (19 shorter events, 0.0 us)
Async XLA Ops:
  3.5 135.9 %copy-start.7 = (s32[4,2]{0,1:T(2,128)S(1)}, s32[4,2]{0,1:T(2,128)}, u32[]{:S(2)}) copy-start(s32[4,2]{0,1:T(2,128)} %param.11) | copy-start | bytes 100
  3.5 2.1 %collective-permute-start = (bf16[144,2048]{1,0:T(8,128)(2,1)S(1)}, bf16[144,2048]{1,0:T(8,128)(2,1)S(1)}, u32[]{:S(2)}, u32[]{:S(2)}) collective-permute-start(bf16[144,2048]{1,0:T(8,128)(2,1)S(1)} %get-tuple-element.19), channel_id=1, source_target_pairs={{0,4},{4,0},{8,12},{12,8},{16,20},{20,16},{24,28},{28,24},{32,36},... | collective-permute-start | bytes 1769480 | tf_op jit(solution)/shard_map/ppermute | solution.py:476
  6.1 6.8 %collective-permute-start.1 = (bf16[144,512]{1,0:T(8,128)(2,1)S(1)}, bf16[144,512]{1,0:T(8,128)(2,1)S(1)}, u32[]{:S(2)}, u32[]{:S(2)}) collective-permute-start(bf16[144,512]{1,0:T(8,128)(2,1)S(1)} %get-tuple-element.22), channel_id=1, source_target_pairs={{0,8},{4,12},{8,16},{12,20},{16,24},{20,28},{24,0},{28,4},{32,40},... | collective-permute-start | bytes 442376 | tf_op jit(solution)/shard_map/ppermute | solution.py:476
  6.5 8.2 %collective-permute-start.2 = (bf16[144,512]{1,0:T(8,128)(2,1)S(1)}, bf16[144,512]{1,0:T(8,128)(2,1)S(1)}, u32[]{:S(2)}, u32[]{:S(2)}) collective-permute-start(bf16[144,512]{1,0:T(8,128)(2,1)S(1)} %get-tuple-element.23), channel_id=1, source_target_pairs={{0,16},{4,20},{8,24},{12,28},{16,0},{20,4},{24,8},{28,12},{32,48},... | collective-permute-start | bytes 442376 | tf_op jit(solution)/shard_map/ppermute | solution.py:476
  9.0 7.7 %collective-permute-start.3 = (bf16[144,512]{1,0:T(8,128)(2,1)S(1)}, bf16[144,512]{1,0:T(8,128)(2,1)S(1)}, u32[]{:S(2)}, u32[]{:S(2)}) collective-permute-start(bf16[144,512]{1,0:T(8,128)(2,1)S(1)} %get-tuple-element.24), channel_id=1, source_target_pairs={{0,24},{4,28},{8,0},{12,4},{16,8},{20,12},{24,16},{28,20},{32,56},... | collective-permute-start | bytes 442376 | tf_op jit(solution)/shard_map/ppermute | solution.py:476
  16.9 8.0 %collective-permute-start.4 = (bf16[144,512]{1,0:T(8,128)(2,1)S(1)}, bf16[144,512]{1,0:T(8,128)(2,1)S(1)}, u32[]{:S(2)}, u32[]{:S(2)}) collective-permute-start(bf16[144,512]{1,0:T(8,128)(2,1)S(1)} %row.1), channel_id=1, source_target_pairs={{0,32},{4,36},{8,40},{12,44},{16,48},{20,52},{24,56},{28,60},{32,6... | collective-permute-start | bytes 442376 | tf_op jit(solution)/shard_map/ppermute | solution.py:476
  19.0 10.0 %collective-permute-start.5 = (bf16[144,512]{1,0:T(8,128)(2,1)S(1)}, bf16[144,512]{1,0:T(8,128)(2,1)S(1)}, u32[]{:S(2)}, u32[]{:S(2)}) collective-permute-start(bf16[144,512]{1,0:T(8,128)(2,1)S(1)} %row.1), channel_id=1, source_target_pairs={{0,64},{4,68},{8,72},{12,76},{16,80},{20,84},{24,88},{28,92},{32,9... | collective-permute-start | bytes 442376 | tf_op jit(solution)/shard_map/ppermute | solution.py:476
  22.6 6.4 %collective-permute-start.6 = (bf16[144,512]{1,0:T(8,128)(2,1)S(1)}, bf16[144,512]{1,0:T(8,128)(2,1)S(1)}, u32[]{:S(2)}, u32[]{:S(2)}) collective-permute-start(bf16[144,512]{1,0:T(8,128)(2,1)S(1)} %row.1), channel_id=1, source_target_pairs={{0,96},{4,100},{8,104},{12,108},{16,112},{20,116},{24,120},{28,124... | collective-permute-start | bytes 442376 | tf_op jit(solution)/shard_map/ppermute | solution.py:476
  29.3 5.5 %collective-permute-start.7 = (bf16[128,512]{1,0:T(8,128)(2,1)S(1)}, bf16[128,512]{1,0:T(8,128)(2,1)S(1)}, u32[]{:S(2)}, u32[]{:S(2)}) collective-permute-start(bf16[128,512]{1,0:T(8,128)(2,1)S(1)} %get-tuple-element.26), channel_id=1, source_target_pairs={{0,8},{4,12},{8,16},{12,20},{16,24},{20,28},{24,0},{28,4},{32,40},... | collective-permute-start | bytes 393224 | tf_op jit(solution)/shard_map/ppermute | solution.py:476
  30.1 6.9 %collective-permute-start.8 = (bf16[128,512]{1,0:T(8,128)(2,1)S(1)}, bf16[128,512]{1,0:T(8,128)(2,1)S(1)}, u32[]{:S(2)}, u32[]{:S(2)}) collective-permute-start(bf16[128,512]{1,0:T(8,128)(2,1)S(1)} %get-tuple-element.27), channel_id=1, source_target_pairs={{0,16},{4,20},{8,24},{12,28},{16,0},{20,4},{24,8},{28,12},{32,48},... | collective-permute-start | bytes 393224 | tf_op jit(solution)/shard_map/ppermute | solution.py:476
  32.0 6.5 %collective-permute-start.9 = (bf16[128,512]{1,0:T(8,128)(2,1)S(1)}, bf16[128,512]{1,0:T(8,128)(2,1)S(1)}, u32[]{:S(2)}, u32[]{:S(2)}) collective-permute-start(bf16[128,512]{1,0:T(8,128)(2,1)S(1)} %get-tuple-element.28), channel_id=1, source_target_pairs={{0,24},{4,28},{8,0},{12,4},{16,8},{20,12},{24,16},{28,20},{32,56},... | collective-permute-start | bytes 393224 | tf_op jit(solution)/shard_map/ppermute | solution.py:476
  39.5 12.1 %collective-permute-start.10 = (bf16[128,2048]{1,0:T(8,128)(2,1)S(1)}, bf16[128,2048]{1,0:T(8,128)(2,1)S(1)}, u32[]{:S(2)}, u32[]{:S(2)}) collective-permute-start(bf16[128,2048]{1,0:T(8,128)(2,1)S(1)} %get-tuple-element.29), channel_id=1, source_target_pairs={{0,4},{4,0},{8,12},{12,8},{16,20},{20,16},{24,28},{28,24},{32,36},... | collective-permute-start | bytes 1572872 | tf_op jit(solution)/shard_map/ppermute | solution.py:476
  42.6 97.5 %copy-start.1 = (bf16[256,1024]{1,0:T(8,128)(2,1)}, bf16[256,1024]{1,0:T(8,128)(2,1)S(1)}, u32[]{:S(2)}) copy-start(bf16[256,1024]{1,0:T(8,128)(2,1)S(1)} %local_other.1.refs_4_) | copy-start | bytes 1572868
  42.6 15.8 %collective-permute-start.21 = (bf16[256,1024]{1,0:T(8,128)(2,1)S(1)}, bf16[256,1024]{1,0:T(8,128)(2,1)}, u32[]{:S(2)}, u32[]{:S(2)}) collective-permute-start(bf16[256,1024]{1,0:T(8,128)(2,1)S(1)} %local_other.1.refs_4_), channel_id=1, source_target_pairs={{0,1},{1,2},{2,3},{3,0},{4,5},{5,6},{6,7},{7,4},{8,9},{9,10},{10,1... | collective-permute-start | bytes 1572872 | tf_op jit(solution)/shard_map/ppermute | solution.py:482
  48.1 17.9 %collective-permute-start.17 = (bf16[256,1280]{1,0:T(8,128)(2,1)}, bf16[256,1280]{1,0:T(8,128)(2,1)S(1)}, u32[]{:S(2)}, u32[]{:S(2)}) collective-permute-start(bf16[256,1280]{1,0:T(8,128)(2,1)} %local_first.1.refs_0_), channel_id=1, source_target_pairs={{0,3},{1,0},{2,1},{3,2},{4,7},{5,4},{6,5},{7,6},{8,11},{9,8},{10,9... | collective-permute-start | bytes 1966088 | tf_op jit(solution)/shard_map/ppermute | solution.py:482
  49.9 27.5 %collective-permute-start.20 = (bf16[256,1024]{1,0:T(8,128)(2,1)S(1)}, bf16[256,1024]{1,0:T(8,128)(2,1)}, u32[]{:S(2)}, u32[]{:S(2)}) collective-permute-start(bf16[256,1024]{1,0:T(8,128)(2,1)S(1)} %local_other.1.refs_4_), channel_id=1, source_target_pairs={{0,3},{1,0},{2,1},{3,2},{4,7},{5,4},{6,5},{7,6},{8,11},{9,8},{10,9... | collective-permute-start | bytes 1572872 | tf_op jit(solution)/shard_map/ppermute | solution.py:482
  55.5 90.6 %copy-start = (bf16[256,1536]{1,0:T(8,128)(2,1)}, bf16[256,1536]{1,0:T(8,128)(2,1)S(1)}, u32[]{:S(2)}) copy-start(bf16[256,1536]{1,0:T(8,128)(2,1)S(1)} %shard_map.64.refs_0_) | copy-start | bytes 2359300
  55.5 47.1 %collective-permute-start.11 = (bf16[256,1536]{1,0:T(8,128)(2,1)S(1)}, bf16[256,1536]{1,0:T(8,128)(2,1)}, u32[]{:S(2)}, u32[]{:S(2)}) collective-permute-start(bf16[256,1536]{1,0:T(8,128)(2,1)S(1)} %shard_map.64.refs_0_), channel_id=1, source_target_pairs={{0,1},{1,2},{2,3},{3,0},{4,5},{5,6},{6,7},{7,4},{8,9},{9,10},{10,1... | collective-permute-start | bytes 2359304 | tf_op jit(solution)/shard_map/ppermute | solution.py:482
  55.8 35.4 %collective-permute-start.19 = (bf16[256,1280]{1,0:T(8,128)(2,1)}, bf16[256,1280]{1,0:T(8,128)(2,1)S(1)}, u32[]{:S(2)}, u32[]{:S(2)}) collective-permute-start(bf16[256,1280]{1,0:T(8,128)(2,1)} %local_first.1.refs_0_), channel_id=1, source_target_pairs={{0,1},{1,2},{2,3},{3,0},{4,5},{5,6},{6,7},{7,4},{8,9},{9,10},{10,1... | collective-permute-start | bytes 1966088 | tf_op jit(solution)/shard_map/ppermute | solution.py:482
  58.4 44.1 %collective-permute-start.22 = (bf16[256,1024]{1,0:T(8,128)(2,1)}, bf16[256,1024]{1,0:T(8,128)(2,1)S(1)}, u32[]{:S(2)}, u32[]{:S(2)}) collective-permute-start(bf16[256,1024]{1,0:T(8,128)(2,1)} %collective-permute-done.21.refs_7_), channel_id=1, source_target_pairs={{0,1},{1,2},{2,3},{3,0},{4,5},{5,6},{6,7},{7,4},{8,9},{9,10},{10,1... | collective-permute-start | bytes 1572872 | tf_op jit(solution)/shard_map/ppermute | solution.py:482
  66.0 74.0 %copy-start.3 = (bf16[256,1280]{1,0:T(8,128)(2,1)}, bf16[256,1280]{1,0:T(8,128)(2,1)S(1)}, u32[]{:S(2)}) copy-start(bf16[256,1280]{1,0:T(8,128)(2,1)S(1)} %collective-permute-done.17.refs_1_) | copy-start | bytes 1966084
  66.0 42.3 %collective-permute-start.18 = (bf16[256,1280]{1,0:T(8,128)(2,1)S(1)}, bf16[256,1280]{1,0:T(8,128)(2,1)}, u32[]{:S(2)}, u32[]{:S(2)}) collective-permute-start(bf16[256,1280]{1,0:T(8,128)(2,1)S(1)} %collective-permute-done.17.refs_1_), channel_id=1, source_target_pairs={{0,3},{1,0},{2,1},{3,2},{4,7},{5,4},{6,5},{7,6},{8,11},{9,8},{10,9... | collective-permute-start | bytes 1966088 | tf_op jit(solution)/shard_map/ppermute | solution.py:482
  77.4 27.2 %collective-permute-start.23 = (bf16[128,2048]{1,0:T(8,128)(2,1)}, bf16[128,2048]{1,0:T(8,128)(2,1)}, u32[]{:S(2)}, u32[]{:S(2)}) collective-permute-start(bf16[128,2048]{1,0:T(8,128)(2,1)} %get-tuple-element.30.refs_8_), channel_id=1, source_target_pairs={{0,3},{1,0},{2,1},{3,2},{4,7},{5,4},{6,5},{7,6},{8,11},{9,8},{10,9... | collective-permute-start | bytes 1572872 | tf_op jit(solution)/shard_map/ppermute | solution.py:482
  91.2 11.3 %copy-start.4 = (bf16[256,1280]{1,0:T(8,128)(2,1)}, bf16[256,1280]{1,0:T(8,128)(2,1)S(1)}, u32[]{:S(2)}) copy-start(bf16[256,1280]{1,0:T(8,128)(2,1)S(1)} %collective-permute-done.19.refs_3_) | copy-start | bytes 1966084
  91.3 22.6 %collective-permute-start.25 = (bf16[128,2048]{1,0:T(8,128)(2,1)}, bf16[128,2048]{1,0:T(8,128)(2,1)}, u32[]{:S(2)}, u32[]{:S(2)}) collective-permute-start(bf16[128,2048]{1,0:T(8,128)(2,1)} %get-tuple-element.30.refs_8_), channel_id=1, source_target_pairs={{0,1},{1,2},{2,3},{3,0},{4,5},{5,6},{6,7},{7,4},{8,9},{9,10},{10,1... | collective-permute-start | bytes 1572872 | tf_op jit(solution)/shard_map/ppermute | solution.py:482
  102.5 2.0 %copy-start.5 = (bf16[256,1024]{1,0:T(8,128)(2,1)}, bf16[256,1024]{1,0:T(8,128)(2,1)S(1)}, u32[]{:S(2)}) copy-start(bf16[256,1024]{1,0:T(8,128)(2,1)S(1)} %collective-permute-done.22.refs_6_) | copy-start | bytes 1572868
  102.5 46.2 %collective-permute-start.15 = (bf16[256,1536]{1,0:T(8,128)(2,1)S(1)}, bf16[256,1536]{1,0:T(8,128)(2,1)}, u32[]{:S(2)}, u32[]{:S(2)}) collective-permute-start(bf16[256,1536]{1,0:T(8,128)(2,1)S(1)} %shard_map.64.refs_0_), channel_id=1, source_target_pairs={{0,3},{1,0},{2,1},{3,2},{4,7},{5,4},{6,5},{7,6},{8,11},{9,8},{10,9... | collective-permute-start | bytes 2359304 | tf_op jit(solution)/shard_map/ppermute | solution.py:482
  102.6 50.4 %collective-permute-start.12 = (bf16[256,1536]{1,0:T(8,128)(2,1)}, bf16[256,1536]{1,0:T(8,128)(2,1)S(1)}, u32[]{:S(2)}, u32[]{:S(2)}) collective-permute-start(bf16[256,1536]{1,0:T(8,128)(2,1)} %collective-permute-done.11.refs_2_), channel_id=1, source_target_pairs={{0,1},{1,2},{2,3},{3,0},{4,5},{5,6},{6,7},{7,4},{8,9},{9,10},{10,1... | collective-permute-start | bytes 2359304 | tf_op jit(solution)/shard_map/ppermute | solution.py:482
  104.5 35.5 %collective-permute-start.24 = (bf16[128,2048]{1,0:T(8,128)(2,1)}, bf16[128,2048]{1,0:T(8,128)(2,1)}, u32[]{:S(2)}, u32[]{:S(2)}) collective-permute-start(bf16[128,2048]{1,0:T(8,128)(2,1)} %collective-permute-done.23.refs_9_), channel_id=1, source_target_pairs={{0,3},{1,0},{2,1},{3,2},{4,7},{5,4},{6,5},{7,6},{8,11},{9,8},{10,9... | collective-permute-start | bytes 1572872 | tf_op jit(solution)/shard_map/ppermute | solution.py:482
  108.4 37.8 %copy-start.2 = (bf16[256,512]{1,0:T(8,128)(2,1)}, bf16[256,512]{1,0:T(8,128)(2,1)S(1)}, u32[]{:S(2)}) copy-start(bf16[256,512]{1,0:T(8,128)(2,1)S(1)} %shard_map.65.refs_0_) | copy-start | bytes 786436
  108.4 27.9 %collective-permute-start.13 = (bf16[256,512]{1,0:T(8,128)(2,1)S(1)}, bf16[256,512]{1,0:T(8,128)(2,1)S(1)}, u32[]{:S(2)}, u32[]{:S(2)}) collective-permute-start(bf16[256,512]{1,0:T(8,128)(2,1)S(1)} %shard_map.65.refs_0_), channel_id=1, source_target_pairs={{0,3},{1,0},{2,1},{3,2},{4,7},{5,4},{6,5},{7,6},{8,11},{9,8},{10,9... | collective-permute-start | bytes 786440 | tf_op jit(solution)/shard_map/ppermute | solution.py:482
  113.8 32.3 %collective-permute-start.16 = (bf16[256,512]{1,0:T(8,128)(2,1)S(1)}, bf16[256,512]{1,0:T(8,128)(2,1)}, u32[]{:S(2)}, u32[]{:S(2)}) collective-permute-start(bf16[256,512]{1,0:T(8,128)(2,1)S(1)} %shard_map.65.refs_0_), channel_id=1, source_target_pairs={{0,1},{1,2},{2,3},{3,0},{4,5},{5,6},{6,7},{7,4},{8,9},{9,10},{10,1... | collective-permute-start | bytes 786440 | tf_op jit(solution)/shard_map/ppermute | solution.py:482
  136.3 9.9 %copy-start.6 = (bf16[256,512]{1,0:T(8,128)(2,1)}, bf16[256,512]{1,0:T(8,128)(2,1)S(1)}, u32[]{:S(2)}) copy-start(bf16[256,512]{1,0:T(8,128)(2,1)S(1)} %collective-permute-done.13.refs_1_) | copy-start | bytes 786436
  136.3 15.2 %collective-permute-start.14 = (bf16[256,512]{1,0:T(8,128)(2,1)S(1)}, bf16[256,512]{1,0:T(8,128)(2,1)S(1)}, u32[]{:S(2)}, u32[]{:S(2)}) collective-permute-start(bf16[256,512]{1,0:T(8,128)(2,1)S(1)} %collective-permute-done.13.refs_1_), channel_id=1, source_target_pairs={{0,3},{1,0},{2,1},{3,2},{4,7},{5,4},{6,5},{7,6},{8,11},{9,8},{10,9... | collective-permute-start | bytes 786440 | tf_op jit(solution)/shard_map/ppermute | solution.py:482
